TPU v7x, 32 devices: a whole 2x2x4 slice. The times are simulated.
32 devices in a mesh: head: 2 (over core), blk: 16 (over z, y, x).
Axes of the slice: x: 2, y: 2, z: 4, core: 2. Of those that a mesh axis runs over, the one named last changes fastest.
Arguments:
- tokens: bfloat16 [16, 2048, 768], P('blk', 'head'), may hold values from -6 to 6
- lengths: int32 [8], replicated, may hold values from 2049 to 4096, as said below
- pair_flip: int32 [8, 12], replicated, may hold values from 0 to 1
- w_qkv: bfloat16 [768, 2304], P(('head', 'blk')), may hold values from -0.21875 to 0.21875
- q_bias: bfloat16 [768], P(('head', 'blk')), may hold values from -3 to 3
- v_bias: bfloat16 [768], P(('head', 'blk')), may hold values from -3 to 3
- w_out: bfloat16 [768, 768], P(('head', 'blk')), may hold values from -6 to 6
- out_bias: bfloat16 [768], P(('head', 'blk')), may hold values from -3 to 3
- norm1_gain: bfloat16 [768], P(('head', 'blk')), may hold values from 0.5 to 1.5
- norm1_shift: bfloat16 [768], P(('head', 'blk')), may hold values from -3 to 3
- w_in: bfloat16 [768, 3072], P(('head', 'blk')), may hold values from -0.21875 to 0.21875
- in_bias: bfloat16 [3072], P(('head', 'blk')), may hold values from -3 to 3
- w_back: bfloat16 [3072, 768], P(('head', 'blk')), may hold values from -0.109375 to 0.109375
- back_bias: bfloat16 [768], P(('head', 'blk')), may hold values from -3 to 3
- norm2_gain: bfloat16 [768], P(('head', 'blk')), may hold values from 0.5 to 1.5
- norm2_shift: bfloat16 [768], P(('head', 'blk')), may hold values from -3 to 3
- cotangent: bfloat16 [16, 2048, 768], P('blk', 'head'), may hold values from -6 to 6
Outputs:
- out: bfloat16 [16, 2048, 768], P('blk', 'head')
- grad_tokens: float32 [16, 2048, 768], P('blk', 'head')
- grad_w_qkv: float32 [768, 2304], P(('head', 'blk'))
- grad_q_bias: float32 [768], P(('head', 'blk'))
- grad_v_bias: float32 [768], P(('head', 'blk'))
- grad_w_out: float32 [768, 768], P(('head', 'blk'))
- grad_out_bias: float32 [768], P(('head', 'blk'))
- grad_norm1_gain: float32 [768], P(('head', 'blk'))
- grad_norm1_shift: float32 [768], P(('head', 'blk'))
- grad_w_in: float32 [768, 3072], P(('head', 'blk'))
- grad_in_bias: float32 [3072], P(('head', 'blk'))
- grad_w_back: float32 [3072, 768], P(('head', 'blk'))
- grad_back_bias: float32 [768], P(('head', 'blk'))
- grad_norm2_gain: float32 [768], P(('head', 'blk'))
- grad_norm2_shift: float32 [768], P(('head', 'blk'))
Inputs may be any that keep to these rules, and one draw needn't show every extreme that they name: Keys at positions of lengths[s] or more in sequence s are padding; some sequence is full and some has only 2049 tokens.
All inputs are finite; a program needn't handle non-finite values.
Results may differ from a plain program's by a relative error of at most 0.013.
Values may be sent and summed in bfloat16 or wider, within the bound.
No kernel may reach another device: no remote copies, remote signals or barrier semaphores. Data moves between devices by JAX's collectives and lax.ppermute only.
A program may use at most 512 MiB of HBM per device.

v0:
```python
import jax
import jax.numpy as jnp
from jax import lax
from jax.sharding import PartitionSpec as P

HEADS = 12
HD = 64


def partner(value, axis, apart):
    mask = 2**apart
    pairs = [(source, source ^ mask) for source in range(lax.axis_size(axis))]
    return lax.ppermute(value, axis, pairs)


def layer_norm(value, gain, shift):
    center = value - jnp.mean(value, axis=-1, keepdims=True)
    spread = jnp.mean(center * center, axis=-1, keepdims=True)
    return center * lax.rsqrt(spread + 1e-06) * gain + shift


def gelu_exact(value):
    return jax.nn.gelu(value, approximate=False)


def per_device(
    tokens,
    lengths,
    pair_flip,
    w_qkv,
    q_bias,
    v_bias,
    w_out,
    out_bias,
    norm1_gain,
    norm1_shift,
    w_in,
    in_bias,
    w_back,
    back_bias,
    norm2_gain,
    norm2_shift,
    cotangent,
):
    whole = (
        lax.all_gather(w_qkv, ("head", "blk"), axis=0, tiled=True),
        lax.all_gather(w_out, ("head", "blk"), axis=0, tiled=True),
        lax.all_gather(w_in, ("head", "blk"), axis=0, tiled=True),
        lax.all_gather(w_back, ("head", "blk"), axis=0, tiled=True),
        lax.all_gather(q_bias, ("head", "blk"), axis=0, tiled=True),
        lax.all_gather(v_bias, ("head", "blk"), axis=0, tiled=True),
        lax.all_gather(out_bias, ("head", "blk"), axis=0, tiled=True),
        lax.all_gather(in_bias, ("head", "blk"), axis=0, tiled=True),
        lax.all_gather(back_bias, ("head", "blk"), axis=0, tiled=True),
        lax.all_gather(norm1_gain, ("head", "blk"), axis=0, tiled=True),
        lax.all_gather(norm1_shift, ("head", "blk"), axis=0, tiled=True),
        lax.all_gather(norm2_gain, ("head", "blk"), axis=0, tiled=True),
        lax.all_gather(norm2_shift, ("head", "blk"), axis=0, tiled=True),
    )
    (
        full_qkv,
        full_out,
        full_in,
        full_back,
        full_qbias,
        full_vbias,
        full_obias,
        full_ibias,
        full_bbias,
        full_gain1,
        full_shift1,
        full_gain2,
        full_shift2,
    ) = whole
    head_count = lax.axis_size("head")
    group_heads = HEADS // head_count
    group_width = group_heads * HD
    local_rows = tokens.shape[1]
    model_width = tokens.shape[2]
    half_rows = local_rows * head_count
    block_rows = min(512, half_rows)
    block_count = half_rows // block_rows
    scale = HD ** (-0.5)
    block_index = lax.axis_index("blk")
    group_index = lax.axis_index("head")
    sequence = block_index // 2
    own_half = block_index % 2
    seq_length = lax.dynamic_index_in_dim(lengths, sequence, 0, keepdims=False)
    flag_row = lax.dynamic_index_in_dim(pair_flip, sequence, 0, keepdims=False)
    head_flags = lax.dynamic_slice_in_dim(flag_row, group_index * group_heads, group_heads)
    inputs = tokens[0]
    zero_bias = jnp.zeros((model_width,), jnp.float32)
    qkv_bias = jnp.concatenate(
        [full_qbias.astype(jnp.float32), zero_bias, full_vbias.astype(jnp.float32)]
    )
    projected = jnp.dot(inputs, full_qkv, preferred_element_type=jnp.float32) + qkv_bias
    projected = projected.astype(jnp.bfloat16).reshape(1, local_rows, 3, head_count, group_width)
    per_head = lax.all_to_all(projected, "head", split_axis=3, concat_axis=1, tiled=True)
    queries = per_head[0, :, 0, 0]
    kv_local = jnp.stack([per_head[0, :, 1, 0], per_head[0, :, 2, 0]])
    kv_far = partner(kv_local, "blk", 0)
    column_flag = jnp.repeat(head_flags, HD) == 1
    kv_used = jnp.where(column_flag, kv_far, kv_local)
    source_half = jnp.where(head_flags == 1, 1 - own_half, own_half)
    positions = source_half[:, None] * half_rows + jnp.arange(half_rows)[None, :]
    key_valid = positions < seq_length
    keys_three = kv_used[0].reshape(half_rows, group_heads, HD)
    values_three = kv_used[1].reshape(half_rows, group_heads, HD)

    def logits_of(query_block):
        scores = jnp.einsum(
            "qhd,khd->hqk", query_block, keys_three, preferred_element_type=jnp.float32
        )
        return jnp.where(key_valid[:, None, :], scores * scale, -1e30)

    context_parts = []
    lse_parts = []
    for block in range(block_count):
        query_block = queries[block * block_rows : (block + 1) * block_rows].reshape(
            block_rows, group_heads, HD
        )
        logits = logits_of(query_block)
        peak = jnp.max(logits, axis=-1, keepdims=True)
        expo = jnp.exp(logits - peak)
        total = jnp.sum(expo, axis=-1, keepdims=True)
        probs_low = (expo / total).astype(jnp.bfloat16)
        context = jnp.einsum(
            "hqk,khd->qhd", probs_low, values_three, preferred_element_type=jnp.float32
        )
        context_parts.append(context.reshape(block_rows, group_width))
        lse_parts.append(peak + jnp.log(total))
    context_all = (
        jnp.concatenate(context_parts, axis=0)
        .astype(jnp.bfloat16)
        .reshape(1, half_rows, 1, group_width)
    )
    context_rows = lax.all_to_all(
        context_all, "head", split_axis=1, concat_axis=2, tiled=True
    ).reshape(local_rows, model_width)
    attended = jnp.dot(
        context_rows, full_out, preferred_element_type=jnp.float32
    ) + full_obias.astype(jnp.float32)
    resid_one = inputs.astype(jnp.float32) + attended
    gain_one = full_gain1.astype(jnp.float32)
    shift_one = full_shift1.astype(jnp.float32)
    normed_one, norm_one_pull = jax.vjp(layer_norm, resid_one, gain_one, shift_one)
    normed_low = normed_one.astype(jnp.bfloat16)
    hidden = jnp.dot(normed_low, full_in, preferred_element_type=jnp.float32) + full_ibias.astype(
        jnp.float32
    )
    activ, gelu_pull = jax.vjp(gelu_exact, hidden)
    activ_low = activ.astype(jnp.bfloat16)
    branch = jnp.dot(activ_low, full_back, preferred_element_type=jnp.float32) + full_bbias.astype(
        jnp.float32
    )
    resid_two = normed_one + branch
    gain_two = full_gain2.astype(jnp.float32)
    shift_two = full_shift2.astype(jnp.float32)
    output, norm_two_pull = jax.vjp(layer_norm, resid_two, gain_two, shift_two)
    back_qkv = whole[0]
    back_out = whole[1]
    back_in = whole[2]
    back_back = whole[3]
    grad_output = cotangent[0].astype(jnp.float32)
    grad_resid2, grad_gain2, grad_shift2 = norm_two_pull(grad_output)
    grad_branch = grad_resid2.astype(jnp.bfloat16)
    grad_backb = jnp.sum(grad_branch.astype(jnp.float32), axis=0)
    grad_wback = jnp.einsum("rf,rd->fd", activ_low, grad_branch, preferred_element_type=jnp.float32)
    grad_activ = jnp.einsum("rd,fd->rf", grad_branch, back_back, preferred_element_type=jnp.float32)
    (grad_hidden,) = gelu_pull(grad_activ)
    grad_hidden_low = grad_hidden.astype(jnp.bfloat16)
    grad_inb = jnp.sum(grad_hidden_low.astype(jnp.float32), axis=0)
    grad_win = jnp.einsum(
        "rd,rf->df", normed_low, grad_hidden_low, preferred_element_type=jnp.float32
    )
    grad_normed = grad_resid2 + jnp.einsum(
        "rf,df->rd", grad_hidden_low, back_in, preferred_element_type=jnp.float32
    )
    grad_resid1, grad_gain1, grad_shift1 = norm_one_pull(grad_normed)
    grad_attn = grad_resid1.astype(jnp.bfloat16)
    grad_outb = jnp.sum(grad_attn.astype(jnp.float32), axis=0)
    grad_wout = jnp.einsum("rc,rd->cd", context_rows, grad_attn, preferred_element_type=jnp.float32)
    grad_context = jnp.einsum(
        "rd,cd->rc", grad_attn, back_out, preferred_element_type=jnp.float32
    ).astype(jnp.bfloat16)
    grad_ctx_heads = lax.all_to_all(
        grad_context.reshape(1, local_rows, head_count, group_width),
        "head",
        split_axis=2,
        concat_axis=1,
        tiled=True,
    )
    grad_ctx_all = grad_ctx_heads[0, :, 0]
    grad_keys = jnp.zeros((half_rows, group_heads, HD), jnp.float32)
    grad_values = jnp.zeros((half_rows, group_heads, HD), jnp.float32)
    grad_query_parts = []
    for block in range(block_count):
        query_block = queries[block * block_rows : (block + 1) * block_rows].reshape(
            block_rows, group_heads, HD
        )
        grad_ctx_block = grad_ctx_all[block * block_rows : (block + 1) * block_rows].reshape(
            block_rows, group_heads, HD
        )
        logits = logits_of(query_block)
        probs = jnp.exp(logits - lse_parts[block])
        probs_low = probs.astype(jnp.bfloat16)
        grad_probs = jnp.einsum(
            "qhd,khd->hqk", grad_ctx_block, values_three, preferred_element_type=jnp.float32
        )
        grad_values = grad_values + jnp.einsum(
            "hqk,qhd->khd", probs_low, grad_ctx_block, preferred_element_type=jnp.float32
        )
        inner = jnp.sum(probs * grad_probs, axis=-1, keepdims=True)
        grad_scores = (probs * (grad_probs - inner) * scale).astype(jnp.bfloat16)
        grad_query_block = jnp.einsum(
            "hqk,khd->qhd", grad_scores, keys_three, preferred_element_type=jnp.float32
        )
        grad_query_parts.append(grad_query_block.reshape(block_rows, group_width))
        grad_keys = grad_keys + jnp.einsum(
            "hqk,qhd->khd", grad_scores, query_block, preferred_element_type=jnp.float32
        )
    grad_kv_used = jnp.stack(
        [grad_keys.reshape(half_rows, group_width), grad_values.reshape(half_rows, group_width)]
    ).astype(jnp.bfloat16)
    grad_kv_far = partner(grad_kv_used, "blk", 0)
    grad_kv_mine = jnp.where(column_flag, grad_kv_far, grad_kv_used)
    grad_queries = jnp.concatenate(grad_query_parts, axis=0).astype(jnp.bfloat16)
    grad_stack = jnp.stack([grad_queries, grad_kv_mine[0], grad_kv_mine[1]], axis=1).reshape(
        1, half_rows, 3, 1, group_width
    )
    grad_proj = lax.all_to_all(grad_stack, "head", split_axis=1, concat_axis=3, tiled=True).reshape(
        local_rows, 3 * model_width
    )
    grad_qbias = jnp.sum(grad_proj[:, :model_width].astype(jnp.float32), axis=0)
    grad_vbias = jnp.sum(grad_proj[:, 2 * model_width :].astype(jnp.float32), axis=0)
    grad_wqkv = jnp.einsum("rd,rc->dc", inputs, grad_proj, preferred_element_type=jnp.float32)
    grad_inputs = grad_resid1 + jnp.einsum(
        "rc,dc->rd", grad_proj, back_qkv, preferred_element_type=jnp.float32
    )
    summed = (
        lax.psum_scatter(grad_wqkv, ("head", "blk"), scatter_dimension=0, tiled=True),
        lax.psum_scatter(grad_wout, ("head", "blk"), scatter_dimension=0, tiled=True),
        lax.psum_scatter(grad_win, ("head", "blk"), scatter_dimension=0, tiled=True),
        lax.psum_scatter(grad_wback, ("head", "blk"), scatter_dimension=0, tiled=True),
        lax.psum_scatter(grad_qbias, ("head", "blk"), scatter_dimension=0, tiled=True),
        lax.psum_scatter(grad_vbias, ("head", "blk"), scatter_dimension=0, tiled=True),
        lax.psum_scatter(grad_outb, ("head", "blk"), scatter_dimension=0, tiled=True),
        lax.psum_scatter(grad_inb, ("head", "blk"), scatter_dimension=0, tiled=True),
        lax.psum_scatter(grad_backb, ("head", "blk"), scatter_dimension=0, tiled=True),
        lax.psum_scatter(grad_gain1, ("head", "blk"), scatter_dimension=0, tiled=True),
        lax.psum_scatter(grad_shift1, ("head", "blk"), scatter_dimension=0, tiled=True),
        lax.psum_scatter(grad_gain2, ("head", "blk"), scatter_dimension=0, tiled=True),
        lax.psum_scatter(grad_shift2, ("head", "blk"), scatter_dimension=0, tiled=True),
    )
    (
        sum_wqkv,
        sum_wout,
        sum_win,
        sum_wback,
        sum_qbias,
        sum_vbias,
        sum_outb,
        sum_inb,
        sum_backb,
        sum_gain1,
        sum_shift1,
        sum_gain2,
        sum_shift2,
    ) = summed
    return (
        output.astype(jnp.bfloat16)[None],
        grad_inputs[None],
        sum_wqkv,
        sum_qbias,
        sum_vbias,
        sum_wout,
        sum_outb,
        sum_gain1,
        sum_shift1,
        sum_win,
        sum_inb,
        sum_wback,
        sum_backb,
        sum_gain2,
        sum_shift2,
    )


def solution(mesh):
    placed = (
        P("blk", "head", None),
        P(),
        P(),
        P(("head", "blk"), None),
        P(("head", "blk")),
        P(("head", "blk")),
        P(("head", "blk"), None),
        P(("head", "blk")),
        P(("head", "blk")),
        P(("head", "blk")),
        P(("head", "blk"), None),
        P(("head", "blk")),
        P(("head", "blk"), None),
        P(("head", "blk")),
        P(("head", "blk")),
        P(("head", "blk")),
        P("blk", "head", None),
    )
    return jax.shard_map(
        per_device,
        mesh=mesh,
        in_specs=placed,
        out_specs=(
            P("blk", "head", None),
            P("blk", "head", None),
            P(("head", "blk"), None),
            P(("head", "blk")),
            P(("head", "blk")),
            P(("head", "blk"), None),
            P(("head", "blk")),
            P(("head", "blk")),
            P(("head", "blk")),
            P(("head", "blk"), None),
            P(("head", "blk")),
            P(("head", "blk"), None),
            P(("head", "blk")),
            P(("head", "blk")),
            P(("head", "blk")),
        ),
        check_vma=False,
    )
```

profile of v0, /device:TPU:0, one launch (start us, length us, event | category | flops | bytes accessed | tf_op | source)
XLA Modules:
  0.0 1208.8 jit_solution(14878470684103308758)
XLA Ops:
  17.0 42.5 %all-reduce.19 = (bf16[768]{0:T(1024)(128)(2,1)S(1)}, bf16[768]{0:T(1024)(128)(2,1)S(1)}, bf16[768]{0:T(1024)(128)(2,1)S(1)}, bf16[768]{0:T(1024)(128)(2,1)S(1)}...) all-reduce(bf16[768]{0:T(1024)(128)(2,1)S(1)} %dynamic-update-slice, ...), channel_id=1, replica_groups=mesh['head'=2,'blk'=16] {'head','blk'}, use_global_device_ids=true, to_apply=%add.1 | all-reduce | flops 9216 | bytes 36864
  59.5 14.2 %all-gather.5.cloned.1.call-done = bf16[768,2304]{1,0:T(8,128)(2,1)} async-done(((bf16[24,2304]{1,0:T(8,128)(2,1)}), bf16[768,2304]{1,0:T(8,128)(2,1)}) %all-gather.5.cloned.1.call-update) | async-done | bytes 3538960 | tf_op jit(solution)/shard_map/all_gather | solution.py:46
  130.3 58.6 %collective-permute-done = bf16[2,2048,384]{2,1,0:T(8,128)(2,1)} collective-permute-done((bf16[2,2048,384]{2,1,0:T(8,128)(2,1)}, bf16[2,2048,384]{2,1,0:T(8,128)(2,1)}, u32[]{:S(2)}, u32[]{:S(2)}) %collective-permute-start) | collective-permute-done | bytes 3145760 | tf_op jit(solution)/shard_map/ppermute | solution.py:13
  227.1 36.4 %fusion.8 = (f32[6,512]{1,0:T(8,128)}, f32[6,512]{1,0:T(8,128)}, f32[6,512]{1,0:T(8,128)}, f32[6,512]{1,0:T(8,128)}, f32[6,512,2048]{2,1,0:T(8,128)}) fusion(f32[6,512,2048]{2,1,0:T(8,128)} %get-tuple-element.148, f32[6,512]{1,0:T(8,128)} %get-tuple-element.147, pred[6,2048]{1,0:T(8,128)(4,1)S(1)} %add_compare_fusion, f32[6,512,2048]{2,1,0:T(8,128)} %fusion.241, ...), kind=kOutput, calls=%fused_computation.32 | convolution fusion | flops 887083008 | bytes 102703104 | tf_op jit(solution)/shard_map/qhd,khd->hqk/dot_general | solution.py:111
  263.6 26.0 %fusion.9 = (f32[6,512]{1,0:T(8,128)S(1)}, f32[6,512]{1,0:T(8,128)S(1)}, f32[6,512]{1,0:T(8,128)S(1)}) fusion(f32[6,512,2048]{2,1,0:T(8,128)} %get-tuple-element.149, f32[6,512]{1,0:T(8,128)} %get-tuple-element.100, pred[6,2048]{1,0:T(8,128)(4,1)S(1)} %add_compare_fusion, f32[6,512]{1,0:T(8,128)} %get-tuple-element.101, f32[6,512,2048]{2,1,0:T(8,128)} %fusion.241, ...), kind=kLoop, calls=%fused_computation.33 | loop fusion | flops 75488256 | bytes 75583488 | tf_op jit(solution)/shard_map/reduce_sum | solution.py:125
  342.3 17.7 %fusion.240 = bf16[2048,1,1,384]{3,2,1,0:T(2,128)(2,1)S(1)} fusion(bf16[1,512,1,384]{3,2,0,1:T(2,128)(2,1)} %copy.144, bf16[1,512,1,384]{3,2,0,1:T(2,128)(2,1)} %copy.143, bf16[1,512,1,384]{3,2,0,1:T(2,128)(2,1)} %copy.142, bf16[1,512,1,384]{3,2,0,1:T(2,128)(2,1)} %copy.141), kind=kLoop, calls=%fused_computation.236 | loop fusion | flops 2359296 | bytes 3145728
  360.5 34.4 %reduce.1 = bf16[2048,384]{1,0:T(8,128)(2,1)} reduce(bf16[2048,1,1,384]{3,2,1,0:T(2,128)(2,1)S(1)} %fusion.240, bf16[]{:T(256)} %broadcast.325), dimensions={1,2}, to_apply=%fusion.240.reduce_sub_computation | reduce | bytes 3145730
  413.3 38.1 %multiply_convert_fusion.4 = (bf16[1024,3072]{1,0:T(8,128)(2,1)}, f32[1024,3072]{1,0:T(8,128)}, f32[1024,3072]{1,0:T(8,128)}) fusion(f32[3072]{0:T(1024)S(1)} %copy-done.51, bf16[768,3072]{1,0:T(8,128)(2,1)} %all-gather.9.cloned.1.call-done, f32[1024,768]{0,1:T(8,128)S(1)} %get-tuple-element.151, f32[768]{0:T(1024)S(1)} %copy-done.53, ...), kind=kOutput, calls=%fused_computation.64 | convolution fusion | flops 5043388416 | bytes 39348224 | tf_op jit(solution)/shard_map/dot_general | solution.py:148
  467.4 18.0 %convert_reduce_fusion = (f32[3072]{0:T(1024)}, bf16[1024,3072]{1,0:T(8,128)(2,1)}) fusion(f32[1024,3072]{1,0:T(8,128)} %get-tuple-element.131, bf16[1024,768]{0,1:T(8,128)(2,1)S(1)} %get-tuple-element.125, bf16[3072,768]{1,0:T(8,128)(2,1)} %all-gather.11.cloned.1.call-done, f32[1024,3072]{1,0:T(8,128)} %get-tuple-element.152, f32[3072]{0:T(1024)S(1)} %copy-done.51), kind=kOutput, calls=%fused_computation.54 | convolution fusion | flops 4885312512 | bytes 37773312 | tf_op jit(solution)/shard_map/rd,fd->rf/dot_general | solution.py:169
  527.4 13.0 %fusion.110 = f32[6,64,2048]{2,1,0:T(8,128)} fusion(bf16[512,6,64]{0,2,1:T(8,128)(2,1)S(1)} %bitcast.206, f32[6,512,2048]{2,1,0:T(8,128)} %get-tuple-element.149, f32[6,512]{1,0:T(8,128)S(1)} %get-tuple-element.160, pred[6,2048]{1,0:T(8,128)(4,1)S(1)} %copy-done.28), kind=kOutput, calls=%fused_computation.95 | convolution fusion | flops 830472192 | bytes 28729344 | tf_op jit(solution)/shard_map/hqk,qhd->khd/dot_general | solution.py:210
  540.4 12.9 %fusion.108 = f32[6,64,2048]{2,1,0:T(8,128)} fusion(bf16[512,6,64]{0,2,1:T(8,128)(2,1)S(1)} %bitcast.208, f32[6,512,2048]{2,1,0:T(8,128)} %fusion.241, f32[6,512]{1,0:T(8,128)S(1)} %get-tuple-element.159, pred[6,2048]{1,0:T(8,128)(4,1)S(1)} %copy-done.28), kind=kOutput, calls=%fused_computation.94 | convolution fusion | flops 830472192 | bytes 28729344 | tf_op jit(solution)/shard_map/hqk,qhd->khd/dot_general | solution.py:210
  553.3 12.9 %fusion.106 = f32[6,64,2048]{2,1,0:T(8,128)} fusion(bf16[512,6,64]{0,2,1:T(8,128)(2,1)S(1)} %bitcast.204, f32[6,512,2048]{2,1,0:T(8,128)} %fusion.242, f32[6,512]{1,0:T(8,128)S(1)} %get-tuple-element.158, pred[6,2048]{1,0:T(8,128)(4,1)S(1)} %copy-done.28), kind=kOutput, calls=%fused_computation.93 | convolution fusion | flops 830472192 | bytes 28729344 | tf_op jit(solution)/shard_map/hqk,qhd->khd/dot_general | solution.py:210
  573.9 15.9 %add_convert_fusion.2 = bf16[6,64,2048]{2,1,0:T(8,128)(2,1)} fusion(f32[6,64,2048]{2,1,0:T(8,128)} %fusion.106, f32[6,64,2048]{2,1,0:T(8,128)} %fusion.108, f32[6,64,2048]{2,1,0:T(8,128)} %fusion.110, bf16[512,6,64]{0,2,1:T(8,128)(2,1)S(1)} %bitcast.196, f32[6,512,2048]{2,1,0:T(8,128)} %get-tuple-element.148, f32[6,512]{1,0:T(8,128)S(1)} %get-tuple-element.161, ...), kind=kOutput, calls=%fused_computation.136 | convolution fusion | flops 833617920 | bytes 36593664 | tf_op jit(solution)/shard_map/hqk,qhd->khd/dot_general | solution.py:210
  601.9 46.8 %fusion.20 = f32[6,64,2048]{2,1,0:T(8,128)} fusion(bf16[512,6,64]{0,2,1:T(8,128)(2,1)} %bitcast.202, f32[6,512,2048]{2,1,0:T(8,128)} %fusion.243, f32[6,512,2048]{2,1,0:T(8,128)} %get-tuple-element.148, f32[6,512]{1,0:T(8,128)} %copy-done.33, pred[6,2048]{1,0:T(8,128)(4,1)S(1)} %copy-done.28), kind=kOutput, calls=%fused_computation.42 | convolution fusion | flops 874517504 | bytes 53895168 | tf_op jit(solution)/shard_map/hqk,qhd->khd/dot_general | solution.py:219
  659.8 46.7 %fusion.38 = f32[6,64,2048]{2,1,0:T(8,128)} fusion(bf16[512,6,64]{0,2,1:T(8,128)(2,1)S(1)} %bitcast.201, f32[6,512,2048]{2,1,0:T(8,128)} %fusion.245, f32[6,512,2048]{2,1,0:T(8,128)} %fusion.241, f32[6,512]{1,0:T(8,128)} %copy-done.49, pred[6,2048]{1,0:T(8,128)(4,1)S(1)} %copy-done.28), kind=kOutput, calls=%fused_computation.48 | convolution fusion | flops 874517504 | bytes 53895168 | tf_op jit(solution)/shard_map/hqk,qhd->khd/dot_general | solution.py:219
  717.8 46.9 %fusion.29 = f32[6,64,2048]{2,1,0:T(8,128)} fusion(bf16[512,6,64]{0,2,1:T(8,128)(2,1)S(1)} %bitcast.215, f32[6,512,2048]{2,1,0:T(8,128)} %fusion.244, f32[6,512,2048]{2,1,0:T(8,128)} %get-tuple-element.149, f32[6,512]{1,0:T(8,128)} %copy-done.48, pred[6,2048]{1,0:T(8,128)(4,1)S(1)} %copy-done.28), kind=kOutput, calls=%fused_computation.45 | convolution fusion | flops 874517504 | bytes 53895168 | tf_op jit(solution)/shard_map/hqk,qhd->khd/dot_general | solution.py:219
  776.8 44.8 %add_convert_fusion.3 = bf16[6,64,2048]{2,1,0:T(8,128)(2,1)} fusion(f32[6,64,2048]{2,1,0:T(8,128)} %fusion.38, f32[6,64,2048]{2,1,0:T(8,128)} %fusion.20, f32[6,64,2048]{2,1,0:T(8,128)} %fusion.29, bf16[512,6,64]{0,2,1:T(8,128)(2,1)S(1)} %bitcast.199, f32[6,512,2048]{2,1,0:T(8,128)} %fusion.246, f32[6,512,2048]{2,1,0:T(8,128)} %fusion.242, ...), kind=kOutput, calls=%fused_computation.137 | convolution fusion | flops 877663232 | bytes 61759488 | tf_op jit(solution)/shard_map/hqk,qhd->khd/dot_general | solution.py:219
  829.9 44.2 %fusion.165 = bf16[6,64,512]{2,1,0:T(8,128)(2,1)} fusion(bf16[2048,6,64]{0,2,1:T(8,128)(2,1)S(1)} %bitcast.181, f32[6,512,2048]{2,1,0:T(8,128)} %fusion.243, f32[6,512,2048]{2,1,0:T(8,128)} %get-tuple-element.148, f32[6,512]{1,0:T(8,128)} %copy-done.33, pred[6,2048]{1,0:T(8,128)(4,1)S(1)} %copy-done.28), kind=kOutput, calls=%fused_computation.166 | convolution fusion | flops 874714112 | bytes 52322304 | tf_op jit(solution)/shard_map/hqk,khd->qhd/dot_general | solution.py:215
  875.3 44.0 %fusion.156 = bf16[6,64,512]{2,1,0:T(8,128)(2,1)} fusion(bf16[2048,6,64]{0,2,1:T(8,128)(2,1)S(1)} %bitcast.182, f32[6,512,2048]{2,1,0:T(8,128)} %fusion.246, f32[6,512,2048]{2,1,0:T(8,128)} %fusion.242, f32[6,512]{1,0:T(8,128)} %copy-done.50, pred[6,2048]{1,0:T(8,128)(4,1)S(1)} %copy-done.28), kind=kOutput, calls=%fused_computation.163 | convolution fusion | flops 874714112 | bytes 52322304 | tf_op jit(solution)/shard_map/hqk,khd->qhd/dot_general | solution.py:215
  921.3 44.2 %fusion.159 = bf16[6,64,512]{2,1,0:T(8,128)(2,1)} fusion(bf16[2048,6,64]{0,2,1:T(8,128)(2,1)S(1)} %bitcast.183, f32[6,512,2048]{2,1,0:T(8,128)} %fusion.245, f32[6,512,2048]{2,1,0:T(8,128)} %fusion.241, f32[6,512]{1,0:T(8,128)} %copy-done.49, pred[6,2048]{1,0:T(8,128)(4,1)S(1)} %copy-done.28), kind=kOutput, calls=%fused_computation.164 | convolution fusion | flops 874714112 | bytes 52322304 | tf_op jit(solution)/shard_map/hqk,khd->qhd/dot_general | solution.py:215
  967.4 44.5 %fusion.162 = bf16[6,64,512]{2,1,0:T(8,128)(2,1)} fusion(bf16[2048,6,64]{0,2,1:T(8,128)(2,1)S(1)} %bitcast.184, f32[6,512,2048]{2,1,0:T(8,128)} %fusion.244, f32[6,512,2048]{2,1,0:T(8,128)} %get-tuple-element.149, f32[6,512]{1,0:T(8,128)} %copy-done.48, pred[6,2048]{1,0:T(8,128)(4,1)S(1)} %copy-done.28), kind=kOutput, calls=%fused_computation.165 | convolution fusion | flops 874714112 | bytes 52322304 | tf_op jit(solution)/shard_map/hqk,khd->qhd/dot_general | solution.py:215
  1017.2 31.8 %copy.159 = bf16[1,2048,3,1,384]{4,2,3,0,1:T(4,128)(2,1)S(1)} copy(bf16[1,2048,3,1,384]{4,1,2,3,0:T(8,128)(2,1)S(1)} %maximum_bitcast_fusion) | data formatting | bytes 9437184 | tf_op jit(solution)/shard_map/reshape | solution.py:228
  1099.0 39.7 %all-reduce.18 = (f32[768]{0:T(1024)S(1)}, f32[768]{0:T(1024)S(1)}, f32[768]{0:T(1024)S(1)}, f32[768]{0:T(1024)S(1)}, f32[768]{0:T(1024)S(1)}, /*index=5*/f32[30...) all-reduce(f32[768]{0:T(1024)S(1)} %get-tuple-element.95, ...), channel_id=3, replica_groups=mesh['head'=2,'blk'=16] {'head','blk'}, use_global_device_ids=true, to_apply=%region_22.23.clone | all-reduce | flops 9216 | bytes 73728
  1143.9 57.8 %reduce-scatter.13.cloned.1.call-done = f32[24,2304]{1,0:T(8,128)} async-done(((f32[768,2304]{1,0:T(8,128)}), f32[24,2304]{1,0:T(8,128)}) %reduce-scatter.13.cloned.1.call-update) | async-done | bytes 221200
  (281 shorter events, 361.6 us)
Async XLA Ops:
  7.2 66.5 %all-gather.5.cloned.1.call-start = ((), (), s32[]{:S(2)}) async-start(), calls=%async_computation.8 | async-start | bytes 3649536 | tf_op jit(solution)/shard_map/all_gather | solution.py:46
  7.9 401.0 %all-gather.7.cloned.1.call-start = ((), (), s32[]{:S(2)}) async-start(), calls=%async_computation.9 | async-start | bytes 1216512 | tf_op jit(solution)/shard_map/all_gather | solution.py:47
  8.7 404.6 %all-gather.9.cloned.1.call-start = ((), (), s32[]{:S(2)}) async-start(), calls=%async_computation.10 | async-start | bytes 4866048 | tf_op jit(solution)/shard_map/all_gather | solution.py:48
  9.4 442.0 %all-gather.11.cloned.1.call-start = ((), (), s32[]{:S(2)}) async-start(), calls=%async_computation.11 | async-start | bytes 4866048 | tf_op jit(solution)/shard_map/all_gather | solution.py:49
  107.3 81.6 %collective-permute-start = (bf16[2,2048,384]{2,1,0:T(8,128)(2,1)}, bf16[2,2048,384]{2,1,0:T(8,128)(2,1)}, u32[]{:S(2)}, u32[]{:S(2)}) collective-permute-start(bf16[2,2048,384]{2,1,0:T(8,128)(2,1)} %pad_maximum_fusion), channel_id=1, source_target_pairs={{0,1},{1,0},{2,3},{3,2},{4,5},{5,4},{6,7},{7,6},{8,9},{9,8},{10,11... | collective-permute-start | bytes 9437192 | tf_op jit(solution)/shard_map/ppermute | solution.py:13
  108.8 1035.2 %reduce-scatter.7.cloned.1.call-start = ((), (), s32[]{:S(2)}) async-start(), calls=%async_computation.12 | async-start | bytes 2433024 | tf_op jit(solution)/shard_map/reduce_scatter | solution.py:242
  121.9 201.8 %copy-start.27 = (pred[6,2048]{1,0:T(8,128)(4,1)}, pred[6,2048]{1,0:T(8,128)(4,1)S(1)}, u32[]{:S(2)}) copy-start(pred[6,2048]{1,0:T(8,128)(4,1)S(1)} %add_compare_fusion) | copy-start | bytes 36868
  130.3 75.7 %copy-start.12 = (bf16[1,512,1,1,384]{1,4,3,2,0:T(8,128)(2,1)}, bf16[1,512,1,1,384]{1,4,3,2,0:T(8,128)(2,1)S(1)}, u32[]{:S(2)}) copy-start(bf16[1,512,1,1,384]{1,4,3,2,0:T(8,128)(2,1)S(1)} %copy.140) | copy-start | bytes 1179652
  193.5 33.7 %copy-start.2 = (bf16[1,2048,384]{1,2,0:T(8,128)(2,1)}, bf16[1,2048,384]{1,2,0:T(8,128)(2,1)S(1)}, u32[]{:S(2)}) copy-start(bf16[1,2048,384]{1,2,0:T(8,128)(2,1)S(1)} %copy.137) | copy-start | bytes 4718596
  195.8 127.9 %copy-start = (bf16[1,2048,384]{1,2,0:T(8,128)(2,1)}, bf16[1,2048,384]{1,2,0:T(8,128)(2,1)S(1)}, u32[]{:S(2)}) copy-start(bf16[1,2048,384]{1,2,0:T(8,128)(2,1)S(1)} %copy.135) | copy-start | bytes 4718596
  263.6 26.0 %copy-start.34 = (f32[6,512]{1,0:T(8,128)S(1)}, f32[6,512]{1,0:T(8,128)}, u32[]{:S(2)}) copy-start(f32[6,512]{1,0:T(8,128)} %get-tuple-element.101) | copy-start | bytes 36868
  289.6 34.2 %copy-start.39 = (f32[6,512]{1,0:T(8,128)}, f32[6,512]{1,0:T(8,128)S(1)}, u32[]{:S(2)}) copy-start(f32[6,512]{1,0:T(8,128)S(1)} %get-tuple-element.103) | copy-start | bytes 36868
  360.0 49.0 %copy-start.55 = (f32[768]{0:T(1024)S(1)}, f32[768]{0:T(1024)}, u32[]{:S(2)}) copy-start(f32[768]{0:T(1024)} %convert_element_type.136) | copy-start | bytes 9220
  412.8 38.6 %copy-start.8 = (f32[1024,768]{0,1:T(8,128)}, f32[1024,768]{0,1:T(8,128)S(1)}, u32[]{:S(2)}) copy-start(f32[1024,768]{0,1:T(8,128)S(1)} %get-tuple-element.151) | copy-start | bytes 9437188
  413.2 38.2 %copy-start.54 = (f32[768]{0:T(1024)S(1)}, f32[768]{0:T(1024)}, u32[]{:S(2)}) copy-start(f32[768]{0:T(1024)} %convert_element_type.142) | copy-start | bytes 9220
  504.5 639.4 %reduce-scatter.9.cloned.1.call-start = ((), (), s32[]{:S(2)}) async-start(), calls=%async_computation.13 | async-start | bytes 9732096 | tf_op jit(solution)/shard_map/reduce_scatter | solution.py:243
  515.1 628.8 %reduce-scatter.11.cloned.1.call-start = ((), (), s32[]{:S(2)}) async-start(), calls=%async_computation.14 | async-start | bytes 9732096 | tf_op jit(solution)/shard_map/reduce_scatter | solution.py:244
  525.2 28.1 %copy-start.17 = (bf16[512,384]{0,1:T(8,128)(2,1)}, bf16[512,384]{0,1:T(8,128)(2,1)S(1)}, u32[]{:S(2)}) copy-start(bf16[512,384]{0,1:T(8,128)(2,1)S(1)} %copy.152) | copy-start | bytes 1179652
  526.6 47.3 %copy-start.33 = (f32[6,512]{1,0:T(8,128)}, f32[6,512]{1,0:T(8,128)S(1)}, u32[]{:S(2)}) copy-start(f32[6,512]{1,0:T(8,128)S(1)} %get-tuple-element.161) | copy-start | bytes 36868
  527.4 25.9 %copy-start.50 = (f32[6,512]{1,0:T(8,128)}, f32[6,512]{1,0:T(8,128)S(1)}, u32[]{:S(2)}) copy-start(f32[6,512]{1,0:T(8,128)S(1)} %get-tuple-element.158) | copy-start | bytes 36868
  540.4 25.8 %slice-start = ((s8[6291456]{0:T(1024)(128)(4,1)}), s8[4194304]{0:T(1024)(128)(4,1)S(1)}, s32[]{:S(2)}) async-start(s8[6291456]{0:T(1024)(128)(4,1)} %bitcast.224), calls=%async_computation.16 | async-start | bytes 8388608
  573.9 627.8 %reduce-scatter.13.cloned.1.call-start = ((), (), s32[]{:S(2)}) async-start(), calls=%async_computation.15 | async-start | bytes 7299072
  776.8 53.1 %copy-start.3 = (bf16[1,2048,384]{1,2,0:T(8,128)(2,1)S(1)}, bf16[1,2048,384]{1,2,0:T(8,128)(2,1)}, u32[]{:S(2)}) copy-start(bf16[1,2048,384]{1,2,0:T(8,128)(2,1)} %copy-done.2) | copy-start | bytes 4718596
  827.7 185.4 %collective-permute-start.1 = (bf16[2,2048,384]{2,1,0:T(8,128)(2,1)}, bf16[2,2048,384]{2,1,0:T(8,128)(2,1)}, u32[]{:S(2)}, u32[]{:S(2)}) collective-permute-start(bf16[2,2048,384]{2,1,0:T(8,128)(2,1)} %pad_maximum_fusion.2), channel_id=1, source_target_pairs={{0,1},{1,0},{2,3},{3,2},{4,5},{5,4},{6,7},{7,6},{8,9},{9,8},{10,11... | collective-permute-start | bytes 9437192 | tf_op jit(solution)/shard_map/ppermute | solution.py:13
  (47 other events, 487.4 us)
Sparse Core Ops, SparseCore 0:
  10.9 62.7 all-gather.4
  76.6 54.3 all-gather.6
  133.9 68.0 all-gather.8
  204.7 62.5 all-gather.10
  504.6 98.8 reduce-scatter.6
  610.9 134.6 reduce-scatter.8
  752.1 142.3 reduce-scatter.10
  1083.9 117.7 reduce-scatter.12
where the time goes:
time: 1220 us; the launch traced here: 1210 us
  matrix products  705 us (58%)
  waiting for transfers between devices  133 us (11%)
  local copies, waits for them, and re-layouts  133 us (11%)
  blocking collectives  110 us (9%)
  other arithmetic  109 us (9%)
  between operations  15.4 us (1%)
    dot_general x4, matrix products, per_device(): jnp.einsum('hqk,qhd->khd', grad_scores, query_block, preferred_element_ty...  185 us
    dot_general x4, matrix products, per_device(): jnp.einsum('hqk,khd->qhd', grad_scores, keys_three, preferred_element_typ...  177 us
    unnamed x2, blocking collectives  82.1 us
    dot_general x4, matrix products, logits_of(): jnp.einsum('qhd,khd->hqk', query_block, keys_three, preferred_element_typ...  67.7 us
    unnamed x9, waiting for transfers between devices  59.9 us
    ppermute x2, waiting for transfers between devices, partner(): return lax.ppermute(value, axis, pairs)  58.6 us
    dot_general x4, matrix products, per_device(): jnp.einsum('hqk,qhd->khd', probs_low, grad_ctx_block, preferred_element_t...  54.6 us
    unnamed x3, other arithmetic  52.1 us
  transfers between devices with their start and end apart: 10, of which 3 were waited for; matrix products, arithmetic and copies ran while one was open for 74% of the time, Pallas kernels for 0%

commit v1 on v0

v1 whole, which is shorter than its diff:
```python
import functools

import jax
import jax.numpy as jnp
from jax import lax
from jax.experimental import pallas as pl
from jax.experimental.pallas import tpu as pltpu
from jax.sharding import PartitionSpec as P

HEADS = 12
HD = 64
LANES = 128
NEG = -1e30
EPS = 1e-06
SAFE_LOGIT = 60.0
BF16 = jnp.bfloat16
F32 = jnp.float32
NT = (((1,), (1,)), ((), ()))
VMEM_BYTES = 58 << 20


def dot(a, b):
    return jnp.dot(a, b, preferred_element_type=F32)


def dot_nt(a, b):
    return lax.dot_general(a, b, NT, preferred_element_type=F32)


def swap(value, axis, apart):
    pairs = [(source, source ^ apart) for source in range(lax.axis_size(axis))]
    return lax.ppermute(value, axis, pairs)


def place(mine, theirs, upper, axis):
    return jnp.stack([jnp.where(upper, theirs, mine), jnp.where(upper, mine, theirs)], axis=axis)


def gather_blk(pair):
    count = lax.axis_size("blk")
    index = lax.axis_index("blk")
    bits = [1 << b for b in range(count.bit_length() - 1)][::-1]
    held = pair
    depth = 1
    for bit in bits[:-2]:
        held = place(held, swap(held, "blk", bit), (index & bit) != 0, depth)
        depth += 1
    first, second = held[0], held[1]
    depth -= 1
    high, low = bits[-2], bits[-1]
    first_in = swap(first, "blk", high)
    second_in = swap(second, "blk", low)
    first = place(first, first_in, (index & high) != 0, depth)
    second = place(second, second_in, (index & low) != 0, depth)
    first_in = swap(first, "blk", low)
    second_in = swap(second, "blk", high)
    first = place(first, first_in, (index & low) != 0, depth + 1)
    second = place(second, second_in, (index & high) != 0, depth)
    return tuple(a.reshape((count,) + pair.shape[1:]) for a in (first, second))


def first_head(rows):
    lane = lax.broadcasted_iota(jnp.int32, (rows, LANES), 1)
    return lane < HD, lane % HD


def key_rows(own, sub, keys, row, sc, source, heads):
    at = lax.broadcasted_iota(jnp.int32, keys.shape, 0) + row
    bound, local, core = sc[heads + source], sc[heads + 2], sc[heads + 3]
    position = jnp.where(at < local, at + core * local, at - core * local)
    bias = jnp.where(position < bound, 0.0, NEG)
    extra = jnp.where(sub < 3, -1.0, jnp.where(sub == 3, bias, 0.0))
    return jnp.where(own, keys.astype(F32), extra).astype(BF16)


def three_parts(value):
    first = value.astype(BF16).astype(F32)
    rest = value - first
    second = rest.astype(BF16).astype(F32)
    return first, second, rest - second


def attend_kernel(
    sc, q_ref, ka_ref, kb_ref, va_ref, vb_ref, o_ref, lse_ref, keys, values, key_norm, *, heads, step
):
    pair = pl.program_id(0)
    count = keys.shape[1]
    rows = q_ref.shape[1]
    scale = HD ** (-0.5)

    @pl.when(pl.program_id(1) == 0)
    def _():
        piece = min(512, count)
        own0, sub = first_head(piece)
        for h, (k_ref, v_ref) in enumerate(((ka_ref, va_ref), (kb_ref, vb_ref))):
            source = sc[2 * pair + h]
            own = own0 if h == 0 else jnp.logical_not(own0)
            largest = jnp.float32(0.0)
            for r in range(0, count, piece):
                k = k_ref[0, r : r + piece, :]
                keys[h, r : r + piece, :] = key_rows(own, sub, k, r, sc, source, heads)
                values[h, :HD, r : r + piece] = v_ref[0, r : r + piece, :].T[h * HD : (h + 1) * HD, :]
                values[h, HD:, r : r + piece] = jnp.ones((16, piece), BF16)
                k = jnp.where(own, k.astype(F32), 0.0)
                largest = jnp.maximum(largest, jnp.max(jnp.sum(k * k, axis=1, keepdims=True)))
            key_norm[h] = largest

    q = q_ref[0].astype(F32) * scale
    own0, sub = first_head(rows)
    one = jnp.where(sub == 3, 1.0, 0.0)
    square = q * q
    norm_a = jnp.max(jnp.sum(jnp.where(own0, square, 0.0), axis=1, keepdims=True))
    norm_b = jnp.max(jnp.sum(jnp.where(own0, 0.0, square), axis=1, keepdims=True))
    largest = jnp.maximum(norm_a * key_norm[0], norm_b * key_norm[1])
    small = largest < SAFE_LOGIT * SAFE_LOGIT

    def queries(h):
        return (jnp.where(own0, q, one) if h == 0 else jnp.where(own0, one, q)).astype(BF16)

    def finish(outs, peaks):
        totals = [jnp.broadcast_to(o[HD : HD + 1, :], (HD, rows)) for o in outs]
        o_ref[...] = (
            jnp.concatenate([o[:HD, :] / t for o, t in zip(outs, totals)], axis=0).T.astype(BF16)
        )
        lse = jnp.concatenate([jnp.log(totals[1]), jnp.log(totals[0])], axis=0).T
        if peaks is not None:
            lse = lse + jnp.where(own0, peaks[1], peaks[0])
        lse_ref[...] = lse

    @pl.when(small)
    def _():
        outs = []
        for h in (0, 1):
            qa = queries(h)
            out = None
            for c in range(0, count, step):
                p = jnp.exp(dot_nt(qa, keys[h, c : c + step, :])).astype(BF16)
                part = dot_nt(values[h, :, c : c + step], p)
                out = part if out is None else out + part
            outs.append(out)
        finish(outs, None)

    @pl.when(jnp.logical_not(small))
    def _():
        outs, peaks = [], []
        for h in (0, 1):
            s = dot_nt(queries(h), keys[h])
            peak = jnp.max(s, axis=1, keepdims=True)
            outs.append(dot_nt(values[h], jnp.exp(s - peak).astype(BF16)))
            peaks.append(peak)
        finish(outs, peaks)


def pair_specs(count, width):
    pairs = width // LANES

    def key_value(h, base):
        return pl.BlockSpec((1, count, LANES), lambda p, i, sc: (sc[2 * p + h], 0, base * pairs + p))

    return [key_value(0, 1), key_value(1, 1), key_value(0, 2), key_value(1, 2)]


def attend(sc, qkv, width):
    count = qkv.shape[1]
    rows = min(1024, count)
    row_spec = pl.BlockSpec((rows, LANES), lambda p, i, sc: (i, p))
    q_spec = pl.BlockSpec((1, rows, LANES), lambda p, i, sc: (0, i, p))
    heads = width // HD
    return pl.pallas_call(
        functools.partial(attend_kernel, heads=heads, step=min(512, count)),
        grid_spec=pltpu.PrefetchScalarGridSpec(
            num_scalar_prefetch=1,
            grid=(width // LANES, count // rows),
            in_specs=[q_spec] + pair_specs(count, width),
            out_specs=[row_spec, row_spec],
            scratch_shapes=[
                pltpu.VMEM((2, count, LANES), BF16),
                pltpu.VMEM((2, HD + 16, count), BF16),
                pltpu.SMEM((2,), F32),
            ],
        ),
        out_shape=[
            jax.ShapeDtypeStruct((count, width), BF16),
            jax.ShapeDtypeStruct((count, width), F32),
        ],
        compiler_params=pltpu.CompilerParams(vmem_limit_bytes=VMEM_BYTES),
        cost_estimate=pl.CostEstimate(
            flops=4 * 4 * count * count * width,
            bytes_accessed=2 * 6 * count * width,
            transcendentals=heads * count * count,
        ),
        name="attend",
    )(sc, qkv, qkv, qkv, qkv, qkv)


def attend_back_kernel(
    sc,
    q_ref,
    ka_ref,
    kb_ref,
    va_ref,
    vb_ref,
    o_ref,
    lse_ref,
    do_ref,
    dq_ref,
    dk_ref,
    dv_ref,
    keys,
    values,
    dk_sum,
    dv_sum,
    *,
    heads,
    step,
):
    pair = pl.program_id(0)
    block = pl.program_id(1)
    count = keys.shape[1]
    rows = q_ref.shape[1]
    scale = HD ** (-0.5)

    @pl.when(block == 0)
    def _():
        piece = min(512, count)
        own0, sub = first_head(piece)
        for h, (k_ref, v_ref) in enumerate(((ka_ref, va_ref), (kb_ref, vb_ref))):
            source = sc[2 * pair + h]
            own = own0 if h == 0 else jnp.logical_not(own0)
            for r in range(0, count, piece):
                k = k_ref[0, r : r + piece, :]
                keys[h, r : r + piece, :] = key_rows(own, sub, k, r, sc, source, heads)
                v = v_ref[0, r : r + piece, :].astype(F32)
                values[h, r : r + piece, :] = jnp.where(own, v, 1.0).astype(BF16)
        dk_sum[...] = jnp.zeros_like(dk_sum)
        dv_sum[...] = jnp.zeros_like(dv_sum)

    q = q_ref[0]
    do = do_ref[...]
    own0, sub = first_head(rows)
    qf = q.astype(F32) * scale
    first, second, third = three_parts(lse_ref[...])
    q_extra = jnp.where(
        sub == 0, first, jnp.where(sub == 1, second, jnp.where(sub == 2, third, jnp.where(sub == 3, 1.0, 0.0)))
    )
    dof = do.astype(F32)
    product = dof * o_ref[...].astype(F32)
    inner_a = jnp.sum(jnp.where(own0, product, 0.0), axis=1, keepdims=True)
    inner_b = jnp.sum(jnp.where(own0, 0.0, product), axis=1, keepdims=True)
    first, second, third = three_parts(jnp.where(own0, -inner_b, -inner_a))
    do_extra = jnp.where(sub == 0, first, jnp.where(sub == 1, second, jnp.where(sub == 2, third, 0.0)))
    q_t = q.T
    do_t = do.T
    grads = []
    for h in (0, 1):
        qa = (jnp.where(own0, qf, q_extra) if h == 0 else jnp.where(own0, q_extra, qf)).astype(BF16)
        da = (jnp.where(own0, dof, do_extra) if h == 0 else jnp.where(own0, do_extra, dof)).astype(BF16)
        own_rows = slice(h * HD, (h + 1) * HD)
        dq = None
        for c in range(0, count, step):
            part = slice(c, c + step)
            p = jnp.exp(dot_nt(qa, keys[h, part, :]))
            ds = (p * dot_nt(da, values[h, part, :])).astype(BF16)
            p = p.astype(BF16)
            t = dot(ds, keys[h, part, :])
            dq = t if dq is None else dq + t
            dk_sum[own_rows, part] += dot(q_t[own_rows, :], ds)
            dv_sum[own_rows, part] += dot(do_t[own_rows, :], p)
        grads.append(dq)
    dq_ref[...] = (jnp.where(own0, grads[0], grads[1]) * scale).astype(BF16)

    @pl.when(block == pl.num_programs(1) - 1)
    def _():
        for h in (0, 1):
            source = sc[2 * pair + h]
            own_rows = slice(h * HD, (h + 1) * HD)
            dk = dk_sum[own_rows, :] * scale
            dv = dv_sum[own_rows, :]
            for half in (0, 1):
                here = source == half
                dk_ref[half, own_rows, :] = jnp.where(here, dk, 0.0).astype(BF16)
                dv_ref[half, own_rows, :] = jnp.where(here, dv, 0.0).astype(BF16)


def attend_back(sc, qkv, context, lse, grad_context, width):
    count = qkv.shape[1]
    rows = min(1024, count)
    row_spec = pl.BlockSpec((rows, LANES), lambda p, i, sc: (i, p))
    q_spec = pl.BlockSpec((1, rows, LANES), lambda p, i, sc: (0, i, p))
    grad_spec = pl.BlockSpec((2, LANES, count), lambda p, i, sc: (0, p, 0))
    heads = width // HD
    return pl.pallas_call(
        functools.partial(attend_back_kernel, heads=heads, step=min(512, count)),
        grid_spec=pltpu.PrefetchScalarGridSpec(
            num_scalar_prefetch=1,
            grid=(width // LANES, count // rows),
            in_specs=[q_spec] + pair_specs(count, width) + [row_spec, row_spec, row_spec],
            out_specs=[row_spec, grad_spec, grad_spec],
            scratch_shapes=[
                pltpu.VMEM((2, count, LANES), BF16),
                pltpu.VMEM((2, count, LANES), BF16),
                pltpu.VMEM((LANES, count), F32),
                pltpu.VMEM((LANES, count), F32),
            ],
        ),
        out_shape=[
            jax.ShapeDtypeStruct((count, width), BF16),
            jax.ShapeDtypeStruct((2, width, count), BF16),
            jax.ShapeDtypeStruct((2, width, count), BF16),
        ],
        compiler_params=pltpu.CompilerParams(vmem_limit_bytes=VMEM_BYTES),
        cost_estimate=pl.CostEstimate(
            flops=10 * 4 * count * count * width,
            bytes_accessed=2 * 12 * count * width,
            transcendentals=heads * count * count,
        ),
        name="attend_back",
    )(sc, qkv, qkv, qkv, qkv, qkv, context, lse, grad_context)


def mean_of(value):
    return jnp.mean(value, axis=-1, keepdims=True)


def norm_of(value):
    center = value - mean_of(value)
    inverse = lax.rsqrt(mean_of(center * center) + EPS)
    return center * inverse, inverse


def norm_back(grad, normed, inverse, gain):
    dn = grad * gain
    return inverse * (dn - mean_of(dn) - normed * mean_of(dn * normed))


def sum_rows(value):
    return jnp.sum(value, axis=0, keepdims=True)


def middle_kernel(
    core,
    x_ref,
    own_ref,
    other_ref,
    cot_ref,
    wo_own,
    wo_other,
    w_in,
    w_back,
    vec,
    out_ref,
    resid_ref,
    gc_own,
    gc_other,
    low_ref,
    act_ref,
    gh_ref,
    gb_ref,
    attn_ref,
    sums,
    slope,
    *,
    width,
    ff,
):
    chunk = width
    in_bias = lambda c: vec[0:1, c : c + chunk]
    row = lambda r, s: vec[r : r + 1, s * width : (s + 1) * width]
    out_bias, back_bias, gain1, shift1 = (row(1, s) for s in range(4))
    gain2, shift2 = row(2, 0), row(2, 1)

    @pl.when(pl.program_id(0) == 0)
    def _():
        sums[...] = jnp.zeros_like(sums)

    attended = dot(own_ref[...], wo_own[...]) + dot(other_ref[...], wo_other[...]) + out_bias
    hat1, inverse1 = norm_of(x_ref[...].astype(F32) + attended)
    normed = hat1 * gain1 + shift1
    low = normed.astype(BF16)
    low_ref[...] = low
    branch = None
    for c in range(0, ff, chunk):
        hidden = dot(low, w_in[:, c : c + chunk]) + in_bias(c)
        cumulative = 0.5 * (1.0 + lax.erf(hidden * 0.7071067811865476))
        density = 0.3989422804014327 * jnp.exp(-0.5 * hidden * hidden)
        slope[:, c : c + chunk] = cumulative + hidden * density
        act = (hidden * cumulative).astype(BF16)
        act_ref[:, c : c + chunk] = act
        part = dot(act, w_back[c : c + chunk, :])
        branch = part if branch is None else branch + part
    hat2, inverse2 = norm_of(normed + (branch + back_bias))
    out_ref[...] = (hat2 * gain2 + shift2).astype(BF16)
    cot = cot_ref[...].astype(F32)
    grad2 = norm_back(cot, hat2, inverse2, gain2)
    gb = grad2.astype(BF16)
    gb_ref[...] = gb
    grad_normed = grad2
    for c in range(0, ff, chunk):
        gh = (dot_nt(gb, w_back[c : c + chunk, :]) * slope[:, c : c + chunk]).astype(BF16)
        gh_ref[:, c : c + chunk] = gh
        sums[0:1, c : c + chunk] += sum_rows(gh.astype(F32))
        grad_normed = grad_normed + dot_nt(gh, w_in[:, c : c + chunk])
    grad1 = norm_back(grad_normed, hat1, inverse1, gain1)
    resid_ref[...] = grad1
    attn = grad1.astype(BF16)
    attn_ref[...] = attn
    gc_own[...] = dot_nt(attn, wo_own[...]).astype(BF16)
    gc_other[...] = dot_nt(attn, wo_other[...]).astype(BF16)
    at = lambda r, s, v: sums.__setitem__(
        (slice(r, r + 1), slice(s * width, (s + 1) * width)),
        sums[r : r + 1, s * width : (s + 1) * width] + sum_rows(v),
    )
    at(1, 0, attn.astype(F32))
    at(1, 1, gb.astype(F32))
    at(1, 2, grad_normed * hat1)
    at(1, 3, grad_normed)
    at(2, 0, cot * hat2)
    at(2, 1, cot)


def middle(core, x, own, other, cot, w_out, w_in, w_back, vec):
    count, width = x.shape
    ff = w_in.shape[1]
    half = own.shape[1]
    rows = min(256, count)
    tile = lambda w: pl.BlockSpec((rows, w), lambda i, core: (i, 0))
    once = pl.Buffered(1)
    whole = lambda a: pl.BlockSpec(a.shape, lambda i, core: (0, 0), pipeline_mode=once)
    return pl.pallas_call(
        functools.partial(middle_kernel, width=width, ff=ff),
        grid_spec=pltpu.PrefetchScalarGridSpec(
            num_scalar_prefetch=1,
            grid=(count // rows,),
            in_specs=[
                tile(width),
                tile(half),
                tile(half),
                tile(width),
                pl.BlockSpec((half, width), lambda i, core: (core[0], 0), pipeline_mode=once),
                pl.BlockSpec((half, width), lambda i, core: (1 - core[0], 0), pipeline_mode=once),
                whole(w_in),
                whole(w_back),
                whole(vec),
            ],
            out_specs=[
                tile(width),
                tile(width),
                tile(half),
                tile(half),
                tile(width),
                tile(ff),
                tile(ff),
                tile(width),
                tile(width),
                pl.BlockSpec((8, ff), lambda i, core: (0, 0)),
            ],
            scratch_shapes=[pltpu.VMEM((rows, ff), F32)],
        ),
        out_shape=[
            jax.ShapeDtypeStruct((count, width), BF16),
            jax.ShapeDtypeStruct((count, width), F32),
            jax.ShapeDtypeStruct((count, half), BF16),
            jax.ShapeDtypeStruct((count, half), BF16),
            jax.ShapeDtypeStruct((count, width), BF16),
            jax.ShapeDtypeStruct((count, ff), BF16),
            jax.ShapeDtypeStruct((count, ff), BF16),
            jax.ShapeDtypeStruct((count, width), BF16),
            jax.ShapeDtypeStruct((count, width), BF16),
            jax.ShapeDtypeStruct((8, ff), F32),
        ],
        compiler_params=pltpu.CompilerParams(vmem_limit_bytes=VMEM_BYTES),
        cost_estimate=pl.CostEstimate(
            flops=2 * count * width * (4 * ff + 2 * width),
            bytes_accessed=2 * (4 * width * ff + 2 * count * ff + 8 * count * width),
            transcendentals=2 * count * ff,
        ),
        name="middle",
    )(core, x, own, other, cot, w_out, w_out, w_in, w_back, vec)


def dot_tn(a, b):
    return lax.dot_general(a, b, (((0,), (0,)), ((), ())), preferred_element_type=F32)


def per_device(
    tokens,
    lengths,
    pair_flip,
    w_qkv,
    q_bias,
    v_bias,
    w_out,
    out_bias,
    norm1_gain,
    norm1_shift,
    w_in,
    in_bias,
    w_back,
    back_bias,
    norm2_gain,
    norm2_shift,
    cotangent,
):
    both = ("head", "blk")
    cores = lax.axis_size("head")
    blocks = lax.axis_size("blk")
    core = lax.axis_index("head")
    block = lax.axis_index("blk")
    local, width = tokens.shape[1:]
    half = local * cores
    heads = HEADS // cores
    group = heads * HD
    ff = w_in.shape[1]
    parts = ff // width
    rows = w_qkv.shape[0]
    x = tokens[0]

    shard = jnp.concatenate(
        [w_in, w_back.reshape(parts, rows, width).transpose(1, 0, 2).reshape(rows, ff), w_out], axis=1
    )
    gathered = lax.all_gather(shard, both, axis=0, tiled=True)
    full_in = gathered[:, :ff]
    full_back = (
        gathered[:, ff : 2 * ff]
        .reshape(cores * blocks, rows, parts, width)
        .transpose(0, 2, 1, 3)
        .reshape(ff, width)
    )
    full_out = gathered[:, 2 * ff :]

    x_sib = swap(x, "head", 1)
    x_far = swap(x, "blk", 1)
    vectors = jnp.concatenate(
        [q_bias, v_bias, out_bias, back_bias, norm1_gain, norm1_shift, norm2_gain, norm2_shift, in_bias]
    )
    vectors = jnp.pad(vectors, (0, 3 * group - vectors.shape[0]))
    extra = jnp.pad(vectors[None], ((0, 7), (0, 0)))
    columns = w_qkv.reshape(rows, 3, cores, group)
    kept = lax.dynamic_index_in_dim(columns, core, 2, keepdims=False).reshape(rows, 3 * group)
    given = lax.dynamic_index_in_dim(columns, 1 - core, 2, keepdims=False).reshape(rows, 3 * group)
    mine = jnp.concatenate([kept, extra], axis=0)
    theirs = swap(jnp.concatenate([given, extra], axis=0), "head", 1)
    first, second = gather_blk(place(mine, theirs, core == 1, 0))
    x_far_sib = swap(x_far, "head", 1)
    weight = jnp.concatenate([first[:, :rows], second[:, :rows]], axis=0).reshape(width, 3 * group)
    small = jnp.concatenate([first[:, rows], second[:, rows]], axis=0)

    def vector(slot, size=rows):
        return small[:, slot * rows : slot * rows + size].reshape(-1).astype(F32)

    bias = jnp.concatenate(
        [
            lax.dynamic_slice_in_dim(vector(0), core * group, group),
            jnp.zeros((group,), F32),
            lax.dynamic_slice_in_dim(vector(1), core * group, group),
        ]
    )
    vec = jnp.concatenate(
        [
            vector(8, parts * rows)[None],
            jnp.pad(jnp.concatenate([vector(2), vector(3), vector(4), vector(5)]), (0, ff - 4 * width))[None],
            jnp.pad(jnp.concatenate([vector(6), vector(7)]), (0, ff - 2 * width))[None],
            jnp.zeros((5, ff), F32),
        ],
        axis=0,
    )

    xs = jnp.concatenate([x, x_sib, x_far, x_far_sib], axis=0)
    qkv = (dot(xs, weight) + bias).astype(BF16).reshape(2, half, 3 * group)

    sequence = block // 2
    own_half = block % 2
    length = lax.dynamic_index_in_dim(lengths, sequence, 0, keepdims=False)
    flags = lax.dynamic_index_in_dim(pair_flip, sequence, 0, keepdims=False)
    flags = lax.dynamic_slice_in_dim(flags, core * heads, heads)
    bounds = [jnp.clip(length - h * half, 0, half) for h in (own_half, 1 - own_half)]
    sc = jnp.concatenate([flags, jnp.stack(bounds + [jnp.int32(local), core])]).astype(jnp.int32)

    context, lse = attend(sc, qkv, group)
    other = swap(context[local:], "head", 1)
    out, grad_resid1, gc_own, gc_other, low, act, gh, gb, attn, sums = middle(
        core.reshape(1).astype(jnp.int32),
        x,
        context[:local],
        other,
        cotangent[0],
        full_out,
        full_in,
        full_back,
        vec,
    )
    grad_context = jnp.concatenate([gc_own, swap(gc_other, "head", 1)], axis=0)

    context_rows = place(context[:local], other, core == 1, 1).reshape(local, width)
    grad_in = dot_tn(low, gh).astype(BF16)
    grad_back = dot_tn(act, gb).astype(BF16)
    grad_out = dot_tn(context_rows, attn).astype(BF16)
    packed = jnp.concatenate(
        [
            grad_in,
            grad_back.reshape(cores * blocks, parts, rows, width).transpose(0, 2, 1, 3).reshape(width, ff),
            grad_out,
        ],
        axis=1,
    )
    reduced = lax.psum_scatter(packed, both, scatter_dimension=0, tiled=True)
    sum_win = reduced[:, :ff].astype(F32)
    sum_wback = (
        reduced[:, ff : 2 * ff].reshape(rows, parts, width).transpose(1, 0, 2).reshape(parts * rows, width)
    ).astype(F32)
    sum_wout = reduced[:, 2 * ff :].astype(F32)

    dq, dk, dv = attend_back(sc, qkv, context, lse, grad_context, group)
    wq, wk, wv = weight[:, :group], weight[:, group : 2 * group], weight[:, 2 * group :]

    def back_rows(which):
        return lax.dot_general(dk[which], wk, (((0,), (1,)), ((), ())), preferred_element_type=F32) + (
            lax.dot_general(dv[which], wv, (((0,), (1,)), ((), ())), preferred_element_type=F32)
        )

    dx_far = back_rows(1)
    dx_near = back_rows(0) + dot_nt(dq, wq)
    far_sib = swap(dx_far[local:].astype(BF16), "head", 1)
    far_in = swap((dx_far[:local] + far_sib.astype(F32)).astype(BF16), "blk", 1)
    near_sib = swap(dx_near[local:].astype(BF16), "head", 1)
    grad_tokens = grad_resid1 + dx_near[:local] + near_sib.astype(F32) + far_in.astype(F32)

    both_halves = xs.reshape(2, half, width)
    over = (((0, 1), (0, 2)), ((), ()))
    grad_w = jnp.concatenate(
        [
            dot_tn(both_halves[0], dq),
            lax.dot_general(both_halves, dk, over, preferred_element_type=F32),
            lax.dot_general(both_halves, dv, over, preferred_element_type=F32),
        ],
        axis=1,
    ).astype(BF16)
    at_group = lambda v: lax.dynamic_update_slice_in_dim(jnp.zeros((width,), F32), v, core * group, 0)
    grad_small = [
        at_group(jnp.sum(dq.astype(F32), axis=0)),
        at_group(jnp.sum(dv.astype(F32), axis=(0, 2))),
        sums[1, :width],
        sums[1, width : 2 * width],
        sums[1, 2 * width : 3 * width],
        sums[1, 3 * width : 4 * width],
        sums[2, :width],
        sums[2, width : 2 * width],
    ]
    grad_small = jnp.concatenate(
        [jnp.stack(grad_small, 0).reshape(8, cores, blocks, rows).transpose(1, 2, 0, 3).reshape(cores, blocks, -1)]
        + [sums[0].reshape(cores, blocks, parts * rows)],
        axis=2,
    )
    small_size = grad_small.shape[2]
    grad_small = jnp.pad(grad_small, ((0, 0), (0, 0), (0, 3 * group - small_size)))
    high = grad_small.astype(BF16)
    low_part = (grad_small - high.astype(F32)).astype(BF16)
    small_rows = jnp.pad(jnp.stack([high, low_part], axis=2), ((0, 0), (0, 0), (0, 6), (0, 0)))
    outgoing = jnp.concatenate([grad_w.reshape(cores, blocks, rows, 3 * group), small_rows], axis=2)
    keep = lax.dynamic_index_in_dim(outgoing, core, 0, keepdims=False)
    send = lax.dynamic_index_in_dim(outgoing, 1 - core, 0, keepdims=False)
    came = swap(send, "head", 1)
    exchanged = lax.all_to_all(jnp.stack([keep, came], axis=1), "blk", 0, 0, tiled=True).astype(F32)
    total = jnp.sum(exchanged, axis=0)
    own_w, other_w = (total[s, :rows].reshape(rows, 3, group) for s in (0, 1))
    sum_wqkv = place(own_w, other_w, core == 1, 2).reshape(rows, 3 * width)
    vectors = total[0, rows] + total[0, rows + 1] + total[1, rows] + total[1, rows + 1]

    def summed(slot, size=rows):
        return vectors[slot * rows : slot * rows + size]

    return (
        out[None],
        grad_tokens[None],
        sum_wqkv,
        summed(0),
        summed(1),
        sum_wout,
        summed(2),
        summed(4),
        summed(5),
        sum_win,
        summed(8, parts * rows),
        sum_wback,
        summed(3),
        summed(6),
        summed(7),
    )


def solution(mesh):
    split = P(("head", "blk"))
    matrix = P(("head", "blk"), None)
    rows = P("blk", "head", None)
    return jax.shard_map(
        per_device,
        mesh=mesh,
        in_specs=(
            rows,
            P(),
            P(),
            matrix,
            split,
            split,
            matrix,
            split,
            split,
            split,
            matrix,
            split,
            matrix,
            split,
            split,
            split,
            rows,
        ),
        out_specs=(
            rows,
            rows,
            matrix,
            split,
            split,
            matrix,
            split,
            split,
            split,
            matrix,
            split,
            matrix,
            split,
            split,
            split,
        ),
        check_vma=False,
    )
```

time: 1220 us -> 508 us (0.42)
  matrix products: 705 us -> 60.5 us
  Pallas kernels: 0 us -> 147 us
  blocking collectives: 110 us -> 0 us
  other arithmetic: 109 us -> 37.8 us
  local copies, waits for them, and re-layouts: 133 us -> 62.1 us
  waiting for transfers between devices: 133 us -> 154 us
  starting transfers between devices: 4.15 us -> 21.8 us
    dot_general x36 -> x12, matrix products: 705 us -> 60.5 us  [the longest x4 18.2 us: dot_tn(): lax.dot_general(a, b, (((0,), (0,)), ((), ())), preferred_element_type=F32)]
    pallas_call x0 -> x3, Pallas kernels: none -> 147 us  [the longest x1 68.4 us: attend_back(): pl.pallas_call(functools.partial(attend_back_kernel, heads=heads, step=mi...]
    ppermute x2 -> x16, waiting for transfers between devices: 58.6 us -> 154 us  [swap(): return lax.ppermute(value, axis, pairs)]
    unnamed x2 -> x0, blocking collectives: 82.1 us -> none
    unnamed x9 -> x2, waiting for transfers between devices: 59.9 us -> 0.03 us
    unnamed x3 -> x1, other arithmetic: 52.1 us -> 0.01 us
    unnamed x158 -> x43, local copies, waits for them, and re-layouts: 41 us -> 3.09 us
    reduce_sum x9 -> x3, other arithmetic: 37.1 us -> 6.44 us  [the longest x1 2.64 us: per_device(): jnp.sum(dv.astype(F32), axis=(0, 2))]
  transfers between devices with their start and end apart: 10 -> 19, of which waited for: 3 -> 8; matrix products, arithmetic and copies ran while one was open for 74% -> 23% of each run, Pallas kernels for 0% -> 22%
where the time goes in v1:
time: 508 us; the launch traced here: 499 us
  waiting for transfers between devices  154 us (30%)
  Pallas kernels  147 us (29%)
  local copies, waits for them, and re-layouts  62.1 us (12%)
  matrix products  60.5 us (12%)
  other arithmetic  37.8 us (7%)
  starting transfers between devices  21.8 us (4%)
  between operations  16.6 us (3%)
    ppermute x16, waiting for transfers between devices, swap(): return lax.ppermute(value, axis, pairs)  154 us
    pallas_call x1, Pallas kernels, attend_back(): pl.pallas_call(functools.partial(attend_back_kernel, heads=heads, step=mi...  68.4 us
    pallas_call x1, Pallas kernels, attend(): pl.pallas_call(functools.partial(attend_kernel, heads=heads, step=min(512...  39.3 us
    pallas_call x1, Pallas kernels, middle(): pl.pallas_call(functools.partial(middle_kernel, width=width, ff=ff), grid...  38.9 us
    dot_general x4, matrix products, dot_tn(): lax.dot_general(a, b, (((0,), (0,)), ((), ())), preferred_element_type=F32)  18.2 us
    reshape x2, local copies, waits for them, and re-layouts, per_device(): full_back = gathered[:, ff:2 * ff].reshape(cores * blocks, rows, parts, w...  15.1 us
    ppermute x16, starting transfers between devices, swap(): return lax.ppermute(value, axis, pairs)  14.5 us
    dot_general x1, matrix products, dot(): return jnp.dot(a, b, preferred_element_type=F32)  14.4 us
  transfers between devices with their start and end apart: 19, of which 8 were waited for; matrix products, arithmetic and copies ran while one was open for 23% of the time, Pallas kernels for 22%

profile of v1, /device:TPU:0, one launch (start us, length us, event | category | flops | bytes accessed | tf_op | source)
XLA Modules:
  0.0 499.4 jit_solution(259816807060860875)
XLA Ops:
  11.8 6.1 %concatenate.62 = bf16[288]{0:T(512)(128)(2,1)S(1)} concatenate(bf16[24]{0:T(256)(128)(2,1)} %param.21, bf16[24]{0:T(256)(128)(2,1)} %param.22, bf16[24]{0:T(256)(128)(2,1)} %param.24, bf16[24]{0:T(256)(128)(2,1)} %param.30, bf16[24]{0:T(256)(128)(2,1)} %param.25, bf16[24]{0:T(256)(128)(2,1)} %param.26, bf16[24]{0:T(256)(128)(2,1)} %param.31, bf16[24]{0:T(256)(128)(2,1)} %param.32, ...), dimensions={0} | concatenate | bytes 1152 | tf_op jit(solution)/shard_map/concatenate | solution.py:533
  23.4 11.8 %collective-permute-done.4 = bf16[2,32,1152]{2,1,0:T(8,128)(2,1)S(1)} collective-permute-done((bf16[2,32,1152]{2,1,0:T(8,128)(2,1)S(1)}, bf16[2,32,1152]{2,1,0:T(8,128)(2,1)S(1)}, u32[]{:S(2)}, u32[]{:S(2)}) %collective-permute-start.4) | collective-permute-done | bytes 147488 | tf_op jit(solution)/shard_map/ppermute | solution.py:32
  36.3 7.8 %collective-permute-done.5 = bf16[2,2,32,1152]{3,2,0,1:T(8,128)(2,1)S(1)} collective-permute-done((bf16[2,2,32,1152]{3,2,0,1:T(8,128)(2,1)S(1)}, bf16[2,2,32,1152]{3,2,0,1:T(8,128)(2,1)S(1)}, u32[]{:S(2)}, u32[]{:S(2)}) %collective-permute-start.5) | collective-permute-done | bytes 294944 | tf_op jit(solution)/shard_map/ppermute | solution.py:32
  50.8 6.1 %collective-permute-done.6 = bf16[2,2,32,1152]{3,2,0,1:T(8,128)(2,1)S(1)} collective-permute-done((bf16[2,2,32,1152]{3,2,0,1:T(8,128)(2,1)S(1)}, bf16[2,2,32,1152]{3,2,0,1:T(8,128)(2,1)S(1)}, u32[]{:S(2)}, u32[]{:S(2)}) %collective-permute-start.6) | collective-permute-done | bytes 294944 | tf_op jit(solution)/shard_map/ppermute | solution.py:32
  58.3 56.1 %collective-permute-done.8 = bf16[2,2,32,1152]{3,2,0,1:T(8,128)(2,1)S(1)} collective-permute-done((bf16[2,2,32,1152]{3,2,0,1:T(8,128)(2,1)S(1)}, bf16[2,2,32,1152]{3,2,0,1:T(8,128)(2,1)S(1)}, u32[]{:S(2)}, u32[]{:S(2)}) %collective-permute-start.8) | collective-permute-done | bytes 294944 | tf_op jit(solution)/shard_map/ppermute | solution.py:32
  115.1 12.7 %collective-permute-done.7 = bf16[2,2,2,32,1152]{4,3,0,1,2:T(8,128)(2,1)S(1)} collective-permute-done((bf16[2,2,2,32,1152]{4,3,0,1,2:T(8,128)(2,1)S(1)}, bf16[2,2,2,32,1152]{4,3,0,1,2:T(8,128)(2,1)S(1)}, u32[]{:S(2)}, u32[]{:S(2)}) %collective-permute-start.7) | collective-permute-done | bytes 589856 | tf_op jit(solution)/shard_map/ppermute | solution.py:32
  132.5 14.4 %add_convert_fusion = bf16[4096,1152]{1,0:T(8,128)(2,1)} fusion(bf16[768,1152]{1,0:T(8,128)(2,1)S(1)} %bitcast.151, f32[1152]{0:T(1024)S(1)} %pad_maximum_fusion.17, bf16[1024,768]{1,0:T(8,128)(2,1)} %collective-permute-done.2, bf16[1024,768]{1,0:T(8,128)(2,1)} %collective-permute-done.1, bf16[1024,768]{1,0:T(8,128)(2,1)} %collective-permute-done, ...), kind=kOutput, calls=%fused_computation | convolution fusion | flops 7282360320 | bytes 17502720 | tf_op jit(solution)/shard_map/dot_general | solution.py:23
  147.0 39.3 %attend.1 = (bf16[2048,384]{1,0:T(8,128)(2,1)}, f32[2048,384]{1,0:T(8,128)}) custom-call(s32[10]{0:T(128)} %concatenate.60.sc, bf16[2,2048,1152]{2,1,0:T(8,128)(2,1)} %bitcast.189, bf16[2,2048,1152]{2,1,0:T(8,128)(2,1)} %bitcast.190, bf16[2,2048,1152]{2,1,0:T(8,128)(2,1)} %bitcast.191, bf16[2,2048,1152]{2,1,0:T(8,128)(2,1)} %bitcast.192, ...), custom_call_target="tpu_custom_call" | custom-call | flops 25769803776 | bytes 9437184 | tf_op jit(solution)/shard_map/attend/pallas_call | solution.py:169
  189.2 5.8 %pad_maximum_fusion.1 = bf16[4096,768]{1,0:T(8,128)(2,1)} fusion(bf16[1024,768]{1,0:T(8,128)(2,1)} %collective-permute-done.2, bf16[1024,768]{1,0:T(8,128)(2,1)} %collective-permute-done.1, bf16[1024,768]{1,0:T(8,128)(2,1)} %collective-permute-done, bf16[1024,768]{1,0:T(8,128)(2,1)S(1)} %bitcast.171), kind=kLoop, calls=%fused_computation.2 | loop fusion | flops 25165824 | bytes 12582912 | tf_op jit(solution)/shard_map/concatenate | solution.py:568
  195.0 8.9 %copy.116 = bf16[2,2048,768]{1,2,0:T(8,128)(2,1)} copy(bf16[2,2048,768]{2,1,0:T(8,128)(2,1)} %bitcast.148) | data formatting | bytes 12582912 | tf_op jit(solution)/shard_map/reshape | solution.py:628
  207.3 8.3 %fusion.61 = (bf16[768,3072]{1,0:T(8,128)(2,1)}, bf16[768,3072]{1,0:T(8,128)(2,1)}) fusion(bf16[768,6912]{1,0:T(8,128)(2,1)} %all-gather.2.cloned.1.call-done), kind=kLoop, calls=%fused_computation.161 | loop fusion | bytes 18874368 | tf_op jit(solution)/shard_map/slice | solution.py:524
  215.6 9.7 %reshape.208 = bf16[32,24,4,768]{3,2,1,0:T(4,128)(2,1)} reshape(bf16[768,3072]{1,0:T(8,128)(2,1)} %get-tuple-element.47) | data formatting | bytes 9437184 | tf_op jit(solution)/shard_map/reshape | solution.py:525
  225.3 5.4 %copy.115 = bf16[32,24,4,768]{3,1,2,0:T(8,128)(2,1)} copy(bf16[32,24,4,768]{3,2,1,0:T(4,128)(2,1)} %reshape.208) | data formatting | bytes 9437184 | tf_op jit(solution)/shard_map/reshape | solution.py:525
  233.1 38.9 %middle.1 = (bf16[1024,768]{1,0:T(8,128)(2,1)}, f32[1024,768]{1,0:T(8,128)}, bf16[1024,384]{1,0:T(8,128)(2,1)}, bf16[1024,384]{1,0:T(8,128)(2,1)}, bf16[1024,768...) custom-call(s32[1]{0:T(128)} %bitcast.core, ...), custom_call_target="tpu_custom_call" | custom-call | flops 21743271936 | bytes 44040192 | tf_op jit(solution)/shard_map/middle/pallas_call | solution.py:429
  272.0 8.1 %convolution_convert_fusion = bf16[3072,768]{1,0:T(8,128)(2,1)S(1)} fusion(bf16[1024,3072]{1,0:T(8,128)(2,1)} %get-tuple-element.42, bf16[1024,768]{1,0:T(8,128)(2,1)} %get-tuple-element.43), kind=kOutput, calls=%fused_computation.9 | convolution fusion | flops 4834197504 | bytes 12582912 | tf_op jit(solution)/shard_map/dot_general | solution.py:482
  285.2 5.4 %convolution_convert_fusion.1 = bf16[768,3072]{1,0:T(8,128)(2,1)S(1)} fusion(bf16[1024,768]{1,0:T(8,128)(2,1)S(1)} %copy-done.16, bf16[1024,3072]{1,0:T(8,128)(2,1)S(1)} %bitcast.201), kind=kOutput, calls=%fused_computation.10 | convolution fusion | flops 4834197504 | bytes 12582912 | tf_op jit(solution)/shard_map/dot_general | solution.py:482
  292.1 8.0 %pad_maximum_fusion = bf16[768,6912]{1,0:T(8,128)(2,1)} fusion(bf16[768,768]{1,0:T(8,128)(2,1)S(1)} %convolution_convert_fusion.2, bf16[768,3072]{1,0:T(8,128)(2,1)S(1)} %bitcast.150, bf16[768,3072]{1,0:T(8,128)(2,1)S(1)} %convolution_convert_fusion.1), kind=kLoop, calls=%fused_computation.1 | loop fusion | flops 31850496 | bytes 21233664 | tf_op jit(solution)/shard_map/concatenate | solution.py:598
  303.3 68.4 %attend_back.1 = (bf16[2048,384]{1,0:T(8,128)(2,1)}, bf16[2,384,2048]{2,1,0:T(8,128)(2,1)}, bf16[2,384,2048]{2,1,0:T(8,128)(2,1)}) custom-call(s32[10]{0:T(128)} %concatenate.60.sc, bf16[2,2048,1152]{2,1,0:T(8,128)(2,1)} %bitcast.194, bf16[2,2048,1152]{2,1,0:T(8,128)(2,1)} %bitcast.195, bf16[2,2048,1152]{2,1,0:T(8,128)(2,1)} %bitcast.196, ...), custom_call_target="tpu_custom_call" | custom-call | flops 64424509440 | bytes 18874368 | tf_op jit(solution)/shard_map/attend_back/pallas_call | solution.py:292
  377.0 6.0 %fusion = bf16[2,16,24,384,1]{3,2,0,1,4:T(8,128)(2,1)S(1)} fusion(bf16[2,16,24,2,2048]{4,2,1,0,3:T(8,128)(2,1)} %bitcast.157, bf16[2,384,2048]{2,1,0:T(8,128)(2,1)S(1)} %copy-done.2), kind=kOutput, calls=%fused_computation.5 | convolution fusion | flops 2415919104 | bytes 10027008 | tf_op jit(solution)/shard_map/dot_general | solution.py:634
  383.1 5.8 %fusion.2 = bf16[2,16,24,384,1]{3,2,0,1,4:T(8,128)(2,1)S(1)} fusion(bf16[2,16,24,2,2048]{4,2,1,0,3:T(8,128)(2,1)} %bitcast.158, bf16[2,384,2048]{2,1,0:T(8,128)(2,1)S(1)} %copy-done.5), kind=kOutput, calls=%fused_computation.7 | convolution fusion | flops 2415919104 | bytes 10027008 | tf_op jit(solution)/shard_map/dot_general | solution.py:633
  393.5 5.6 %fusion.15 = f32[2048,768]{1,0:T(8,128)} fusion(bf16[2,384,2048]{2,1,0:T(8,128)(2,1)S(1)} %copy-done.5, bf16[768,1152]{1,0:T(8,128)(2,1)} %bitcast.152), kind=kOutput, calls=%fused_computation.34 | convolution fusion | flops 1207959552 | bytes 8454144 | tf_op jit(solution)/shard_map/dot_general | solution.py:617
  400.8 7.3 %all-to-all-start = ((bf16[16,2,32,1152]{3,2,1,0:T(8,128)(2,1)}), bf16[16,2,32,1152]{3,2,1,0:T(8,128)(2,1)}, u32[]{:S(2)}, u32[]{:S(2)}) async-start(bf16[16,2,32,1152]{3,2,1,0:T(8,128)(2,1)} %pad_maximum_fusion.3), calls=%async_computation | async-start | bytes 4718592 | tf_op jit(solution)/shard_map/all_to_all | solution.py:663
  408.0 4.9 convolution_add_fusion
  424.9 56.4 %collective-permute-done.14 = bf16[1024,768]{1,0:T(8,128)(2,1)S(1)} collective-permute-done((bf16[1024,768]{1,0:T(8,128)(2,1)S(1)}, bf16[1024,768]{1,0:T(8,128)(2,1)S(1)}, u32[]{:S(2)}, u32[]{:S(2)}) %collective-permute-start.14) | collective-permute-done | bytes 1572896 | tf_op jit(solution)/shard_map/ppermute | solution.py:32
  (181 shorter events, 75.7 us)
Async XLA Ops:
  7.2 42.2 %copy-start = (s32[8,12]{1,0:T(8,128)S(1)}, s32[8,12]{1,0:T(8,128)}, u32[]{:S(2)}) copy-start(s32[8,12]{1,0:T(8,128)} %param.19) | copy-start | bytes 1156
  7.2 200.1 %all-gather.2.cloned.1.call-start = ((), (), s32[]{:S(2)}) async-start(), calls=%async_computation.2 | async-start | bytes 10948608 | tf_op jit(solution)/shard_map/all_gather | solution.py:521
  8.2 37.8 %copy-start.10 = (bf16[1,1024,768]{2,1,0:T(8,128)(2,1)S(1)}, bf16[1,1024,768]{2,1,0:T(8,128)(2,1)}, u32[]{:S(2)}) copy-start(bf16[1,1024,768]{2,1,0:T(8,128)(2,1)} %param.17) | copy-start | bytes 4718596
  8.3 39.2 %copy-start.14 = (s32[8]{0:T(128)S(1)}, s32[8]{0:T(128)}, u32[]{:S(2)}) copy-start(s32[8]{0:T(128)} %param.18) | copy-start | bytes 100
  10.1 477.9 %reduce-scatter.2.cloned.1.call-start = ((), (), s32[]{:S(2)}) async-start(), calls=%async_computation.3 | async-start | bytes 10948608 | tf_op jit(solution)/shard_map/reduce_scatter | solution.py:606
  18.0 1.4 collective-permute-start.3
  19.4 15.8 %collective-permute-start.4 = (bf16[2,32,1152]{2,1,0:T(8,128)(2,1)S(1)}, bf16[2,32,1152]{2,1,0:T(8,128)(2,1)S(1)}, u32[]{:S(2)}, u32[]{:S(2)}) collective-permute-start(bf16[2,32,1152]{2,1,0:T(8,128)(2,1)S(1)} %pad_maximum_fusion.15), channel_id=1, source_target_pairs={{0,8},{1,9},{2,10},{3,11},{4,12},{5,13},{6,14},{7,15},{8,0},{9,1},... | collective-permute-start | bytes 442376 | tf_op jit(solution)/shard_map/ppermute | solution.py:32
  35.3 8.8 %collective-permute-start.5 = (bf16[2,2,32,1152]{3,2,0,1:T(8,128)(2,1)S(1)}, bf16[2,2,32,1152]{3,2,0,1:T(8,128)(2,1)S(1)}, u32[]{:S(2)}, u32[]{:S(2)}) collective-permute-start(bf16[2,2,32,1152]{3,2,0,1:T(8,128)(2,1)S(1)} %pad_maximum_fusion.13), channel_id=1, source_target_pairs={{0,4},{1,5},{2,6},{3,7},{4,0},{5,1},{6,2},{7,3},{8,12},{9,13},{10,... | collective-permute-start | bytes 884744 | tf_op jit(solution)/shard_map/ppermute | solution.py:32
  44.2 12.6 %collective-permute-start.6 = (bf16[2,2,32,1152]{3,2,0,1:T(8,128)(2,1)S(1)}, bf16[2,2,32,1152]{3,2,0,1:T(8,128)(2,1)S(1)}, u32[]{:S(2)}, u32[]{:S(2)}) collective-permute-start(bf16[2,2,32,1152]{3,2,0,1:T(8,128)(2,1)S(1)} %get-tuple-element.60), channel_id=1, source_target_pairs={{0,2},{1,3},{2,0},{3,1},{4,6},{5,7},{6,4},{7,5},{8,10},{9,11},{10,... | collective-permute-start | bytes 884744 | tf_op jit(solution)/shard_map/ppermute | solution.py:32
  46.1 82.5 %collective-permute-start.1 = (bf16[1024,768]{1,0:T(8,128)(2,1)S(1)}, bf16[1024,768]{1,0:T(8,128)(2,1)}, u32[]{:S(2)}, u32[]{:S(2)}) collective-permute-start(bf16[1024,768]{1,0:T(8,128)(2,1)S(1)} %bitcast.168), channel_id=1, source_target_pairs={{0,1},{1,0},{2,3},{3,2},{4,5},{5,4},{6,7},{7,6},{8,9},{9,8},{10,11... | collective-permute-start | bytes 4718600 | tf_op jit(solution)/shard_map/ppermute | solution.py:32
  47.4 83.0 %collective-permute-start = (bf16[1024,768]{1,0:T(8,128)(2,1)S(1)}, bf16[1024,768]{1,0:T(8,128)(2,1)}, u32[]{:S(2)}, u32[]{:S(2)}) collective-permute-start(bf16[1024,768]{1,0:T(8,128)(2,1)S(1)} %bitcast.169), channel_id=1, source_target_pairs={{0,16},{16,0},{1,17},{17,1},{2,18},{18,2},{3,19},{19,3},{4,20},{20... | collective-permute-start | bytes 4718600 | tf_op jit(solution)/shard_map/ppermute | solution.py:32
  50.1 64.3 %collective-permute-start.8 = (bf16[2,2,32,1152]{3,2,0,1:T(8,128)(2,1)S(1)}, bf16[2,2,32,1152]{3,2,0,1:T(8,128)(2,1)S(1)}, u32[]{:S(2)}, u32[]{:S(2)}) collective-permute-start(bf16[2,2,32,1152]{3,2,0,1:T(8,128)(2,1)S(1)} %get-tuple-element.61), channel_id=1, source_target_pairs={{0,1},{1,0},{2,3},{3,2},{4,5},{5,4},{6,7},{7,6},{8,9},{9,8},{10,11... | collective-permute-start | bytes 884744 | tf_op jit(solution)/shard_map/ppermute | solution.py:32
  57.0 70.9 %collective-permute-start.7 = (bf16[2,2,2,32,1152]{4,3,0,1,2:T(8,128)(2,1)S(1)}, bf16[2,2,2,32,1152]{4,3,0,1,2:T(8,128)(2,1)S(1)}, u32[]{:S(2)}, u32[]{:S(2)}) collective-permute-start(bf16[2,2,2,32,1152]{4,3,0,1,2:T(8,128)(2,1)S(1)} %pad_maximum_fusion.9), channel_id=1, source_target_pairs={{0,1},{1,0},{2,3},{3,2},{4,5},{5,4},{6,7},{7,6},{8,9},{9,8},{10,11... | collective-permute-start | bytes 1769480 | tf_op jit(solution)/shard_map/ppermute | solution.py:32
  114.5 13.9 %collective-permute-start.9 = (bf16[2,2,2,32,1152]{4,3,0,1,2:T(8,128)(2,1)S(1)}, bf16[2,2,2,32,1152]{4,3,0,1,2:T(8,128)(2,1)S(1)}, u32[]{:S(2)}, u32[]{:S(2)}) collective-permute-start(bf16[2,2,2,32,1152]{4,3,0,1,2:T(8,128)(2,1)S(1)} %pad_maximum_fusion.10), channel_id=1, source_target_pairs={{0,2},{1,3},{2,0},{3,1},{4,6},{5,7},{6,4},{7,5},{8,10},{9,11},{10,... | collective-permute-start | bytes 1769480 | tf_op jit(solution)/shard_map/ppermute | solution.py:32
  128.5 4.0 collective-permute-start.2
  130.4 16.6 %copy-start.3 = (bf16[32,24,1152]{2,1,0:T(8,128)(2,1)}, bf16[32,24,1152]{2,1,0:T(8,128)(2,1)S(1)}, u32[]{:S(2)}) copy-start(bf16[32,24,1152]{2,1,0:T(8,128)(2,1)S(1)} %pad_maximum_fusion.4) | copy-start | bytes 5308420
  188.3 15.5 %collective-permute-start.10 = (bf16[1024,384]{1,0:T(8,128)(2,1)}, bf16[1024,384]{1,0:T(8,128)(2,1)}, u32[]{:S(2)}, u32[]{:S(2)}) collective-permute-start(bf16[1024,384]{1,0:T(8,128)(2,1)} %slice.210), channel_id=1, source_target_pairs={{0,16},{16,0},{1,17},{17,1},{2,18},{18,2},{3,19},{19,3},{4,20},{20... | collective-permute-start | bytes 2359304 | tf_op jit(solution)/shard_map/ppermute | solution.py:32
  283.6 18.4 %collective-permute-start.11 = (bf16[1024,384]{1,0:T(8,128)(2,1)}, bf16[1024,384]{1,0:T(8,128)(2,1)S(1)}, u32[]{:S(2)}, u32[]{:S(2)}) collective-permute-start(bf16[1024,384]{1,0:T(8,128)(2,1)} %get-tuple-element.35), channel_id=1, source_target_pairs={{0,16},{16,0},{1,17},{17,1},{2,18},{18,2},{3,19},{19,3},{4,20},{20... | collective-permute-start | bytes 2359304 | tf_op jit(solution)/shard_map/ppermute | solution.py:32
  393.1 6.0 %collective-permute-start.15 = (bf16[16,32,1152]{2,1,0:T(8,128)(2,1)S(1)}, bf16[16,32,1152]{2,1,0:T(8,128)(2,1)S(1)}, u32[]{:S(2)}, u32[]{:S(2)}) collective-permute-start(bf16[16,32,1152]{2,1,0:T(8,128)(2,1)S(1)} %get-tuple-element.52), channel_id=1, source_target_pairs={{0,16},{16,0},{1,17},{17,1},{2,18},{18,2},{3,19},{19,3},{4,20},{20... | collective-permute-start | bytes 3538952 | tf_op jit(solution)/shard_map/ppermute | solution.py:32
  400.8 82.8 %all-to-all-start = ((bf16[16,2,32,1152]{3,2,1,0:T(8,128)(2,1)}), bf16[16,2,32,1152]{3,2,1,0:T(8,128)(2,1)}, u32[]{:S(2)}, u32[]{:S(2)}) async-start(bf16[16,2,32,1152]{3,2,1,0:T(8,128)(2,1)} %pad_maximum_fusion.3), calls=%async_computation | async-start | bytes 4718592 | tf_op jit(solution)/shard_map/all_to_all | solution.py:663
  414.2 6.6 %collective-permute-start.13 = (bf16[1024,768]{1,0:T(8,128)(2,1)}, bf16[1024,768]{1,0:T(8,128)(2,1)}, u32[]{:S(2)}, u32[]{:S(2)}) collective-permute-start(bf16[1024,768]{1,0:T(8,128)(2,1)} %slice.449), channel_id=1, source_target_pairs={{0,16},{16,0},{1,17},{17,1},{2,18},{18,2},{3,19},{19,3},{4,20},{20... | collective-permute-start | bytes 4718600 | tf_op jit(solution)/shard_map/ppermute | solution.py:32
  420.7 60.5 %copy-start.9 = (f32[1024,768]{1,0:T(8,128)S(1)}, f32[1024,768]{1,0:T(8,128)}, u32[]{:S(2)}) copy-start(f32[1024,768]{1,0:T(8,128)} %get-tuple-element.32) | copy-start | bytes 9437188
  420.7 4.2 collective-permute-start.12
  422.8 58.4 %collective-permute-start.14 = (bf16[1024,768]{1,0:T(8,128)(2,1)S(1)}, bf16[1024,768]{1,0:T(8,128)(2,1)S(1)}, u32[]{:S(2)}, u32[]{:S(2)}) collective-permute-start(bf16[1024,768]{1,0:T(8,128)(2,1)S(1)} %fusion.4), channel_id=1, source_target_pairs={{0,1},{1,0},{2,3},{3,2},{4,5},{5,4},{6,7},{7,6},{8,9},{9,8},{10,11... | collective-permute-start | bytes 4718600 | tf_op jit(solution)/shard_map/ppermute | solution.py:32
  (14 other events, 66.3 us)
Sparse Core Ops, SparseCore 0:
  10.9 122.9 all-gather.1
  300.2 174.3 reduce-scatter.1

commit v2 on v1

--- a/solution.py
+++ b/solution.py
@@ -36,7 +36,7 @@
     return jnp.stack([jnp.where(upper, theirs, mine), jnp.where(upper, mine, theirs)], axis=axis)
 
 
-def gather_blk(pair):
+def gather_blk(pair, also):
     count = lax.axis_size("blk")
     index = lax.axis_index("blk")
     bits = [1 << b for b in range(count.bit_length() - 1)][::-1]
@@ -45,6 +45,8 @@
     for bit in bits[:-2]:
         held = place(held, swap(held, "blk", bit), (index & bit) != 0, depth)
         depth += 1
+    if GATE >= 4:
+        held, also = lax.optimization_barrier((held, also))
     first, second = held[0], held[1]
     depth -= 1
     high, low = bits[-2], bits[-1]
@@ -56,7 +58,7 @@
     second_in = swap(second, "blk", high)
     first = place(first, first_in, (index & low) != 0, depth + 1)
     second = place(second, second_in, (index & high) != 0, depth)
-    return tuple(a.reshape((count,) + pair.shape[1:]) for a in (first, second))
+    return tuple(a.reshape((count,) + pair.shape[1:]) for a in (first, second)) + (also,)
 
 
 def first_head(rows):
@@ -204,9 +206,10 @@
     lse_ref,
     do_ref,
     dq_ref,
-    dk_ref,
-    dv_ref,
+    dkv_ref,
+    sum_ref,
     keys,
+    keys_t,
     values,
     dk_sum,
     dv_sum,
@@ -230,8 +233,10 @@
             for r in range(0, count, piece):
                 k = k_ref[0, r : r + piece, :]
                 keys[h, r : r + piece, :] = key_rows(own, sub, k, r, sc, source, heads)
+                keys_t[h, :, r : r + piece] = k.T[h * HD : (h + 1) * HD, :]
                 v = v_ref[0, r : r + piece, :].astype(F32)
                 values[h, r : r + piece, :] = jnp.where(own, v, 1.0).astype(BF16)
+        sum_ref[...] = jnp.zeros_like(sum_ref)
         dk_sum[...] = jnp.zeros_like(dk_sum)
         dv_sum[...] = jnp.zeros_like(dv_sum)
 
@@ -262,12 +267,15 @@
             p = jnp.exp(dot_nt(qa, keys[h, part, :]))
             ds = (p * dot_nt(da, values[h, part, :])).astype(BF16)
             p = p.astype(BF16)
-            t = dot(ds, keys[h, part, :])
+            t = dot_nt(keys_t[h, :, part], ds)
             dq = t if dq is None else dq + t
             dk_sum[own_rows, part] += dot(q_t[own_rows, :], ds)
             dv_sum[own_rows, part] += dot(do_t[own_rows, :], p)
         grads.append(dq)
-    dq_ref[...] = (jnp.where(own0, grads[0], grads[1]) * scale).astype(BF16)
+    dq = (jnp.concatenate(grads, axis=0) * scale).astype(BF16)
+    dq_ref[...] = dq
+    for c in range(0, rows, LANES):
+        sum_ref[...] += dq[:, c : c + LANES].astype(F32)
 
     @pl.when(block == pl.num_programs(1) - 1)
     def _():
@@ -278,8 +286,8 @@
             dv = dv_sum[own_rows, :]
             for half in (0, 1):
                 here = source == half
-                dk_ref[half, own_rows, :] = jnp.where(here, dk, 0.0).astype(BF16)
-                dv_ref[half, own_rows, :] = jnp.where(here, dv, 0.0).astype(BF16)
+                dkv_ref[half, 0, own_rows, :] = jnp.where(here, dk, 0.0).astype(BF16)
+                dkv_ref[half, 1, own_rows, :] = jnp.where(here, dv, 0.0).astype(BF16)
 
 
 def attend_back(sc, qkv, context, lse, grad_context, width):
@@ -287,7 +295,8 @@
     rows = min(1024, count)
     row_spec = pl.BlockSpec((rows, LANES), lambda p, i, sc: (i, p))
     q_spec = pl.BlockSpec((1, rows, LANES), lambda p, i, sc: (0, i, p))
-    grad_spec = pl.BlockSpec((2, LANES, count), lambda p, i, sc: (0, p, 0))
+    dq_spec = pl.BlockSpec((LANES, rows), lambda p, i, sc: (p, i))
+    dkv_spec = pl.BlockSpec((2, 2, LANES, count), lambda p, i, sc: (0, 0, p, 0))
     heads = width // HD
     return pl.pallas_call(
         functools.partial(attend_back_kernel, heads=heads, step=min(512, count)),
@@ -295,18 +304,19 @@
             num_scalar_prefetch=1,
             grid=(width // LANES, count // rows),
             in_specs=[q_spec] + pair_specs(count, width) + [row_spec, row_spec, row_spec],
-            out_specs=[row_spec, grad_spec, grad_spec],
+            out_specs=[dq_spec, dkv_spec, pl.BlockSpec((LANES, LANES), lambda p, i, sc: (p, 0))],
             scratch_shapes=[
                 pltpu.VMEM((2, count, LANES), BF16),
+                pltpu.VMEM((2, HD, count), BF16),
                 pltpu.VMEM((2, count, LANES), BF16),
                 pltpu.VMEM((LANES, count), F32),
                 pltpu.VMEM((LANES, count), F32),
             ],
         ),
         out_shape=[
-            jax.ShapeDtypeStruct((count, width), BF16),
-            jax.ShapeDtypeStruct((2, width, count), BF16),
-            jax.ShapeDtypeStruct((2, width, count), BF16),
+            jax.ShapeDtypeStruct((width, count), BF16),
+            jax.ShapeDtypeStruct((2, 2, width, count), BF16),
+            jax.ShapeDtypeStruct((width, LANES), F32),
         ],
         compiler_params=pltpu.CompilerParams(vmem_limit_bytes=VMEM_BYTES),
         cost_estimate=pl.CostEstimate(
@@ -343,27 +353,34 @@
     own_ref,
     other_ref,
     cot_ref,
-    wo_own,
-    wo_other,
-    w_in,
-    w_back,
-    vec,
-    out_ref,
-    resid_ref,
-    gc_own,
-    gc_other,
-    low_ref,
-    act_ref,
-    gh_ref,
-    gb_ref,
-    attn_ref,
-    sums,
-    slope,
-    *,
+    wo_own_ref,
+    wo_other_ref,
+    *refs,
     width,
     ff,
 ):
     chunk = width
+    parts = ff // width
+    w_in_refs = refs[:parts]
+    (
+        w_back_ref,
+        vec,
+        out_ref,
+        resid_ref,
+        gc_own,
+        gc_other,
+        low_ref,
+        act_ref,
+        gh_ref,
+        gb_ref,
+        attn_ref,
+        sums,
+        slope,
+        wo_own,
+        wo_other,
+        w_in,
+        w_back,
+    ) = refs[parts:]
     in_bias = lambda c: vec[0:1, c : c + chunk]
     row = lambda r, s: vec[r : r + 1, s * width : (s + 1) * width]
     out_bias, back_bias, gain1, shift1 = (row(1, s) for s in range(4))
@@ -372,6 +389,14 @@
     @pl.when(pl.program_id(0) == 0)
     def _():
         sums[...] = jnp.zeros_like(sums)
+        wo_own[...] = wo_own_ref[...].reshape(wo_own.shape)
+        wo_other[...] = wo_other_ref[...].reshape(wo_other.shape)
+        for j in range(parts):
+            w_in[j] = w_in_refs[j][...].reshape(w_in.shape[1:])
+        devices, rows = w_back_ref.shape[:2]
+        some = devices // parts
+        for j in range(parts):
+            w_back[j] = w_back_ref[j * some : (j + 1) * some].reshape(some * rows, width)
 
     attended = dot(own_ref[...], wo_own[...]) + dot(other_ref[...], wo_other[...]) + out_bias
     hat1, inverse1 = norm_of(x_ref[...].astype(F32) + attended)
@@ -380,13 +405,13 @@
     low_ref[...] = low
     branch = None
     for c in range(0, ff, chunk):
-        hidden = dot(low, w_in[:, c : c + chunk]) + in_bias(c)
+        hidden = dot(low, w_in[c // chunk]) + in_bias(c)
         cumulative = 0.5 * (1.0 + lax.erf(hidden * 0.7071067811865476))
         density = 0.3989422804014327 * jnp.exp(-0.5 * hidden * hidden)
         slope[:, c : c + chunk] = cumulative + hidden * density
         act = (hidden * cumulative).astype(BF16)
         act_ref[:, c : c + chunk] = act
-        part = dot(act, w_back[c : c + chunk, :])
+        part = dot(act, w_back[c // chunk])
         branch = part if branch is None else branch + part
     hat2, inverse2 = norm_of(normed + (branch + back_bias))
     out_ref[...] = (hat2 * gain2 + shift2).astype(BF16)
@@ -396,10 +421,10 @@
     gb_ref[...] = gb
     grad_normed = grad2
     for c in range(0, ff, chunk):
-        gh = (dot_nt(gb, w_back[c : c + chunk, :]) * slope[:, c : c + chunk]).astype(BF16)
+        gh = (dot_nt(gb, w_back[c // chunk]) * slope[:, c : c + chunk]).astype(BF16)
         gh_ref[:, c : c + chunk] = gh
         sums[0:1, c : c + chunk] += sum_rows(gh.astype(F32))
-        grad_normed = grad_normed + dot_nt(gh, w_in[:, c : c + chunk])
+        grad_normed = grad_normed + dot_nt(gh, w_in[c // chunk])
     grad1 = norm_back(grad_normed, hat1, inverse1, gain1)
     resid_ref[...] = grad1
     attn = grad1.astype(BF16)
@@ -416,15 +441,28 @@
     at(1, 3, grad_normed)
     at(2, 0, cot * hat2)
     at(2, 1, cot)
-
-
-def middle(core, x, own, other, cot, w_out, w_in, w_back, vec):
+    for s, ref in enumerate((gc_own, gc_other)):
+        half = ref.shape[1]
+        lane = slice(2 * width + s * half, 2 * width + (s + 1) * half)
+        sums[2:3, lane] += sum_rows(ref[...].astype(F32))
+
+
+def middle(core, x, own, other, cot, weights, vec):
     count, width = x.shape
-    ff = w_in.shape[1]
+    ff = vec.shape[1]
+    parts = ff // width
+    devices = weights.shape[0]
+    unit = width // devices
+    once = pl.Buffered(1)
+    half_spec = lambda at: pl.BlockSpec(
+        (devices // 2, unit, width), lambda i, core: (at(core[0]), 2 * parts, 0), pipeline_mode=once
+    )
+    in_spec = lambda j: pl.BlockSpec(
+        (devices, unit, width), lambda i, core: (0, parts + j, 0), pipeline_mode=once
+    )
     half = own.shape[1]
     rows = min(256, count)
     tile = lambda w: pl.BlockSpec((rows, w), lambda i, core: (i, 0))
-    once = pl.Buffered(1)
     whole = lambda a: pl.BlockSpec(a.shape, lambda i, core: (0, 0), pipeline_mode=once)
     return pl.pallas_call(
         functools.partial(middle_kernel, width=width, ff=ff),
@@ -436,10 +474,10 @@
                 tile(half),
                 tile(half),
                 tile(width),
-                pl.BlockSpec((half, width), lambda i, core: (core[0], 0), pipeline_mode=once),
-                pl.BlockSpec((half, width), lambda i, core: (1 - core[0], 0), pipeline_mode=once),
-                whole(w_in),
-                whole(w_back),
+                half_spec(lambda c: c),
+                half_spec(lambda c: 1 - c),
+                *[in_spec(j) for j in range(parts)],
+                pl.BlockSpec((devices, parts * unit, width), lambda i, core: (0, 0, 0), pipeline_mode=once),
                 whole(vec),
             ],
             out_specs=[
@@ -454,7 +492,13 @@
                 tile(width),
                 pl.BlockSpec((8, ff), lambda i, core: (0, 0)),
             ],
-            scratch_shapes=[pltpu.VMEM((rows, ff), F32)],
+            scratch_shapes=[
+                pltpu.VMEM((rows, ff), F32),
+                pltpu.VMEM((half, width), BF16),
+                pltpu.VMEM((half, width), BF16),
+                pltpu.VMEM((parts, width, width), BF16),
+                pltpu.VMEM((parts, width, width), BF16),
+            ],
         ),
         out_shape=[
             jax.ShapeDtypeStruct((count, width), BF16),
@@ -475,7 +519,333 @@
             transcendentals=2 * count * ff,
         ),
         name="middle",
-    )(core, x, own, other, cot, w_out, w_out, w_in, w_back, vec)
+    )(core, x, own, other, cot, *([weights] * (3 + parts)), vec)
+
+
+def weight_grads_kernel(
+    core, act, gb, low, gh, own, other, attn, keep_ref, send_ref, stage_a, stage_b, sems, *, parts
+):
+    step = pl.program_id(0)
+    inner, outer, _, unit, width = keep_ref.shape
+    last = 2 * parts
+
+    def tn(a, b):
+        return lax.dot_general(a, b, (((0,), (0,)), ((), ())), preferred_element_type=F32).astype(BF16)
+
+    def copies(t):
+        slot = t % 2
+        runs = 2 * outer // parts if t < parts else 2 * outer
+        found = []
+        for r in range(runs):
+            g = t * runs + r if t < parts else r
+            take = slice(r * inner, (r + 1) * inner)
+            at = (slice(None), g % outer, slice(0, parts) if t < parts else t)
+            source = (stage_a if t < parts else stage_b).at[slot, take]
+            found.append(
+                (g // outer,)
+                + tuple(
+                    functools.partial(pltpu.make_async_copy, source, ref.at[at], sems.at[slot])
+                    for ref in (keep_ref, send_ref)
+                )
+            )
+        return found
+
+    def finish(t):
+        for _, keep, _ in copies(t):
+            keep().wait()
+
+    for t in range(2, last + 1):
+
+        @pl.when(step == t)
+        def _():
+            finish(t - 2)
+
+    slot = lax.rem(step, 2)
+
+    @pl.when(step < parts)
+    def _():
+        stage_a[slot] = tn(act[...], gb[...]).reshape(stage_a.shape[1:])
+
+    @pl.when(jnp.logical_and(step >= parts, step < last))
+    def _():
+        stage_b[slot] = tn(low[...], gh[...]).reshape(stage_b.shape[1:])
+
+    @pl.when(step == last)
+    def _():
+        half = stage_b.shape[1] // 2
+        stage_b[slot, :half] = tn(own[...], attn[...]).reshape((half,) + stage_b.shape[2:])
+        stage_b[slot, half:] = tn(other[...], attn[...]).reshape((half,) + stage_b.shape[2:])
+
+    for t in range(last + 1):
+
+        @pl.when(step == t)
+        def _():
+            for c, keep, send in copies(t):
+                if t == last:
+                    (keep if c == 0 else send)().start()
+                    continue
+
+                @pl.when(core[0] == c)
+                def _():
+                    keep().start()
+
+                @pl.when(core[0] != c)
+                def _():
+                    send().start()
+
+    @pl.when(step == last)
+    def _():
+        finish(last - 1)
+        finish(last)
+
+
+def weight_grads(core, act, gb, low, gh, own, other, attn, inner, outer):
+    count, width = low.shape
+    parts = act.shape[1] // width
+    unit = width // (2 * inner * outer)
+    once = pl.Buffered(1)
+    whole = lambda a: pl.BlockSpec(a.shape, lambda t, core: (0, 0), pipeline_mode=once)
+    shape = jax.ShapeDtypeStruct((inner, outer, 2 * parts + 1, unit, width), BF16)
+    return pl.pallas_call(
+        functools.partial(weight_grads_kernel, parts=parts),
+        grid_spec=pltpu.PrefetchScalarGridSpec(
+            num_scalar_prefetch=1,
+            grid=(2 * parts + 1,),
+            in_specs=[
+                pl.BlockSpec((count, width), lambda t, core: (0, jnp.minimum(t, parts - 1))),
+                whole(gb),
+                whole(low),
+                pl.BlockSpec((count, width), lambda t, core: (0, jnp.clip(t - parts, 0, parts - 1))),
+                whole(own),
+                whole(other),
+                whole(attn),
+            ],
+            out_specs=[pl.BlockSpec(memory_space=pl.ANY)] * 2,
+            scratch_shapes=[
+                pltpu.VMEM((2, 2 * inner * outer // parts, parts, unit, width), BF16),
+                pltpu.VMEM((2, 2 * inner * outer, unit, width), BF16),
+                pltpu.SemaphoreType.DMA((2,)),
+            ],
+        ),
+        out_shape=[shape, shape],
+        compiler_params=pltpu.CompilerParams(vmem_limit_bytes=VMEM_BYTES),
+        cost_estimate=pl.CostEstimate(
+            flops=2 * count * width * width * (2 * parts + 1),
+            bytes_accessed=2 * width * (2 * parts + 4) * (count + width),
+            transcendentals=0,
+        ),
+        name="weight_grads",
+    )(core, act, gb, low, gh, own, other, attn)
+
+
+def project_kernel(x0, x1, x2, x3, first, second, bias, out_ref, weight_ref, *, group):
+    step = pl.program_id(0)
+    blocks, width = pl.num_programs(0) // 4, x0.shape[1]
+    rows = first.shape[0] * (weight_ref.shape[0] // first.shape[0] // 2)
+
+    @pl.when(step == 0)
+    def _():
+        unit = weight_ref.shape[0] // (2 * first.shape[0])
+        weight_ref[:rows, :] = first[:, :unit, :].reshape(rows, 3 * group)
+        weight_ref[rows:, :] = second[:, :unit, :].reshape(rows, 3 * group)
+
+    for p, ref in enumerate((x0, x1, x2, x3)):
+
+        @pl.when(step // blocks == p)
+        def _():
+            start = 0 if p < 2 else group
+            got = dot(ref[...], weight_ref[:, start:]) + bias[0:1, start:]
+            out_ref[0, :, start:] = got.astype(BF16)
+
+
+def project(pieces, first, second, bias):
+    count, width = pieces[0].shape
+    wide = first.shape[2]
+    rows = min(512, count)
+    blocks = count // rows
+    once = pl.Buffered(1)
+    piece = lambda p: pl.BlockSpec((rows, width), lambda i: (jnp.clip(i - p * blocks, 0, blocks - 1), 0))
+    whole = lambda a: pl.BlockSpec(a.shape, lambda i: (0,) * a.ndim, pipeline_mode=once)
+    return pl.pallas_call(
+        functools.partial(project_kernel, group=wide // 3),
+        grid=(4 * blocks,),
+        in_specs=[piece(p) for p in range(4)] + [whole(first), whole(second), whole(bias)],
+        out_specs=[
+            pl.BlockSpec((1, rows, wide), lambda i: (i // (2 * blocks), i % (2 * blocks), 0)),
+            pl.BlockSpec((width, wide), lambda i: (0, 0)),
+        ],
+        out_shape=[
+            jax.ShapeDtypeStruct((2, 2 * count, wide), BF16),
+            jax.ShapeDtypeStruct((width, wide), BF16),
+        ],
+        compiler_params=pltpu.CompilerParams(vmem_limit_bytes=VMEM_BYTES),
+        cost_estimate=pl.CostEstimate(
+            flops=2 * 4 * count * width * wide, bytes_accessed=8 * count * (width + wide), transcendentals=0
+        ),
+        name="project",
+    )(*pieces, first, second, bias)
+
+
+def far_rows_kernel(dkv, weight, keep_ref, send_ref, *, group):
+    step = pl.program_id(0)
+    got = dot_nt(dkv[0].T, weight[:, group:]).astype(BF16)
+
+    @pl.when(step < pl.num_programs(0) // 2)
+    def _():
+        keep_ref[...] = got
+
+    @pl.when(step >= pl.num_programs(0) // 2)
+    def _():
+        send_ref[...] = got
+
+
+def far_rows(dkv, weight):
+    count, (width, wide) = dkv.shape[2], weight.shape
+    rows = min(512, count // 2)
+    blocks = count // rows
+    return pl.pallas_call(
+        functools.partial(far_rows_kernel, group=wide // 3),
+        grid=(blocks,),
+        in_specs=[
+            pl.BlockSpec((1, dkv.shape[1], rows), lambda i: (1, 0, i)),
+            pl.BlockSpec((width, wide), lambda i: (0, 0), pipeline_mode=pl.Buffered(1)),
+        ],
+        out_specs=[
+            pl.BlockSpec((rows, width), lambda i: (jnp.minimum(i, blocks // 2 - 1), 0)),
+            pl.BlockSpec((rows, width), lambda i: (jnp.maximum(i - blocks // 2, 0), 0)),
+        ],
+        out_shape=[jax.ShapeDtypeStruct((count // 2, width), BF16)] * 2,
+        compiler_params=pltpu.CompilerParams(vmem_limit_bytes=VMEM_BYTES),
+        cost_estimate=pl.CostEstimate(
+            flops=2 * count * width * dkv.shape[1], bytes_accessed=8 * count * width, transcendentals=0
+        ),
+        name="far_rows",
+    )(dkv, weight)
+
+
+def near_rows_kernel(dq, dkv, weight, resid, keep_ref, send_ref, *, group):
+    step = pl.program_id(0)
+    got = dot_nt(dq[...].T, weight[:, :group]) + dot_nt(dkv[0].T, weight[:, group:])
+
+    @pl.when(step < pl.num_programs(0) // 2)
+    def _():
+        keep_ref[...] = got + resid[...]
+
+    @pl.when(step >= pl.num_programs(0) // 2)
+    def _():
+        send_ref[...] = got.astype(BF16)
+
+
+def near_rows(dq, dkv, weight, resid):
+    count, (width, wide) = dkv.shape[2], weight.shape
+    rows = min(512, count // 2)
+    blocks = count // rows
+    return pl.pallas_call(
+        functools.partial(near_rows_kernel, group=wide // 3),
+        grid=(blocks,),
+        in_specs=[
+            pl.BlockSpec((dq.shape[0], rows), lambda i: (0, i)),
+            pl.BlockSpec((1, dkv.shape[1], rows), lambda i: (0, 0, i)),
+            pl.BlockSpec((width, wide), lambda i: (0, 0), pipeline_mode=pl.Buffered(1)),
+            pl.BlockSpec((rows, width), lambda i: (jnp.minimum(i, blocks // 2 - 1), 0)),
+        ],
+        out_specs=[
+            pl.BlockSpec((rows, width), lambda i: (jnp.minimum(i, blocks // 2 - 1), 0)),
+            pl.BlockSpec((rows, width), lambda i: (jnp.maximum(i - blocks // 2, 0), 0)),
+        ],
+        out_shape=[
+            jax.ShapeDtypeStruct((count // 2, width), F32),
+            jax.ShapeDtypeStruct((count // 2, width), BF16),
+        ],
+        compiler_params=pltpu.CompilerParams(vmem_limit_bytes=VMEM_BYTES),
+        cost_estimate=pl.CostEstimate(
+            flops=2 * count * width * wide, bytes_accessed=12 * count * width, transcendentals=0
+        ),
+        name="near_rows",
+    )(dq, dkv, weight, resid)
+
+
+def qkv_grads_kernel(core, dq, dkv, x0, x1, x2, x3, small, out_ref):
+    step = pl.program_id(0)
+    blocks, unit = out_ref.shape[1], x0.shape[1] // (2 * out_ref.shape[1])
+    local = x0.shape[0]
+
+    def put(value):
+        value = value.T.astype(BF16)
+        half = value.shape[0] // 2
+        for h in (0, 1):
+            place_at = (core[0] + h) % 2
+            out_ref[place_at, :, :unit, :] = value[h * half : (h + 1) * half].reshape(blocks, unit, -1)
+
+    @pl.when(step == 0)
+    def _():
+        put(dot(dq[:, :local], x0[...]) + dot(dq[:, local:], x1[...]))
+
+    @pl.when(step > 0)
+    def _():
+        near, far = dkv[0, 0], dkv[1, 0]
+        put(
+            dot(near[:, :local], x0[...])
+            + dot(near[:, local:], x1[...])
+            + dot(far[:, :local], x2[...])
+            + dot(far[:, local:], x3[...])
+        )
+
+    out_ref[:, :, unit:, :] = small[...]
+
+
+def qkv_grads(core, dq, dkv, pieces, small):
+    count, width = pieces[0].shape
+    group, full = dq.shape
+    blocks, extra = small.shape[1:3]
+    unit = width // (2 * blocks)
+    once = pl.Buffered(1)
+    whole = pl.BlockSpec((count, width), lambda t, core: (0, 0), pipeline_mode=once)
+    return pl.pallas_call(
+        qkv_grads_kernel,
+        grid_spec=pltpu.PrefetchScalarGridSpec(
+            num_scalar_prefetch=1,
+            grid=(3,),
+            in_specs=[
+                pl.BlockSpec((group, full), lambda t, core: (0, 0), pipeline_mode=once),
+                pl.BlockSpec((2, 1, group, full), lambda t, core: (0, jnp.maximum(t - 1, 0), 0, 0)),
+                whole,
+                whole,
+                whole,
+                whole,
+                pl.BlockSpec((2, blocks, extra, group), lambda t, core: (0, 0, 0, t)),
+            ],
+            out_specs=pl.BlockSpec((2, blocks, unit + extra, group), lambda t, core: (0, 0, 0, t)),
+        ),
+        out_shape=jax.ShapeDtypeStruct((2, blocks, unit + extra, 3 * group), BF16),
+        compiler_params=pltpu.CompilerParams(vmem_limit_bytes=VMEM_BYTES),
+        cost_estimate=pl.CostEstimate(
+            flops=10 * full * width * group, bytes_accessed=16 * full * width, transcendentals=0
+        ),
+        name="qkv_grads",
+    )(core, dq, dkv, *pieces, small)
+
+
+GATE = 4
+ORDER = 0
+
+
+def unpacked(blocks, parts):
+    devices, size, width = blocks.shape
+    rows = size // (2 * parts + 1)
+    back = blocks[:, : parts * rows].reshape(devices * parts * rows, width)
+    into = blocks[:, parts * rows : 2 * parts * rows].reshape(devices, parts, rows, width)
+    into = into.transpose(0, 2, 1, 3).reshape(devices * rows, parts * width)
+    return back, into, blocks[:, 2 * parts * rows :].reshape(devices * rows, width)
+
+
+def packed(back, into, out, devices):
+    rows, width = out.shape[0] // devices, out.shape[1]
+    parts = back.shape[0] // out.shape[0]
+    into = into.reshape(devices, rows, parts, width).transpose(0, 2, 1, 3)
+    return jnp.concatenate(
+        [a.reshape(devices, -1, width) for a in (back, into, out)], axis=1
+    )
 
 
 def dot_tn(a, b):
@@ -515,38 +885,30 @@
     rows = w_qkv.shape[0]
     x = tokens[0]
 
-    shard = jnp.concatenate(
-        [w_in, w_back.reshape(parts, rows, width).transpose(1, 0, 2).reshape(rows, ff), w_out], axis=1
-    )
-    gathered = lax.all_gather(shard, both, axis=0, tiled=True)
-    full_in = gathered[:, :ff]
-    full_back = (
-        gathered[:, ff : 2 * ff]
-        .reshape(cores * blocks, rows, parts, width)
-        .transpose(0, 2, 1, 3)
-        .reshape(ff, width)
-    )
-    full_out = gathered[:, 2 * ff :]
-
     x_sib = swap(x, "head", 1)
     x_far = swap(x, "blk", 1)
-    vectors = jnp.concatenate(
-        [q_bias, v_bias, out_bias, back_bias, norm1_gain, norm1_shift, norm2_gain, norm2_shift, in_bias]
-    )
-    vectors = jnp.pad(vectors, (0, 3 * group - vectors.shape[0]))
-    extra = jnp.pad(vectors[None], ((0, 7), (0, 0)))
+    vectors = jnp.stack(
+        [q_bias, v_bias, out_bias, back_bias, norm1_gain, norm1_shift, norm2_gain, norm2_shift], axis=0
+    )
+    extra = jnp.concatenate(
+        [
+            jnp.pad(vectors, ((0, 0), (0, LANES - rows))),
+            jnp.pad(in_bias[None], ((0, 7), (0, 3 * group - LANES - parts * rows))),
+        ],
+        axis=1,
+    )
     columns = w_qkv.reshape(rows, 3, cores, group)
     kept = lax.dynamic_index_in_dim(columns, core, 2, keepdims=False).reshape(rows, 3 * group)
     given = lax.dynamic_index_in_dim(columns, 1 - core, 2, keepdims=False).reshape(rows, 3 * group)
     mine = jnp.concatenate([kept, extra], axis=0)
     theirs = swap(jnp.concatenate([given, extra], axis=0), "head", 1)
-    first, second = gather_blk(place(mine, theirs, core == 1, 0))
-    x_far_sib = swap(x_far, "head", 1)
-    weight = jnp.concatenate([first[:, :rows], second[:, :rows]], axis=0).reshape(width, 3 * group)
-    small = jnp.concatenate([first[:, rows], second[:, rows]], axis=0)
-
-    def vector(slot, size=rows):
-        return small[:, slot * rows : slot * rows + size].reshape(-1).astype(F32)
+    first, second, x_far = gather_blk(place(mine, theirs, core == 1, 0), x_far)
+    small = jnp.concatenate([first[:, rows:, : 2 * LANES], second[:, rows:, : 2 * LANES]], axis=0)
+
+    def vector(slot):
+        if slot == 8:
+            return small[:, 0, LANES : LANES + parts * rows].reshape(-1).astype(F32)
+        return small[:, slot, :rows].reshape(-1).astype(F32)
 
     bias = jnp.concatenate(
         [
@@ -557,7 +919,7 @@
     )
     vec = jnp.concatenate(
         [
-            vector(8, parts * rows)[None],
+            vector(8)[None],
             jnp.pad(jnp.concatenate([vector(2), vector(3), vector(4), vector(5)]), (0, ff - 4 * width))[None],
             jnp.pad(jnp.concatenate([vector(6), vector(7)]), (0, ff - 2 * width))[None],
             jnp.zeros((5, ff), F32),
@@ -565,8 +927,32 @@
         axis=0,
     )
 
-    xs = jnp.concatenate([x, x_sib, x_far, x_far_sib], axis=0)
-    qkv = (dot(xs, weight) + bias).astype(BF16).reshape(2, half, 3 * group)
+    shard = jnp.concatenate(
+        [w_back, w_in.reshape(rows, parts, width).transpose(1, 0, 2).reshape(parts * rows, width), w_out], axis=0
+    )
+    if GATE in (1, 4):
+        shard, x_far = lax.optimization_barrier((shard, x_far))
+    elif GATE in (2, 6):
+        shard, first = lax.optimization_barrier((shard, first))
+    elif GATE == 3:
+        shard, first, x_far = lax.optimization_barrier((shard, first, x_far))
+    gathered = lax.all_gather(shard, both, axis=0, tiled=True).reshape(cores * blocks, -1, width)
+    direct = rows % 8 == 0 and blocks % 4 == 0 and (2 * blocks) % (4 * parts) == 0
+    if direct:
+        inner, outer = 4, blocks // 4
+    else:
+        inner, outer = 4, 4
+        gathered = packed(*unpacked(gathered, parts), cores * inner * outer)
+
+    pieces = (x, x_sib, x_far, swap(x_far, "head", 1))
+    bias = jnp.pad(bias[None], ((0, 7), (0, 0)))
+    if direct:
+        qkv, weight = project(pieces, first, second, bias)
+    else:
+        shape = (16, width // 32, 3 * group)
+        qkv, weight = project(
+            pieces, first[:, :rows].reshape(shape), second[:, :rows].reshape(shape), bias
+        )
 
     sequence = block // 2
     own_half = block % 2
@@ -578,67 +964,36 @@
 
     context, lse = attend(sc, qkv, group)
     other = swap(context[local:], "head", 1)
+    at_core = core.reshape(1).astype(jnp.int32)
     out, grad_resid1, gc_own, gc_other, low, act, gh, gb, attn, sums = middle(
-        core.reshape(1).astype(jnp.int32),
-        x,
-        context[:local],
-        other,
-        cotangent[0],
-        full_out,
-        full_in,
-        full_back,
-        vec,
+        at_core, x, context[:local], other, cotangent[0], gathered, vec
     )
     grad_context = jnp.concatenate([gc_own, swap(gc_other, "head", 1)], axis=0)
 
-    context_rows = place(context[:local], other, core == 1, 1).reshape(local, width)
-    grad_in = dot_tn(low, gh).astype(BF16)
-    grad_back = dot_tn(act, gb).astype(BF16)
-    grad_out = dot_tn(context_rows, attn).astype(BF16)
-    packed = jnp.concatenate(
-        [
-            grad_in,
-            grad_back.reshape(cores * blocks, parts, rows, width).transpose(0, 2, 1, 3).reshape(width, ff),
-            grad_out,
-        ],
-        axis=1,
-    )
-    reduced = lax.psum_scatter(packed, both, scatter_dimension=0, tiled=True)
-    sum_win = reduced[:, :ff].astype(F32)
-    sum_wback = (
-        reduced[:, ff : 2 * ff].reshape(rows, parts, width).transpose(1, 0, 2).reshape(parts * rows, width)
-    ).astype(F32)
-    sum_wout = reduced[:, 2 * ff :].astype(F32)
-
-    dq, dk, dv = attend_back(sc, qkv, context, lse, grad_context, group)
-    wq, wk, wv = weight[:, :group], weight[:, group : 2 * group], weight[:, 2 * group :]
-
-    def back_rows(which):
-        return lax.dot_general(dk[which], wk, (((0,), (1,)), ((), ())), preferred_element_type=F32) + (
-            lax.dot_general(dv[which], wv, (((0,), (1,)), ((), ())), preferred_element_type=F32)
-        )
-
-    dx_far = back_rows(1)
-    dx_near = back_rows(0) + dot_nt(dq, wq)
-    far_sib = swap(dx_far[local:].astype(BF16), "head", 1)
-    far_in = swap((dx_far[:local] + far_sib.astype(F32)).astype(BF16), "blk", 1)
-    near_sib = swap(dx_near[local:].astype(BF16), "head", 1)
-    grad_tokens = grad_resid1 + dx_near[:local] + near_sib.astype(F32) + far_in.astype(F32)
-
-    both_halves = xs.reshape(2, half, width)
-    over = (((0, 1), (0, 2)), ((), ()))
-    grad_w = jnp.concatenate(
-        [
-            dot_tn(both_halves[0], dq),
-            lax.dot_general(both_halves, dk, over, preferred_element_type=F32),
-            lax.dot_general(both_halves, dv, over, preferred_element_type=F32),
-        ],
-        axis=1,
-    ).astype(BF16)
+    keep, send = weight_grads(at_core, act, gb, low, gh, context[:local], other, attn, inner, outer)
+    chip = (keep.astype(F32) + swap(send, "head", 1).astype(F32)).astype(BF16)
+    if direct:
+        chip = chip.reshape(inner * outer * (2 * parts + 1) * rows, width)
+        near = [[o * inner + i for i in range(inner)] for o in range(outer)]
+        far = [[o * inner + i for o in range(outer)] for i in range(inner)]
+        for groups in (near, far):
+            chip = lax.psum_scatter(chip, "blk", scatter_dimension=0, axis_index_groups=groups, tiled=True)
+    else:
+        chip = chip.transpose(1, 0, 2, 3, 4).reshape(inner * outer, -1, width)
+        chip = packed(*unpacked(chip, parts), blocks)
+        chip = lax.psum_scatter(chip, "blk", scatter_dimension=0, tiled=True)[0]
+    sum_wback = chip[: parts * rows].astype(F32)
+    sum_win = chip[parts * rows : 2 * parts * rows].astype(F32)
+    sum_win = sum_win.reshape(parts, rows, width).transpose(1, 0, 2).reshape(rows, ff)
+    sum_wout = chip[2 * parts * rows :].astype(F32)
+
+    dq, dkv, dq_sum = attend_back(sc, qkv, context, lse, grad_context, group)
+    joint = dkv.reshape(2, 2 * group, half)
+
     at_group = lambda v: lax.dynamic_update_slice_in_dim(jnp.zeros((width,), F32), v, core * group, 0)
     grad_small = [
-        at_group(jnp.sum(dq.astype(F32), axis=0)),
-        at_group(jnp.sum(dv.astype(F32), axis=(0, 2))),
+        at_group(jnp.sum(dq_sum, axis=1)),
+        place(sums[2, 2 * width : 2 * width + group], sums[2, 2 * width + group : 3 * width], core == 1, 0).reshape(-1),
         sums[1, :width],
         sums[1, width : 2 * width],
         sums[1, 2 * width : 3 * width],
@@ -656,11 +1011,22 @@
     high = grad_small.astype(BF16)
     low_part = (grad_small - high.astype(F32)).astype(BF16)
     small_rows = jnp.pad(jnp.stack([high, low_part], axis=2), ((0, 0), (0, 0), (0, 6), (0, 0)))
-    outgoing = jnp.concatenate([grad_w.reshape(cores, blocks, rows, 3 * group), small_rows], axis=2)
-    keep = lax.dynamic_index_in_dim(outgoing, core, 0, keepdims=False)
-    send = lax.dynamic_index_in_dim(outgoing, 1 - core, 0, keepdims=False)
-    came = swap(send, "head", 1)
+    small_rows = jnp.where(core == 0, small_rows, small_rows[::-1])
+    if direct:
+        outgoing = qkv_grads(at_core, dq, dkv, pieces, small_rows)
+    else:
+        none = jnp.zeros((2, 16, 8, 3 * group), BF16)
+        outgoing = qkv_grads(at_core, dq, dkv, pieces, none)[:, :, : width // 32]
+        outgoing = jnp.concatenate([outgoing.reshape(2, blocks, rows, 3 * group), small_rows], axis=2)
+    keep, came = outgoing[0], swap(outgoing[1], "head", 1)
     exchanged = lax.all_to_all(jnp.stack([keep, came], axis=1), "blk", 0, 0, tiled=True).astype(F32)
+    keep_far, send_far = far_rows(joint, weight)
+    far_sib = swap(send_far, "head", 1)
+    far_in = swap((keep_far.astype(F32) + far_sib.astype(F32)).astype(BF16), "blk", 1)
+    keep_near, send_near = near_rows(dq, joint, weight, grad_resid1)
+    near_sib = swap(send_near, "head", 1)
+    grad_tokens = keep_near + near_sib.astype(F32) + far_in.astype(F32)
+
     total = jnp.sum(exchanged, axis=0)
     own_w, other_w = (total[s, :rows].reshape(rows, 3, group) for s in (0, 1))
     sum_wqkv = place(own_w, other_w, core == 1, 2).reshape(rows, 3 * width)

time: 508 us -> 418 us (0.82)
  Pallas kernels: 147 us -> 216 us
  matrix products: 60.5 us -> 0 us
  local copies, waits for them, and re-layouts: 62.1 us -> 19.6 us
  waiting for transfers between devices: 154 us -> 113 us
  other arithmetic: 37.8 us -> 28.2 us
    pallas_call x0 -> x5, Pallas kernels: none -> 63.5 us  [the longest x1 19.6 us: weight_grads(): pl.pallas_call(functools.partial(weight_grads_kernel, parts=parts), grid_...]
    dot_general x12 -> x0, matrix products: 60.5 us -> none  [the longest x4 18.2 us: dot_tn(): lax.dot_general(a, b, (((0,), (0,)), ((), ())), preferred_element_type=F32)]
    ppermute x16 -> x17, waiting for transfers between devices: 154 us -> 113 us  [swap(): return lax.ppermute(value, axis, pairs)]
    reshape x5 -> x2, local copies, waits for them, and re-layouts: 27.4 us -> 0.74 us  [the longest x1 0.73 us: per_device(): sum_win.reshape(parts, rows, width).transpose(1, 0, 2).reshape(rows, ff)]
    concatenate x7 -> x2, other arithmetic: 16.7 us -> 1.48 us  [the longest x1 0.76 us: per_device(): jnp.concatenate([w_back, w_in.reshape(rows, parts, width).transpose(1, 0,...]
    slice x8 -> x2, local copies, waits for them, and re-layouts: 12.3 us -> 0.01 us  [the longest x1 0.01 us: per_device(): second[:, rows:, :2 * LANES]]
    convert_element_type x4 -> x6, other arithmetic: 5.22 us -> 13.9 us  [the longest x1 7.66 us: per_device(): chip = (keep.astype(F32) + swap(send, 'head', 1).astype(F32)).astype(BF16)]
    concatenate x2 -> x1, local copies, waits for them, and re-layouts: 6.18 us -> 0.07 us  [per_device(): jnp.concatenate([vector(8)[None], jnp.pad(jnp.concatenate([vector(2), vec...]
  transfers between devices with their start and end apart: 19 -> 21, of which waited for: 8 -> 13; matrix products, arithmetic and copies ran while one was open for 23% -> 7% of each run, Pallas kernels for 22% -> 38%
where the time goes in v2:
time: 418 us; the launch traced here: 412 us
  Pallas kernels  216 us (52%)
  waiting for transfers between devices  113 us (27%)
  other arithmetic  28.2 us (7%)
  local copies, waits for them, and re-layouts  19.6 us (5%)
  starting transfers between devices  19.4 us (5%)
  between operations  16.1 us (4%)
    ppermute x17, waiting for transfers between devices, swap(): return lax.ppermute(value, axis, pairs)  113 us
    pallas_call x1, Pallas kernels, attend_back(): pl.pallas_call(functools.partial(attend_back_kernel, heads=heads, step=mi...  70.2 us
    pallas_call x1, Pallas kernels, attend(): pl.pallas_call(functools.partial(attend_kernel, heads=heads, step=min(512...  42.3 us
    pallas_call x1, Pallas kernels, middle(): pl.pallas_call(functools.partial(middle_kernel, width=width, ff=ff), grid...  39.8 us
    pallas_call x1, Pallas kernels, weight_grads(): pl.pallas_call(functools.partial(weight_grads_kernel, parts=parts), grid_...  19.6 us
    ppermute x17, starting transfers between devices, swap(): return lax.ppermute(value, axis, pairs)  15.6 us
    pallas_call x1, Pallas kernels, project(): pl.pallas_call(functools.partial(project_kernel, group=wide // 3), grid=(...  14.5 us
    pallas_call x1, Pallas kernels, qkv_grads(): pl.pallas_call(qkv_grads_kernel, grid_spec=pltpu.PrefetchScalarGridSpec(n...  12.4 us
  transfers between devices with their start and end apart: 21, of which 13 were waited for; matrix products, arithmetic and copies ran while one was open for 7% of the time, Pallas kernels for 38%

profile of v2, /device:TPU:0, one launch (start us, length us, event | category | flops | bytes accessed | tf_op | source)
XLA Modules:
  0.0 412.1 jit_solution(3956536725399872226)
XLA Ops:
  12.6 4.0 collective-permute-start.2
  18.1 5.8 %collective-permute-done.2 = bf16[2,32,1152]{2,1,0:T(8,128)(2,1)S(1)} collective-permute-done((bf16[2,32,1152]{2,1,0:T(8,128)(2,1)S(1)}, bf16[2,32,1152]{2,1,0:T(8,128)(2,1)S(1)}, u32[]{:S(2)}, u32[]{:S(2)}) %collective-permute-start.2) | collective-permute-done | bytes 147488 | tf_op jit(solution)/shard_map/ppermute | solution.py:32
  25.6 7.0 %collective-permute-done.3 = bf16[2,2,32,1152]{3,2,0,1:T(8,128)(2,1)S(1)} collective-permute-done((bf16[2,2,32,1152]{3,2,0,1:T(8,128)(2,1)S(1)}, bf16[2,2,32,1152]{3,2,0,1:T(8,128)(2,1)S(1)}, u32[]{:S(2)}, u32[]{:S(2)}) %collective-permute-start.3) | collective-permute-done | bytes 294944 | tf_op jit(solution)/shard_map/ppermute | solution.py:32
  32.7 20.3 %collective-permute-done.4.x2 = bf16[1024,768]{1,0:T(8,128)(2,1)} collective-permute-done((bf16[1024,768]{1,0:T(8,128)(2,1)}, bf16[1024,768]{1,0:T(8,128)(2,1)}, u32[]{:S(2)}, u32[]{:S(2)}) %collective-permute-start.4) | collective-permute-done | bytes 1572896 | tf_op jit(solution)/shard_map/ppermute | solution.py:32
  56.3 4.9 %collective-permute-done.6 = bf16[2,2,32,1152]{3,2,0,1:T(8,128)(2,1)S(1)} collective-permute-done((bf16[2,2,32,1152]{3,2,0,1:T(8,128)(2,1)S(1)}, bf16[2,2,32,1152]{3,2,0,1:T(8,128)(2,1)S(1)}, u32[]{:S(2)}, u32[]{:S(2)}) %collective-permute-start.6) | collective-permute-done | bytes 294944 | tf_op jit(solution)/shard_map/ppermute | solution.py:32
  68.0 10.1 %collective-permute-done.7 = bf16[2,2,2,32,1152]{4,3,0,1,2:T(8,128)(2,1)S(1)} collective-permute-done((bf16[2,2,2,32,1152]{4,3,0,1,2:T(8,128)(2,1)S(1)}, bf16[2,2,2,32,1152]{4,3,0,1,2:T(8,128)(2,1)S(1)}, u32[]{:S(2)}, u32[]{:S(2)}) %collective-permute-start.7) | collective-permute-done | bytes 589856 | tf_op jit(solution)/shard_map/ppermute | solution.py:32
  82.6 14.5 %project.1 = (bf16[2,2048,1152]{2,1,0:T(8,128)(2,1)}, bf16[768,1152]{1,0:T(8,128)(2,1)}) custom-call(bf16[1024,768]{1,0:T(8,128)(2,1)} %bitcast.1.x0.x_ref, bf16[1024,768]{1,0:T(8,128)(2,1)} %collective-permute-done.x1, bf16[1024,768]{1,0:T(8,128)(2,1)} %collective-permute-done.4.x2, bf16[1024,768]{1,0:T(8,128)(2,1)} %collective-permute-done.5.x3, ...), custom_call_target="tpu_custom_call" | custom-call | flops 7247757312 | bytes 15728640 | tf_op jit(solution)/shard_map/project/pallas_call | solution.py:669
  97.1 42.3 %attend.1 = (bf16[2048,384]{1,0:T(8,128)(2,1)}, f32[2048,384]{1,0:T(8,128)}) custom-call(s32[10]{0:T(128)} %concatenate.39.sc, bf16[2,2048,1152]{2,1,0:T(8,128)(2,1)} %get-tuple-element.45.q_ref.ka_ref.kb_ref.va_ref.vb_ref, bf16[2,2048,1152]{2,1,0:T(8,128)(2,1)} %get-tuple-element.45.q_ref.ka_ref.kb_ref.va_ref.vb_ref, ...), custom_call_target="tpu_custom_call" | custom-call | flops 25769803776 | bytes 9437184 | tf_op jit(solution)/shard_map/attend/pallas_call | solution.py:171
  139.3 2.5 fusion.31
  145.0 39.8 %middle.1 = (bf16[1024,768]{1,0:T(8,128)(2,1)}, f32[1024,768]{1,0:T(8,128)}, bf16[1024,384]{1,0:T(8,128)(2,1)}, bf16[1024,384]{1,0:T(8,128)(2,1)}, bf16[1024,768...) custom-call(s32[1]{0:T(128)} %bitcast.core, ...), custom_call_target="tpu_custom_call" | custom-call | flops 21743271936 | bytes 44040192 | tf_op jit(solution)/shard_map/middle/pallas_call | solution.py:467
  184.8 19.6 %weight_grads.1 = (bf16[4,4,9,24,768]{4,3,2,1,0:T(8,128)(2,1)}, bf16[4,4,9,24,768]{4,3,2,1,0:T(8,128)(2,1)}) custom-call(s32[1]{0:T(128)} %bitcast.core, bf16[1024,3072]{1,0:T(8,128)(2,1)} %get-tuple-element.62.act, bf16[1024,768]{1,0:T(8,128)(2,1)} %get-tuple-element.63.gb, bf16[1024,768]{1,0:T(8,128)(2,1)} %get-tuple-element.64.low, ...), custom_call_target="tpu_custom_call" | custom-call | flops 10871635968 | bytes 33030144 | tf_op jit(solution)/shard_map/weight_grads/pallas_call | solution.py:609
  208.2 3.2 collective-permute-done.11
  212.7 2.0 collective-permute-done.16
  214.7 7.7 %add_convert_fusion = bf16[4,4,9,24,768]{4,3,2,1,0:T(8,128)(2,1)} fusion(bf16[4,4,9,24,768]{4,3,2,1,0:T(8,128)(2,1)} %collective-permute-done.16, bf16[4,4,9,24,768]{4,3,2,1,0:T(8,128)(2,1)} %get-tuple-element.67), kind=kLoop, calls=%fused_computation | loop fusion | flops 10616832 | bytes 15925248 | tf_op jit(solution)/shard_map/convert_element_type | solution.py:974
  222.4 70.2 %attend_back.1 = (bf16[384,2048]{1,0:T(8,128)(2,1)}, bf16[2,2,384,2048]{3,2,1,0:T(8,128)(2,1)}, f32[384,128]{1,0:T(8,128)}) custom-call(s32[10]{0:T(128)} %concatenate.39.sc, bf16[2,2048,1152]{2,1,0:T(8,128)(2,1)} %get-tuple-element.45.q_ref.ka_ref.kb_ref.va_ref.vb_ref, bf16[2,2048,1152]{2,1,0:T(8,128)(2,1)} %get-tuple-element.45.q_ref.ka_ref.kb_ref.va_ref.vb_ref, ...), custom_call_target="tpu_custom_call" | custom-call | flops 64424509440 | bytes 18874368 | tf_op jit(solution)/shard_map/attend_back/pallas_call | solution.py:301
  295.8 12.4 %qkv_grads.1 = bf16[2,16,32,1152]{3,2,1,0:T(8,128)(2,1)} custom-call(s32[1]{0:T(128)} %bitcast.core, bf16[384,2048]{1,0:T(8,128)(2,1)} %get-tuple-element.52.dq, bf16[2,2,384,2048]{3,2,1,0:T(8,128)(2,1)} %get-tuple-element.53.dkv, bf16[1024,768]{1,0:T(8,128)(2,1)} %bitcast.1.x0.x_ref, bf16[1024,768]{1,0:T(8,128)(2,1)} %collective-permute-done.x1, ...), custom_call_target="tpu_custom_call" | custom-call | flops 6039797760 | bytes 25165824 | tf_op jit(solution)/shard_map/qkv_grads/pallas_call | solution.py:804
  308.2 1.8 slice_bitcast_fusion.1
  310.2 2.7 collective-permute-done.15
  314.9 3.7 all-to-all-start
  318.7 7.2 %far_rows.1 = (bf16[1024,768]{1,0:T(8,128)(2,1)}, bf16[1024,768]{1,0:T(8,128)(2,1)}) custom-call(bf16[2,768,2048]{2,1,0:T(8,128)(2,1)} %bitcast.149, bf16[768,1152]{1,0:T(8,128)(2,1)} %get-tuple-element.54.weight), custom_call_target="tpu_custom_call" | custom-call | flops 2415919104 | bytes 12582912 | tf_op jit(solution)/shard_map/far_rows/pallas_call | solution.py:706
  326.0 10.0 %near_rows.1 = (f32[1024,768]{1,0:T(8,128)}, bf16[1024,768]{1,0:T(8,128)(2,1)}) custom-call(bf16[384,2048]{1,0:T(8,128)(2,1)} %get-tuple-element.52.dq, bf16[2,768,2048]{2,1,0:T(8,128)(2,1)} %bitcast.150, bf16[768,1152]{1,0:T(8,128)(2,1)} %get-tuple-element.54.weight, f32[1024,768]{1,0:T(8,128)} %get-tuple-element.55.resid), custom_call_target="tpu_custom_call" | custom-call | flops 3623878656 | bytes 18874368 | tf_op jit(solution)/shard_map/near_rows/pallas_call | solution.py:743
  336.3 3.0 add_convert_fusion.1
  341.1 52.5 %collective-permute-done.14 = bf16[1024,768]{1,0:T(8,128)(2,1)} collective-permute-done((bf16[1024,768]{1,0:T(8,128)(2,1)}, bf16[1024,768]{1,0:T(8,128)(2,1)}, u32[]{:S(2)}, u32[]{:S(2)}) %collective-permute-start.14) | collective-permute-done | bytes 1572896 | tf_op jit(solution)/shard_map/ppermute | solution.py:32
  393.6 4.9 %add_bitcast_fusion = f32[1,1024,768]{2,1,0:T(8,128)} fusion(bf16[1024,768]{1,0:T(8,128)(2,1)} %collective-permute-done.14, f32[1024,768]{1,0:T(8,128)} %get-tuple-element.56, bf16[1024,768]{1,0:T(8,128)(2,1)} %collective-permute-done.12), kind=kLoop, calls=%fused_computation.2 | loop fusion | flops 3145728 | bytes 9437184 | tf_op jit(solution)/shard_map/broadcast_in_dim | solution.py:1040
  (159 shorter events, 44.2 us)
Async XLA Ops:
  7.2 60.1 %copy-start = (s32[8,12]{1,0:T(8,128)S(1)}, s32[8,12]{1,0:T(8,128)}, u32[]{:S(2)}) copy-start(s32[8,12]{1,0:T(8,128)} %param.19) | copy-start | bytes 1156
  7.2 136.9 %all-gather.2.cloned.1.call-start = ((), (), s32[]{:S(2)}) async-start(), calls=%async_computation.3 | async-start | bytes 10948608 | tf_op jit(solution)/shard_map/all_gather | solution.py:939
  10.5 1.4 collective-permute-start.1
  12.6 11.3 %collective-permute-start.2 = (bf16[2,32,1152]{2,1,0:T(8,128)(2,1)S(1)}, bf16[2,32,1152]{2,1,0:T(8,128)(2,1)S(1)}, u32[]{:S(2)}, u32[]{:S(2)}) collective-permute-start(bf16[2,32,1152]{2,1,0:T(8,128)(2,1)S(1)} %pad_maximum_fusion.10), channel_id=1, source_target_pairs={{0,8},{1,9},{2,10},{3,11},{4,12},{5,13},{6,14},{7,15},{8,0},{9,1},... | collective-permute-start | bytes 442376 | tf_op jit(solution)/shard_map/ppermute | solution.py:32
  16.6 36.5 %collective-permute-start.4 = (bf16[1024,768]{1,0:T(8,128)(2,1)}, bf16[1024,768]{1,0:T(8,128)(2,1)}, u32[]{:S(2)}, u32[]{:S(2)}) collective-permute-start(bf16[1024,768]{1,0:T(8,128)(2,1)} %bitcast.1.x0.x_ref), channel_id=1, source_target_pairs={{0,1},{1,0},{2,3},{3,2},{4,5},{5,4},{6,7},{7,6},{8,9},{9,8},{10,11... | collective-permute-start | bytes 4718600 | tf_op jit(solution)/shard_map/ppermute | solution.py:32
  24.0 8.6 %collective-permute-start.3 = (bf16[2,2,32,1152]{3,2,0,1:T(8,128)(2,1)S(1)}, bf16[2,2,32,1152]{3,2,0,1:T(8,128)(2,1)S(1)}, u32[]{:S(2)}, u32[]{:S(2)}) collective-permute-start(bf16[2,2,32,1152]{3,2,0,1:T(8,128)(2,1)S(1)} %pad_maximum_fusion.8), channel_id=1, source_target_pairs={{0,4},{1,5},{2,6},{3,7},{4,0},{5,1},{6,2},{7,3},{8,12},{9,13},{10,... | collective-permute-start | bytes 884744 | tf_op jit(solution)/shard_map/ppermute | solution.py:32
  53.1 288.0 %reduce-scatter.3.cloned.1.call-start = ((), (), s32[]{:S(2)}) async-start(), calls=%async_computation.4 | async-start | bytes 6635520 | tf_op jit(solution)/shard_map/reduce_scatter | solution.py:980
  53.2 8.0 %collective-permute-start.6 = (bf16[2,2,32,1152]{3,2,0,1:T(8,128)(2,1)S(1)}, bf16[2,2,32,1152]{3,2,0,1:T(8,128)(2,1)S(1)}, u32[]{:S(2)}, u32[]{:S(2)}) collective-permute-start(bf16[2,2,32,1152]{3,2,0,1:T(8,128)(2,1)S(1)} %get-tuple-element.100), channel_id=1, source_target_pairs={{0,2},{1,3},{2,0},{3,1},{4,6},{5,7},{6,4},{7,5},{8,10},{9,11},{10,... | collective-permute-start | bytes 884744 | tf_op jit(solution)/shard_map/ppermute | solution.py:32
  54.8 7.6 %collective-permute-start.8 = (bf16[2,2,32,1152]{3,2,0,1:T(8,128)(2,1)S(1)}, bf16[2,2,32,1152]{3,2,0,1:T(8,128)(2,1)S(1)}, u32[]{:S(2)}, u32[]{:S(2)}) collective-permute-start(bf16[2,2,32,1152]{3,2,0,1:T(8,128)(2,1)S(1)} %get-tuple-element.99), channel_id=1, source_target_pairs={{0,1},{1,0},{2,3},{3,2},{4,5},{5,4},{6,7},{7,6},{8,9},{9,8},{10,11... | collective-permute-start | bytes 884744 | tf_op jit(solution)/shard_map/ppermute | solution.py:32
  62.6 15.5 %collective-permute-start.7 = (bf16[2,2,2,32,1152]{4,3,0,1,2:T(8,128)(2,1)S(1)}, bf16[2,2,2,32,1152]{4,3,0,1,2:T(8,128)(2,1)S(1)}, u32[]{:S(2)}, u32[]{:S(2)}) collective-permute-start(bf16[2,2,2,32,1152]{4,3,0,1,2:T(8,128)(2,1)S(1)} %pad_maximum_fusion.5), channel_id=1, source_target_pairs={{0,1},{1,0},{2,3},{3,2},{4,5},{5,4},{6,7},{7,6},{8,9},{9,8},{10,11... | collective-permute-start | bytes 1769480 | tf_op jit(solution)/shard_map/ppermute | solution.py:32
  64.2 14.6 %collective-permute-start.9 = (bf16[2,2,2,32,1152]{4,3,0,1,2:T(8,128)(2,1)S(1)}, bf16[2,2,2,32,1152]{4,3,0,1,2:T(8,128)(2,1)S(1)}, u32[]{:S(2)}, u32[]{:S(2)}) collective-permute-start(bf16[2,2,2,32,1152]{4,3,0,1,2:T(8,128)(2,1)S(1)} %pad_maximum_fusion.6), channel_id=1, source_target_pairs={{0,2},{1,3},{2,0},{3,1},{4,6},{5,7},{6,4},{7,5},{8,10},{9,11},{10,... | collective-permute-start | bytes 1769480 | tf_op jit(solution)/shard_map/ppermute | solution.py:32
  64.8 17.8 %collective-permute-start = (bf16[1024,768]{1,0:T(8,128)(2,1)}, bf16[1024,768]{1,0:T(8,128)(2,1)}, u32[]{:S(2)}, u32[]{:S(2)}) collective-permute-start(bf16[1024,768]{1,0:T(8,128)(2,1)} %bitcast.1.x0.x_ref), channel_id=1, source_target_pairs={{0,16},{16,0},{1,17},{17,1},{2,18},{18,2},{3,19},{19,3},{4,20},{20... | collective-permute-start | bytes 4718600 | tf_op jit(solution)/shard_map/ppermute | solution.py:32
  64.8 17.8 %collective-permute-start.5 = (bf16[1024,768]{1,0:T(8,128)(2,1)}, bf16[1024,768]{1,0:T(8,128)(2,1)}, u32[]{:S(2)}, u32[]{:S(2)}) collective-permute-start(bf16[1024,768]{1,0:T(8,128)(2,1)} %collective-permute-done.4.x2), channel_id=1, source_target_pairs={{0,16},{16,0},{1,17},{17,1},{2,18},{18,2},{3,19},{19,3},{4,20},{20... | collective-permute-start | bytes 4718600 | tf_op jit(solution)/shard_map/ppermute | solution.py:32
  141.8 2.3 collective-permute-start.10
  184.8 19.8 %copy-start.9 = (bf16[1024,384]{1,0:T(8,128)(2,1)S(1)}, bf16[1024,384]{1,0:T(8,128)(2,1)}, u32[]{:S(2)}) copy-start(bf16[1024,384]{1,0:T(8,128)(2,1)} %get-tuple-element.51) | copy-start | bytes 2359300
  184.8 26.6 %copy-start.5 = (bf16[1024,384]{1,0:T(8,128)(2,1)S(1)}, bf16[1024,384]{1,0:T(8,128)(2,1)}, u32[]{:S(2)}) copy-start(bf16[1024,384]{1,0:T(8,128)(2,1)} %get-tuple-element.50) | copy-start | bytes 2359300
  204.4 10.3 %collective-permute-start.16 = (bf16[4,4,9,24,768]{4,3,2,1,0:T(8,128)(2,1)}, bf16[4,4,9,24,768]{4,3,2,1,0:T(8,128)(2,1)}, u32[]{:S(2)}, u32[]{:S(2)}) collective-permute-start(bf16[4,4,9,24,768]{4,3,2,1,0:T(8,128)(2,1)} %get-tuple-element.68), channel_id=1, source_target_pairs={{0,16},{16,0},{1,17},{17,1},{2,18},{18,2},{3,19},{19,3},{4,20},{20... | collective-permute-start | bytes 15925256 | tf_op jit(solution)/shard_map/ppermute | solution.py:32
  204.6 6.8 %collective-permute-start.11 = (bf16[1024,384]{1,0:T(8,128)(2,1)S(1)}, bf16[1024,384]{1,0:T(8,128)(2,1)S(1)}, u32[]{:S(2)}, u32[]{:S(2)}) collective-permute-start(bf16[1024,384]{1,0:T(8,128)(2,1)S(1)} %copy-done.9), channel_id=1, source_target_pairs={{0,16},{16,0},{1,17},{17,1},{2,18},{18,2},{3,19},{19,3},{4,20},{20... | collective-permute-start | bytes 2359304 | tf_op jit(solution)/shard_map/ppermute | solution.py:32
  310.0 2.9 collective-permute-start.15
  314.9 83.6 %all-to-all-start = ((bf16[16,2,32,1152]{3,2,1,0:T(8,128)(2,1)}), bf16[16,2,32,1152]{3,2,1,0:T(8,128)(2,1)S(1)}, u32[]{:S(2)}, u32[]{:S(2)}) async-start(bf16[16,2,32,1152]{3,2,1,0:T(8,128)(2,1)} %copy.81), calls=%async_computation | async-start | bytes 4718592 | tf_op jit(solution)/shard_map/all_to_all | solution.py:1022
  318.6 82.7 %reduce-scatter.5.cloned.1.call-start = ((), (), s32[]{:S(2)}) async-start(), calls=%async_computation.5 | async-start | bytes 1658880 | tf_op jit(solution)/shard_map/reduce_scatter | solution.py:980
  325.8 10.5 %collective-permute-start.13 = (bf16[1024,768]{1,0:T(8,128)(2,1)}, bf16[1024,768]{1,0:T(8,128)(2,1)}, u32[]{:S(2)}, u32[]{:S(2)}) collective-permute-start(bf16[1024,768]{1,0:T(8,128)(2,1)} %get-tuple-element.59), channel_id=1, source_target_pairs={{0,16},{16,0},{1,17},{17,1},{2,18},{18,2},{3,19},{19,3},{4,20},{20... | collective-permute-start | bytes 4718600 | tf_op jit(solution)/shard_map/ppermute | solution.py:32
  336.0 5.1 %collective-permute-start.12 = (bf16[1024,768]{1,0:T(8,128)(2,1)}, bf16[1024,768]{1,0:T(8,128)(2,1)}, u32[]{:S(2)}, u32[]{:S(2)}) collective-permute-start(bf16[1024,768]{1,0:T(8,128)(2,1)} %get-tuple-element.57), channel_id=1, source_target_pairs={{0,16},{16,0},{1,17},{17,1},{2,18},{18,2},{3,19},{19,3},{4,20},{20... | collective-permute-start | bytes 4718600 | tf_op jit(solution)/shard_map/ppermute | solution.py:32
  339.3 54.3 %collective-permute-start.14 = (bf16[1024,768]{1,0:T(8,128)(2,1)}, bf16[1024,768]{1,0:T(8,128)(2,1)}, u32[]{:S(2)}, u32[]{:S(2)}) collective-permute-start(bf16[1024,768]{1,0:T(8,128)(2,1)} %add_convert_fusion.1), channel_id=1, source_target_pairs={{0,1},{1,0},{2,3},{3,2},{4,5},{5,4},{6,7},{7,6},{8,9},{9,8},{10,11... | collective-permute-start | bytes 4718600 | tf_op jit(solution)/shard_map/ppermute | solution.py:32
  (9 other events, 76.2 us)
Sparse Core Ops, SparseCore 0:
  53.2 88.3 all-gather.1
  222.5 59.7 reduce-scatter.2
  341.2 47.3 reduce-scatter.4

commit v3 on v2

--- a/solution.py
+++ b/solution.py
@@ -153,11 +153,11 @@
         finish(outs, peaks)
 
 
-def pair_specs(count, width):
+def pair_specs(count, width, skip=0):
     pairs = width // LANES
 
     def key_value(h, base):
-        return pl.BlockSpec((1, count, LANES), lambda p, i, sc: (sc[2 * p + h], 0, base * pairs + p))
+        return pl.BlockSpec((1, count, LANES), lambda p, i, sc: (sc[2 * (p + skip) + h], 0, base * pairs + p + skip))
 
     return [key_value(0, 1), key_value(1, 1), key_value(0, 2), key_value(1, 2)]
 
@@ -187,9 +187,7 @@
         ],
         compiler_params=pltpu.CompilerParams(vmem_limit_bytes=VMEM_BYTES),
         cost_estimate=pl.CostEstimate(
-            flops=4 * 4 * count * count * width,
-            bytes_accessed=2 * 6 * count * width,
-            transcendentals=heads * count * count,
+            flops=4 * 4 * count * count * width, bytes_accessed=2 * 6 * count * width, transcendentals=0
         ),
         name="attend",
     )(sc, qkv, qkv, qkv, qkv, qkv)
@@ -216,8 +214,9 @@
     *,
     heads,
     step,
+    skip,
 ):
-    pair = pl.program_id(0)
+    pair = pl.program_id(0) + skip
     block = pl.program_id(1)
     count = keys.shape[1]
     rows = q_ref.shape[1]
@@ -290,20 +289,20 @@
                 dkv_ref[half, 1, own_rows, :] = jnp.where(here, dv, 0.0).astype(BF16)
 
 
-def attend_back(sc, qkv, context, lse, grad_context, width):
+def attend_back(sc, qkv, context, lse, grad_context, width, skip, pairs):
     count = qkv.shape[1]
     rows = min(1024, count)
-    row_spec = pl.BlockSpec((rows, LANES), lambda p, i, sc: (i, p))
-    q_spec = pl.BlockSpec((1, rows, LANES), lambda p, i, sc: (0, i, p))
+    row_spec = pl.BlockSpec((rows, LANES), lambda p, i, sc: (i, p + skip))
+    q_spec = pl.BlockSpec((1, rows, LANES), lambda p, i, sc: (0, i, p + skip))
     dq_spec = pl.BlockSpec((LANES, rows), lambda p, i, sc: (p, i))
     dkv_spec = pl.BlockSpec((2, 2, LANES, count), lambda p, i, sc: (0, 0, p, 0))
     heads = width // HD
     return pl.pallas_call(
-        functools.partial(attend_back_kernel, heads=heads, step=min(512, count)),
+        functools.partial(attend_back_kernel, heads=heads, step=min(512, count), skip=skip),
         grid_spec=pltpu.PrefetchScalarGridSpec(
             num_scalar_prefetch=1,
-            grid=(width // LANES, count // rows),
-            in_specs=[q_spec] + pair_specs(count, width) + [row_spec, row_spec, row_spec],
+            grid=(pairs, count // rows),
+            in_specs=[q_spec] + pair_specs(count, width, skip) + [row_spec, row_spec, row_spec],
             out_specs=[dq_spec, dkv_spec, pl.BlockSpec((LANES, LANES), lambda p, i, sc: (p, 0))],
             scratch_shapes=[
                 pltpu.VMEM((2, count, LANES), BF16),
@@ -314,15 +313,13 @@
             ],
         ),
         out_shape=[
-            jax.ShapeDtypeStruct((width, count), BF16),
-            jax.ShapeDtypeStruct((2, 2, width, count), BF16),
-            jax.ShapeDtypeStruct((width, LANES), F32),
+            jax.ShapeDtypeStruct((pairs * LANES, count), BF16),
+            jax.ShapeDtypeStruct((2, 2, pairs * LANES, count), BF16),
+            jax.ShapeDtypeStruct((pairs * LANES, LANES), F32),
         ],
         compiler_params=pltpu.CompilerParams(vmem_limit_bytes=VMEM_BYTES),
         cost_estimate=pl.CostEstimate(
-            flops=10 * 4 * count * count * width,
-            bytes_accessed=2 * 12 * count * width,
-            transcendentals=heads * count * count,
+            flops=10 * 4 * count * count * pairs * LANES, bytes_accessed=2 * 12 * count * pairs * LANES, transcendentals=0
         ),
         name="attend_back",
     )(sc, qkv, qkv, qkv, qkv, qkv, context, lse, grad_context)
@@ -514,9 +511,7 @@
         ],
         compiler_params=pltpu.CompilerParams(vmem_limit_bytes=VMEM_BYTES),
         cost_estimate=pl.CostEstimate(
-            flops=2 * count * width * (4 * ff + 2 * width),
-            bytes_accessed=2 * (4 * width * ff + 2 * count * ff + 8 * count * width),
-            transcendentals=2 * count * ff,
+            flops=2 * count * width * (4 * ff + 2 * width), bytes_accessed=2 * (4 * width * ff + 2 * count * ff + 8 * count * width), transcendentals=0
         ),
         name="middle",
     )(core, x, own, other, cot, *([weights] * (3 + parts)), vec)
@@ -630,9 +625,7 @@
         out_shape=[shape, shape],
         compiler_params=pltpu.CompilerParams(vmem_limit_bytes=VMEM_BYTES),
         cost_estimate=pl.CostEstimate(
-            flops=2 * count * width * width * (2 * parts + 1),
-            bytes_accessed=2 * width * (2 * parts + 4) * (count + width),
-            transcendentals=0,
+            flops=2 * count * width * width * (2 * parts + 1), bytes_accessed=2 * width * (2 * parts + 4) * (count + width), transcendentals=0
         ),
         name="weight_grads",
     )(core, act, gb, low, gh, own, other, attn)
@@ -686,9 +679,14 @@
     )(*pieces, first, second, bias)
 
 
-def far_rows_kernel(dkv, weight, keep_ref, send_ref, *, group):
+def stacked(refs, which):
+    return jnp.concatenate([ref[0, kind] for kind in which for ref in refs], axis=0).T
+
+
+def far_rows_kernel(*refs, group):
+    *dkv, weight, keep_ref, send_ref = refs
     step = pl.program_id(0)
-    got = dot_nt(dkv[0].T, weight[:, group:]).astype(BF16)
+    got = dot_nt(stacked(dkv, (0, 1)), weight[:, group:]).astype(BF16)
 
     @pl.when(step < pl.num_programs(0) // 2)
     def _():
@@ -699,17 +697,19 @@
         send_ref[...] = got
 
 
+def dkv_spec(part, rows, source):
+    return pl.BlockSpec((1, 2, part.shape[2], rows), lambda i: (source, 0, 0, i))
+
+
 def far_rows(dkv, weight):
-    count, (width, wide) = dkv.shape[2], weight.shape
+    count, (width, wide) = dkv[0].shape[3], weight.shape
     rows = min(512, count // 2)
     blocks = count // rows
     return pl.pallas_call(
         functools.partial(far_rows_kernel, group=wide // 3),
         grid=(blocks,),
-        in_specs=[
-            pl.BlockSpec((1, dkv.shape[1], rows), lambda i: (1, 0, i)),
-            pl.BlockSpec((width, wide), lambda i: (0, 0), pipeline_mode=pl.Buffered(1)),
-        ],
+        in_specs=[dkv_spec(part, rows, 1) for part in dkv]
+        + [pl.BlockSpec((width, wide), lambda i: (0, 0), pipeline_mode=pl.Buffered(1))],
         out_specs=[
             pl.BlockSpec((rows, width), lambda i: (jnp.minimum(i, blocks // 2 - 1), 0)),
             pl.BlockSpec((rows, width), lambda i: (jnp.maximum(i - blocks // 2, 0), 0)),
@@ -717,15 +717,18 @@
         out_shape=[jax.ShapeDtypeStruct((count // 2, width), BF16)] * 2,
         compiler_params=pltpu.CompilerParams(vmem_limit_bytes=VMEM_BYTES),
         cost_estimate=pl.CostEstimate(
-            flops=2 * count * width * dkv.shape[1], bytes_accessed=8 * count * width, transcendentals=0
+            flops=2 * count * width * wide * 2 // 3, bytes_accessed=8 * count * width, transcendentals=0
         ),
         name="far_rows",
-    )(dkv, weight)
-
-
-def near_rows_kernel(dq, dkv, weight, resid, keep_ref, send_ref, *, group):
+    )(*dkv, weight)
+
+
+def near_rows_kernel(*refs, parts, group):
+    dq, dkv = refs[:parts], refs[parts : 2 * parts]
+    weight, resid, keep_ref, send_ref = refs[2 * parts :]
     step = pl.program_id(0)
-    got = dot_nt(dq[...].T, weight[:, :group]) + dot_nt(dkv[0].T, weight[:, group:])
+    queries = jnp.concatenate([ref[...] for ref in dq], axis=0).T
+    got = dot_nt(queries, weight[:, :group]) + dot_nt(stacked(dkv, (0, 1)), weight[:, group:])
 
     @pl.when(step < pl.num_programs(0) // 2)
     def _():
@@ -737,15 +740,15 @@
 
 
 def near_rows(dq, dkv, weight, resid):
-    count, (width, wide) = dkv.shape[2], weight.shape
+    count, (width, wide) = dkv[0].shape[3], weight.shape
     rows = min(512, count // 2)
     blocks = count // rows
     return pl.pallas_call(
-        functools.partial(near_rows_kernel, group=wide // 3),
+        functools.partial(near_rows_kernel, parts=len(dq), group=wide // 3),
         grid=(blocks,),
-        in_specs=[
-            pl.BlockSpec((dq.shape[0], rows), lambda i: (0, i)),
-            pl.BlockSpec((1, dkv.shape[1], rows), lambda i: (0, 0, i)),
+        in_specs=[pl.BlockSpec((part.shape[0], rows), lambda i: (0, i)) for part in dq]
+        + [dkv_spec(part, rows, 0) for part in dkv]
+        + [
             pl.BlockSpec((width, wide), lambda i: (0, 0), pipeline_mode=pl.Buffered(1)),
             pl.BlockSpec((rows, width), lambda i: (jnp.minimum(i, blocks // 2 - 1), 0)),
         ],
@@ -762,20 +765,31 @@
             flops=2 * count * width * wide, bytes_accessed=12 * count * width, transcendentals=0
         ),
         name="near_rows",
-    )(dq, dkv, weight, resid)
-
-
-def qkv_grads_kernel(core, dq, dkv, x0, x1, x2, x3, small, out_ref):
+    )(*dq, *dkv, weight, resid)
+
+
+def qkv_grads_kernel(core, dq, dkv, x0, x1, x2, x3, *refs):
+    *small, keep_ref, send_ref = refs
     step = pl.program_id(0)
-    blocks, unit = out_ref.shape[1], x0.shape[1] // (2 * out_ref.shape[1])
+    inner, outer = keep_ref.shape[:2]
+    unit = x0.shape[1] // (2 * inner * outer)
     local = x0.shape[0]
 
     def put(value):
         value = value.T.astype(BF16)
         half = value.shape[0] // 2
         for h in (0, 1):
-            place_at = (core[0] + h) % 2
-            out_ref[place_at, :, :unit, :] = value[h * half : (h + 1) * half].reshape(blocks, unit, -1)
+            part = value[h * half : (h + 1) * half].reshape(outer, inner, unit, -1)
+
+            @pl.when(core[0] == h)
+            def _():
+                for o in range(outer):
+                    keep_ref[:, o, :unit, :] = part[o]
+
+            @pl.when(core[0] != h)
+            def _():
+                for o in range(outer):
+                    send_ref[:, o, :unit, :] = part[o]
 
     @pl.when(step == 0)
     def _():
@@ -791,16 +805,19 @@
             + dot(far[:, local:], x3[...])
         )
 
-    out_ref[:, :, unit:, :] = small[...]
-
-
-def qkv_grads(core, dq, dkv, pieces, small):
+    for extra in small:
+        keep_ref[:, :, unit:, :] = extra[0]
+        send_ref[:, :, unit:, :] = extra[1]
+
+
+def qkv_grads(core, dq, dkv, pieces, inner, outer, *small):
     count, width = pieces[0].shape
     group, full = dq.shape
-    blocks, extra = small.shape[1:3]
-    unit = width // (2 * blocks)
+    extra = sum(part.shape[3] for part in small)
+    unit = width // (2 * inner * outer)
     once = pl.Buffered(1)
     whole = pl.BlockSpec((count, width), lambda t, core: (0, 0), pipeline_mode=once)
+    out_spec = pl.BlockSpec((inner, outer, unit + extra, group), lambda t, core: (0, 0, 0, t))
     return pl.pallas_call(
         qkv_grads_kernel,
         grid_spec=pltpu.PrefetchScalarGridSpec(
@@ -813,21 +830,70 @@
                 whole,
                 whole,
                 whole,
-                pl.BlockSpec((2, blocks, extra, group), lambda t, core: (0, 0, 0, t)),
+                *[pl.BlockSpec((2, inner, outer, extra, group), lambda t, core: (0, 0, 0, 0, t)) for _ in small],
             ],
-            out_specs=pl.BlockSpec((2, blocks, unit + extra, group), lambda t, core: (0, 0, 0, t)),
-        ),
-        out_shape=jax.ShapeDtypeStruct((2, blocks, unit + extra, 3 * group), BF16),
+            out_specs=[out_spec, out_spec],
+        ),
+        out_shape=[jax.ShapeDtypeStruct((inner, outer, unit + extra, 3 * group), BF16)] * 2,
         compiler_params=pltpu.CompilerParams(vmem_limit_bytes=VMEM_BYTES),
         cost_estimate=pl.CostEstimate(
-            flops=10 * full * width * group, bytes_accessed=16 * full * width, transcendentals=0
+            flops=10 * full * width * group, bytes_accessed=8 * full * width + 20 * full * group, transcendentals=0
         ),
         name="qkv_grads",
-    )(core, dq, dkv, *pieces, small)
+    )(core, dq, dkv, *pieces, *small)
+
+
+def unpack_kernel(core, chip, moved, back_ref, in_ref, out_ref, qkv_ref, vec_ref, *, rows, parts):
+    width = chip.shape[1]
+    at = lambda slot, count=1: chip[slot * rows : (slot + count) * rows, :].astype(F32)
+    back_ref[...] = at(0, parts)
+    for j in range(parts):
+        in_ref[:, j * width : (j + 1) * width] = at(parts + j)
+    out_ref[...] = at(2 * parts)
+    total = jnp.sum(moved[...].astype(F32), axis=0)
+    vec_ref[...] = total[rows : rows + 8]
+    half = total.shape[1] // 2
+    firsts = at(2 * parts + 1), at(2 * parts + 2)
+    seconds = total[:rows, :half], total[:rows, half:]
+    wide, narrow = width // 3, half // 3
+    for h in (0, 1):
+        own = core[0] == h
+        first = jnp.where(own, *firsts)
+        second = jnp.where(own, *seconds)
+        for t in range(3):
+            start = (2 * t + h) * (wide + narrow)
+            qkv_ref[:, start : start + wide] = first[:, t * wide : (t + 1) * wide]
+            qkv_ref[:, start + wide : start + wide + narrow] = second[:, t * narrow : (t + 1) * narrow]
+
+
+def unpack(core, chip, moved, rows, parts):
+    width = chip.shape[1]
+    whole = lambda a: pl.BlockSpec(a.shape, lambda i, core: (0,) * len(a.shape))
+    outs = [
+        jax.ShapeDtypeStruct(shape, F32)
+        for shape in (
+            (parts * rows, width),
+            (rows, parts * width),
+            (rows, width),
+            (rows, 3 * width),
+            (8, moved.shape[2]),
+        )
+    ]
+    return pl.pallas_call(
+        functools.partial(unpack_kernel, rows=rows, parts=parts),
+        grid_spec=pltpu.PrefetchScalarGridSpec(
+            num_scalar_prefetch=1,
+            grid=(1,),
+            in_specs=[whole(chip), whole(moved)],
+            out_specs=[whole(a) for a in outs],
+        ),
+        out_shape=outs,
+        name="unpack",
+    )(core, chip, moved)
 
 
 GATE = 4
-ORDER = 0
+SHARES = (20,)
 
 
 def unpacked(blocks, parts):
@@ -972,65 +1038,119 @@
 
     keep, send = weight_grads(at_core, act, gb, low, gh, context[:local], other, attn, inner, outer)
     chip = (keep.astype(F32) + swap(send, "head", 1).astype(F32)).astype(BF16)
+    grad_context, chip = lax.optimization_barrier((grad_context, chip))
+    near_groups = [[o * inner + i for i in range(inner)] for o in range(outer)]
+    far_groups = [[o * inner + i for o in range(outer)] for i in range(inner)]
+
+    def over_plane(value):
+        flat = value.reshape(-1, value.shape[3])
+        flat = lax.psum_scatter(flat, "blk", scatter_dimension=0, axis_index_groups=near_groups, tiled=True)
+        return flat.reshape(value.shape[1:])
+
+    def over_column(value):
+        flat = value.reshape(-1, value.shape[2])
+        return lax.psum_scatter(flat, "blk", scatter_dimension=0, axis_index_groups=far_groups, tiled=True)
+
     if direct:
-        chip = chip.reshape(inner * outer * (2 * parts + 1) * rows, width)
-        near = [[o * inner + i for i in range(inner)] for o in range(outer)]
-        far = [[o * inner + i for o in range(outer)] for i in range(inner)]
-        for groups in (near, far):
-            chip = lax.psum_scatter(chip, "blk", scatter_dimension=0, axis_index_groups=groups, tiled=True)
+        chip = over_plane(chip.reshape(inner, outer, (2 * parts + 1) * rows, width))
     else:
         chip = chip.transpose(1, 0, 2, 3, 4).reshape(inner * outer, -1, width)
         chip = packed(*unpacked(chip, parts), blocks)
         chip = lax.psum_scatter(chip, "blk", scatter_dimension=0, tiled=True)[0]
-    sum_wback = chip[: parts * rows].astype(F32)
-    sum_win = chip[parts * rows : 2 * parts * rows].astype(F32)
-    sum_win = sum_win.reshape(parts, rows, width).transpose(1, 0, 2).reshape(rows, ff)
-    sum_wout = chip[2 * parts * rows :].astype(F32)
-
-    dq, dkv, dq_sum = attend_back(sc, qkv, context, lse, grad_context, group)
-    joint = dkv.reshape(2, 2 * group, half)
-
-    at_group = lambda v: lax.dynamic_update_slice_in_dim(jnp.zeros((width,), F32), v, core * group, 0)
-    grad_small = [
-        at_group(jnp.sum(dq_sum, axis=1)),
-        place(sums[2, 2 * width : 2 * width + group], sums[2, 2 * width + group : 3 * width], core == 1, 0).reshape(-1),
-        sums[1, :width],
-        sums[1, width : 2 * width],
-        sums[1, 2 * width : 3 * width],
-        sums[1, 3 * width : 4 * width],
-        sums[2, :width],
-        sums[2, width : 2 * width],
-    ]
-    grad_small = jnp.concatenate(
-        [jnp.stack(grad_small, 0).reshape(8, cores, blocks, rows).transpose(1, 2, 0, 3).reshape(cores, blocks, -1)]
-        + [sums[0].reshape(cores, blocks, parts * rows)],
-        axis=2,
-    )
-    small_size = grad_small.shape[2]
-    grad_small = jnp.pad(grad_small, ((0, 0), (0, 0), (0, 3 * group - small_size)))
+
+    v_sums = place(
+        sums[2, 2 * width : 2 * width + group], sums[2, 2 * width + group : 3 * width], core == 1, 0
+    ).reshape(-1)
+    by_rows = [v_sums] + [sums[1, s * width : (s + 1) * width] for s in range(4)]
+    by_rows = jnp.stack(by_rows + [sums[2, s * width : (s + 1) * width] for s in range(2)], axis=0)
+    by_rows = by_rows.reshape(7, cores, blocks, rows).transpose(1, 2, 0, 3).reshape(cores, blocks, -1)
+    early_small = jnp.concatenate([by_rows, sums[0].reshape(cores, blocks, parts * rows)], axis=2)
+    early_small, grad_context = lax.optimization_barrier((early_small, grad_context))
+
+    def part_rows(dq, dkv, *small_rows):
+        columns = 3 * dq.shape[0]
+        keep, send = qkv_grads(at_core, dq, dkv, pieces, inner, outer, *(small_rows if direct else ()))
+        if not direct:
+            keep, send = (
+                jnp.concatenate(
+                    [a.transpose(1, 0, 2, 3).reshape(blocks, rows, columns)]
+                    + [b[i].transpose(1, 0, 2, 3).reshape(blocks, -1, columns) for b in small_rows],
+                    axis=1,
+                )
+                for i, a in enumerate((keep, send))
+            )
+        return keep, swap(send, "head", 1)
+
+    def finish_part(keep, came):
+        both_cores = jnp.concatenate([keep, came], axis=-1)
+        if direct:
+            both_cores = both_cores.transpose(1, 0, 2, 3).reshape((blocks,) + both_cores.shape[2:])
+        return lax.all_to_all(both_cores, "blk", 0, 0, tiled=True)
+
+    def total_of(moved):
+        return jnp.sum(moved.astype(F32), axis=0).reshape(moved.shape[1], 2, -1)
+
+    pairs = group // LANES
+    first_pairs = pairs - pairs // 3
+    dq_a, dkv_a, sum_a = attend_back(sc, qkv, context, lse, grad_context, group, 0, first_pairs)
+    keep_a, came_a = part_rows(dq_a, dkv_a)
+    if direct:
+        part_a = jnp.concatenate([keep_a, came_a], axis=2)
+        grad_context, part_a, chip = lax.optimization_barrier((grad_context, part_a, chip))
+        chip = over_column(jnp.concatenate([chip, over_plane(part_a)], axis=1))
+    else:
+        total_a = total_of(finish_part(keep_a, came_a))
+    dq_b, dkv_b, sum_b = attend_back(
+        sc, qkv, context, lse, grad_context, group, first_pairs, pairs - first_pairs
+    )
+
+    q_sums = jnp.sum(jnp.concatenate([sum_a, sum_b], axis=0), axis=1)
+    q_sums = lax.dynamic_update_slice_in_dim(jnp.zeros((width,), F32), q_sums, core * group, 0)
+    grad_small = jnp.concatenate([q_sums.reshape(cores, blocks, rows), early_small], axis=2)
+    room = 3 * (pairs - first_pairs) * LANES
+    grad_small = jnp.pad(grad_small, ((0, 0), (0, 0), (0, room - grad_small.shape[2])))
     high = grad_small.astype(BF16)
     low_part = (grad_small - high.astype(F32)).astype(BF16)
     small_rows = jnp.pad(jnp.stack([high, low_part], axis=2), ((0, 0), (0, 0), (0, 6), (0, 0)))
     small_rows = jnp.where(core == 0, small_rows, small_rows[::-1])
+    small_rows = small_rows.reshape(2, blocks // inner, inner, 8, room).transpose(0, 2, 1, 3, 4)
+
+    dkv = (dkv_a, dkv_b)
+    keep_far, send_far = far_rows(dkv, weight)
+    far_sib = swap(send_far, "head", 1)
+    cuts = [0, *(local * share // 32 for share in SHARES), local]
+    far_sums = [
+        (keep_far[lo:hi].astype(F32) + far_sib[lo:hi].astype(F32)).astype(BF16)
+        for lo, hi in zip(cuts, cuts[1:])
+    ]
+    far_sums, dq_b = lax.optimization_barrier((far_sums, dq_b))
+    far_in = [swap(part, "blk", 1) for part in far_sums]
+    keep_b, came_b = part_rows(dq_b, dkv_b, small_rows)
+    far_in[0], came_b = lax.optimization_barrier((far_in[0], came_b))
+    moved_b = finish_part(keep_b, came_b)
+    came_b, dq_a = lax.optimization_barrier((came_b, dq_a))
+    keep_near, send_near = near_rows((dq_a, dq_b), dkv, weight, grad_resid1)
+    chip, send_near = lax.optimization_barrier((chip, send_near))
+    near_sib = swap(send_near, "head", 1)
+    grad_tokens = keep_near + near_sib.astype(F32) + jnp.concatenate(far_in, axis=0).astype(F32)
+
     if direct:
-        outgoing = qkv_grads(at_core, dq, dkv, pieces, small_rows)
+        sum_wback, sum_win, sum_wout, sum_wqkv, vectors = unpack(at_core, chip, moved_b, rows, parts)
+        vectors = vectors[0] + vectors[1]
+        vectors = vectors[: vectors.shape[0] // 2] + vectors[vectors.shape[0] // 2 :]
     else:
-        none = jnp.zeros((2, 16, 8, 3 * group), BF16)
-        outgoing = qkv_grads(at_core, dq, dkv, pieces, none)[:, :, : width // 32]
-        outgoing = jnp.concatenate([outgoing.reshape(2, blocks, rows, 3 * group), small_rows], axis=2)
-    keep, came = outgoing[0], swap(outgoing[1], "head", 1)
-    exchanged = lax.all_to_all(jnp.stack([keep, came], axis=1), "blk", 0, 0, tiled=True).astype(F32)
-    keep_far, send_far = far_rows(joint, weight)
-    far_sib = swap(send_far, "head", 1)
-    far_in = swap((keep_far.astype(F32) + far_sib.astype(F32)).astype(BF16), "blk", 1)
-    keep_near, send_near = near_rows(dq, joint, weight, grad_resid1)
-    near_sib = swap(send_near, "head", 1)
-    grad_tokens = keep_near + near_sib.astype(F32) + far_in.astype(F32)
-
-    total = jnp.sum(exchanged, axis=0)
-    own_w, other_w = (total[s, :rows].reshape(rows, 3, group) for s in (0, 1))
-    sum_wqkv = place(own_w, other_w, core == 1, 2).reshape(rows, 3 * width)
-    vectors = total[0, rows] + total[0, rows + 1] + total[1, rows] + total[1, rows + 1]
+        total_b = total_of(moved_b)
+        sum_wback = chip[: parts * rows].astype(F32)
+        sum_win = chip[parts * rows : 2 * parts * rows].astype(F32)
+        sum_win = sum_win.reshape(parts, rows, width).transpose(1, 0, 2).reshape(rows, ff)
+        sum_wout = chip[2 * parts * rows : (2 * parts + 1) * rows].astype(F32)
+
+        def columns_of(total):
+            own_w, other_w = (total[:rows, s].reshape(rows, 3, -1) for s in (0, 1))
+            return place(own_w, other_w, core == 1, 2)
+
+        sum_wqkv = jnp.concatenate([columns_of(total_a), columns_of(total_b)], axis=3).reshape(rows, 3 * width)
+        vectors = jnp.sum(total_b[rows : rows + 2], axis=(0, 1))
 
     def summed(slot, size=rows):
         return vectors[slot * rows : slot * rows + size]

time: 418 us -> 403 us (0.964)
  waiting for transfers between devices: 113 us -> 89.3 us
  Pallas kernels: 216 us -> 225 us
    ppermute x17 -> x19, waiting for transfers between devices: 113 us -> 81.3 us  [swap(): return lax.ppermute(value, axis, pairs)]
    all_to_all x1, waiting for transfers between devices: 0.01 us -> 7.88 us  [finish_part(): return lax.all_to_all(both_cores, 'blk', 0, 0, tiled=True)]
    convert_element_type x3 -> x2, other arithmetic: 6.08 us -> 1.18 us  [per_device(): (keep_far[lo:hi].astype(F32) + far_sib[lo:hi].astype(F32)).astype(BF16)]
    pallas_call x1 -> x2, Pallas kernels: 12.4 us -> 17.2 us  [qkv_grads(): pl.pallas_call(qkv_grads_kernel, grid_spec=pltpu.PrefetchScalarGridSpec(n...]
    concatenate x0 -> x3, other arithmetic: none -> 4.53 us  [the longest x1 2.28 us: per_device(): chip = over_column(jnp.concatenate([chip, over_plane(part_a)], axis=1))]
    pallas_call x1 -> x2, Pallas kernels: 70.2 us -> 74.7 us  [attend_back(): pl.pallas_call(functools.partial(attend_back_kernel, heads=heads, step=mi...]
    pallas_call x1 -> x2, Pallas kernels: 9.97 us -> 12.2 us  [the longest x1 10 us: near_rows(): pl.pallas_call(functools.partial(near_rows_kernel, parts=len(dq), group=w...]
    ppermute x17 -> x19, starting transfers between devices: 15.6 us -> 15.4 us  [swap(): return lax.ppermute(value, axis, pairs)]
  transfers between devices with their start and end apart: 21 -> 24, of which waited for: 13 -> 17; matrix products, arithmetic and copies ran while one was open for 7% -> 7% of each run, Pallas kernels for 38% -> 42%
where the time goes in v3:
time: 403 us; the launch traced here: 396 us
  Pallas kernels  225 us (56%)
  waiting for transfers between devices  89.3 us (22%)
  other arithmetic  28.4 us (7%)
  starting transfers between devices  19.2 us (5%)
  local copies, waits for them, and re-layouts  18.3 us (5%)
  between operations  16.1 us (4%)
    ppermute x19, waiting for transfers between devices, swap(): return lax.ppermute(value, axis, pairs)  81.3 us
    pallas_call x2, Pallas kernels, attend_back(): pl.pallas_call(functools.partial(attend_back_kernel, heads=heads, step=mi...  74.7 us
    pallas_call x1, Pallas kernels, middle(): pl.pallas_call(functools.partial(middle_kernel, width=width, ff=ff), grid...  40 us
    pallas_call x1, Pallas kernels, attend(): pl.pallas_call(functools.partial(attend_kernel, heads=heads, step=min(512...  39.3 us
    pallas_call x1, Pallas kernels, weight_grads(): pl.pallas_call(functools.partial(weight_grads_kernel, parts=parts), grid_...  19.8 us
    pallas_call x2, Pallas kernels, qkv_grads(): pl.pallas_call(qkv_grads_kernel, grid_spec=pltpu.PrefetchScalarGridSpec(n...  17.2 us
    ppermute x19, starting transfers between devices, swap(): return lax.ppermute(value, axis, pairs)  15.4 us
    pallas_call x1, Pallas kernels, project(): pl.pallas_call(functools.partial(project_kernel, group=wide // 3), grid=(...  14.4 us
  transfers between devices with their start and end apart: 24, of which 17 were waited for; matrix products, arithmetic and copies ran while one was open for 7% of the time, Pallas kernels for 42%

profile of v3, /device:TPU:0, one launch (start us, length us, event | category | flops | bytes accessed | tf_op | source)
XLA Modules:
  0.0 396.2 jit_solution(10510960739698506846)
XLA Ops:
  12.6 4.0 %collective-permute-start.2 = (bf16[2,32,1152]{2,1,0:T(8,128)(2,1)S(1)}, bf16[2,32,1152]{2,1,0:T(8,128)(2,1)S(1)}, u32[]{:S(2)}, u32[]{:S(2)}) collective-permute-start(bf16[2,32,1152]{2,1,0:T(8,128)(2,1)S(1)} %pad_maximum_fusion.10), channel_id=1, source_target_pairs={{0,8},{1,9},{2,10},{3,11},{4,12},{5,13},{6,14},{7,15},{8,0},{9,1},... | collective-permute-start | bytes 442376 | tf_op jit(solution)/shard_map/ppermute | solution.py:32
  18.1 5.8 %collective-permute-done.2 = bf16[2,32,1152]{2,1,0:T(8,128)(2,1)S(1)} collective-permute-done((bf16[2,32,1152]{2,1,0:T(8,128)(2,1)S(1)}, bf16[2,32,1152]{2,1,0:T(8,128)(2,1)S(1)}, u32[]{:S(2)}, u32[]{:S(2)}) %collective-permute-start.2) | collective-permute-done | bytes 147488 | tf_op jit(solution)/shard_map/ppermute | solution.py:32
  25.6 7.0 %collective-permute-done.3 = bf16[2,2,32,1152]{3,2,0,1:T(8,128)(2,1)S(1)} collective-permute-done((bf16[2,2,32,1152]{3,2,0,1:T(8,128)(2,1)S(1)}, bf16[2,2,32,1152]{3,2,0,1:T(8,128)(2,1)S(1)}, u32[]{:S(2)}, u32[]{:S(2)}) %collective-permute-start.3) | collective-permute-done | bytes 294944 | tf_op jit(solution)/shard_map/ppermute | solution.py:32
  32.8 20.1 %collective-permute-done.4.x2 = bf16[1024,768]{1,0:T(8,128)(2,1)} collective-permute-done((bf16[1024,768]{1,0:T(8,128)(2,1)S(1)}, bf16[1024,768]{1,0:T(8,128)(2,1)}, u32[]{:S(2)}, u32[]{:S(2)}) %collective-permute-start.4) | collective-permute-done | bytes 1572896 | tf_op jit(solution)/shard_map/ppermute | solution.py:32
  56.1 5.0 %collective-permute-done.6 = bf16[2,2,32,1152]{3,2,0,1:T(8,128)(2,1)} collective-permute-done((bf16[2,2,32,1152]{3,2,0,1:T(8,128)(2,1)S(1)}, bf16[2,2,32,1152]{3,2,0,1:T(8,128)(2,1)}, u32[]{:S(2)}, u32[]{:S(2)}) %collective-permute-start.6) | collective-permute-done | bytes 294944 | tf_op jit(solution)/shard_map/ppermute | solution.py:32
  70.5 8.1 %collective-permute-done.7 = bf16[2,2,2,32,1152]{4,3,0,1,2:T(8,128)(2,1)S(1)} collective-permute-done((bf16[2,2,2,32,1152]{4,3,0,1,2:T(8,128)(2,1)}, bf16[2,2,2,32,1152]{4,3,0,1,2:T(8,128)(2,1)S(1)}, u32[]{:S(2)}, u32[]{:S(2)}) %collective-permute-start.7) | collective-permute-done | bytes 589856 | tf_op jit(solution)/shard_map/ppermute | solution.py:32
  85.8 14.4 %project.1 = (bf16[2,2048,1152]{2,1,0:T(8,128)(2,1)}, bf16[768,1152]{1,0:T(8,128)(2,1)}) custom-call(bf16[1024,768]{1,0:T(8,128)(2,1)} %bitcast.121, bf16[1024,768]{1,0:T(8,128)(2,1)} %collective-permute-done.x1, bf16[1024,768]{1,0:T(8,128)(2,1)} %collective-permute-done.4.x2, bf16[1024,768]{1,0:T(8,128)(2,1)} %collective-permute-done.5.x3, ...), custom_call_target="tpu_custom_call" | custom-call | flops 7247757312 | bytes 15728640 | tf_op jit(solution)/shard_map/project/pallas_call | solution.py:662
  100.2 39.3 %attend.1 = (bf16[2048,384]{1,0:T(8,128)(2,1)}, f32[2048,384]{1,0:T(8,128)}) custom-call(s32[10]{0:T(128)} %concatenate.57.sc, bf16[2,2048,1152]{2,1,0:T(8,128)(2,1)} %get-tuple-element.72.q_ref.ka_ref.kb_ref.va_ref.vb_ref, bf16[2,2048,1152]{2,1,0:T(8,128)(2,1)} %get-tuple-element.72.q_ref.ka_ref.kb_ref.va_ref.vb_ref, ...), custom_call_target="tpu_custom_call" | custom-call | flops 25769803776 | bytes 9437184 | tf_op jit(solution)/shard_map/attend/pallas_call | solution.py:171
  139.5 2.4 fusion.31
  145.2 40.0 %middle.1 = (bf16[1024,768]{1,0:T(8,128)(2,1)}, f32[1024,768]{1,0:T(8,128)}, bf16[1024,384]{1,0:T(8,128)(2,1)}, bf16[1024,384]{1,0:T(8,128)(2,1)}, bf16[1024,768...) custom-call(s32[1]{0:T(128)} %bitcast.core, ...), custom_call_target="tpu_custom_call" | custom-call | flops 21743271936 | bytes 44040192 | tf_op jit(solution)/shard_map/middle/pallas_call | solution.py:464
  185.2 19.8 %weight_grads.1 = (bf16[4,4,9,24,768]{4,3,2,1,0:T(8,128)(2,1)}, bf16[4,4,9,24,768]{4,3,2,1,0:T(8,128)(2,1)}) custom-call(s32[1]{0:T(128)} %bitcast.core, bf16[1024,3072]{1,0:T(8,128)(2,1)} %get-tuple-element.80.act, bf16[1024,768]{1,0:T(8,128)(2,1)} %get-tuple-element.81.gb, bf16[1024,768]{1,0:T(8,128)(2,1)} %get-tuple-element.82.low, ...), custom_call_target="tpu_custom_call" | custom-call | flops 10871635968 | bytes 33030144 | tf_op jit(solution)/shard_map/weight_grads/pallas_call | solution.py:604
  205.6 6.5 %collective-permute-done.11 = bf16[1024,384]{1,0:T(8,128)(2,1)S(1)} collective-permute-done((bf16[1024,384]{1,0:T(8,128)(2,1)S(1)}, bf16[1024,384]{1,0:T(8,128)(2,1)S(1)}, u32[]{:S(2)}, u32[]{:S(2)}) %collective-permute-start.11) | collective-permute-done | bytes 786464 | tf_op jit(solution)/shard_map/ppermute | solution.py:32
  215.2 6.1 %add_convert_fusion = bf16[4,4,9,24,768]{4,3,2,1,0:T(8,128)(2,1)} fusion(bf16[4,4,9,24,768]{4,3,2,1,0:T(8,128)(2,1)S(1)} %collective-permute-done.12, bf16[4,4,9,24,768]{4,3,2,1,0:T(8,128)(2,1)} %get-tuple-element.85), kind=kLoop, calls=%fused_computation | loop fusion | flops 10616832 | bytes 15925248 | tf_op jit(solution)/shard_map/convert_element_type | solution.py:1040
  225.0 48.8 %attend_back.2 = (bf16[256,2048]{1,0:T(8,128)(2,1)}, bf16[2,2,256,2048]{3,2,1,0:T(8,128)(2,1)}, f32[256,128]{1,0:T(8,128)}) custom-call(s32[10]{0:T(128)} %concatenate.57.sc, bf16[2,2048,1152]{2,1,0:T(8,128)(2,1)} %get-tuple-element.72.q_ref.ka_ref.kb_ref.va_ref.vb_ref, bf16[2,2048,1152]{2,1,0:T(8,128)(2,1)} %get-tuple-element.72.q_ref.ka_ref.kb_ref.va_ref.vb_ref, ...), custom_call_target="tpu_custom_call" | custom-call | flops 42949672960 | bytes 12582912 | tf_op jit(solution)/shard_map/attend_back/pallas_call | solution.py:300
  273.7 9.9 %qkv_grads.2 = (bf16[4,4,24,768]{3,2,1,0:T(8,128)(2,1)}, bf16[4,4,24,768]{3,2,1,0:T(8,128)(2,1)}) custom-call(s32[1]{0:T(128)} %bitcast.core, bf16[256,2048]{1,0:T(8,128)(2,1)} %get-tuple-element.107.dq.refs_0_, bf16[2,2,256,2048]{3,2,1,0:T(8,128)(2,1)} %get-tuple-element.89.dkv.refs_0_.refs_2_, bf16[1024,768]{1,0:T(8,128)(2,1)} %bitcast.123, ...), custom_call_target="tpu_custom_call" | custom-call | flops 4026531840 | bytes 23068672 | tf_op jit(solution)/shard_map/qkv_grads/pallas_call | solution.py:821
  288.1 25.9 %attend_back.3 = (bf16[128,2048]{1,0:T(8,128)(2,1)}, bf16[2,2,128,2048]{3,2,1,0:T(8,128)(2,1)}, f32[128,128]{1,0:T(8,128)}) custom-call(s32[10]{0:T(128)} %concatenate.57.sc, bf16[2,2048,1152]{2,1,0:T(8,128)(2,1)} %get-tuple-element.72.q_ref.ka_ref.kb_ref.va_ref.vb_ref, bf16[2,2048,1152]{2,1,0:T(8,128)(2,1)} %get-tuple-element.72.q_ref.ka_ref.kb_ref.va_ref.vb_ref, ...), custom_call_target="tpu_custom_call" | custom-call | flops 21474836480 | bytes 6291456 | tf_op jit(solution)/shard_map/attend_back/pallas_call | solution.py:300
  314.1 7.3 %far_rows.1 = (bf16[1024,768]{1,0:T(8,128)(2,1)}, bf16[1024,768]{1,0:T(8,128)(2,1)}) custom-call(bf16[2,2,256,2048]{3,2,1,0:T(8,128)(2,1)} %get-tuple-element.89.dkv.refs_0_.refs_2_, bf16[2,2,128,2048]{3,2,1,0:T(8,128)(2,1)} %get-tuple-element.95.refs_1_.dkv.refs_3_, bf16[768,1152]{1,0:T(8,128)(2,1)} %get-tuple-element.96.refs_2_.refs_4_), custom_call_target="tpu_custom_call" | custom-call | flops 2415919104 | bytes 12582912 | tf_op jit(solution)/shard_map/far_rows/pallas_call | solution.py:708
  327.3 7.3 %qkv_grads.3 = (bf16[4,4,32,384]{3,2,1,0:T(8,128)(2,1)}, bf16[4,4,32,384]{3,2,1,0:T(8,128)(2,1)}) custom-call(s32[1]{0:T(128)} %bitcast.core, bf16[128,2048]{1,0:T(8,128)(2,1)} %get-tuple-element.101.dq.refs_1_, bf16[2,2,128,2048]{3,2,1,0:T(8,128)(2,1)} %get-tuple-element.95.refs_1_.dkv.refs_3_, bf16[1024,768]{1,0:T(8,128)(2,1)} %bitcast.124, ...), custom_call_target="tpu_custom_call" | custom-call | flops 2013265920 | bytes 17825792 | tf_op jit(solution)/shard_map/qkv_grads/pallas_call | solution.py:821
  336.6 13.8 %collective-permute-done.15 = bf16[640,768]{1,0:T(8,128)(2,1)S(1)} collective-permute-done((bf16[640,768]{1,0:T(8,128)(2,1)S(1)}, bf16[640,768]{1,0:T(8,128)(2,1)S(1)}, u32[]{:S(2)}, u32[]{:S(2)}) %collective-permute-start.15) | collective-permute-done | bytes 983072 | tf_op jit(solution)/shard_map/ppermute | solution.py:32
  352.5 3.6 all-to-all-start
  356.2 10.0 %near_rows.1 = (f32[1024,768]{1,0:T(8,128)}, bf16[1024,768]{1,0:T(8,128)(2,1)}) custom-call(bf16[256,2048]{1,0:T(8,128)(2,1)} %get-tuple-element.107.dq.refs_0_, bf16[128,2048]{1,0:T(8,128)(2,1)} %get-tuple-element.101.dq.refs_1_, bf16[2,2,256,2048]{3,2,1,0:T(8,128)(2,1)} %get-tuple-element.89.dkv.refs_0_.refs_2_, ...), custom_call_target="tpu_custom_call" | custom-call | flops 3623878656 | bytes 18874368 | tf_op jit(solution)/shard_map/near_rows/pallas_call | solution.py:746
  368.1 7.9 %all-to-all-done.moved = bf16[16,32,768]{2,1,0:T(8,128)(2,1)S(1)} async-done(((bf16[16,32,768]{2,1,0:T(8,128)(2,1)}), bf16[16,32,768]{2,1,0:T(8,128)(2,1)S(1)}, u32[]{:S(2)}, u32[]{:S(2)}) %all-to-all-start) | async-done | bytes 786464 | tf_op jit(solution)/shard_map/all_to_all | solution.py:1088
  381.1 4.1 %collective-permute-done.18 = bf16[384,768]{1,0:T(8,128)(2,1)} collective-permute-done((bf16[384,768]{1,0:T(8,128)(2,1)}, bf16[384,768]{1,0:T(8,128)(2,1)}, u32[]{:S(2)}, u32[]{:S(2)}) %collective-permute-start.18) | collective-permute-done | bytes 589856 | tf_op jit(solution)/shard_map/ppermute | solution.py:32
  385.1 4.1 %add_bitcast_fusion = f32[1,1024,768]{2,1,0:T(8,128)} fusion(f32[1024,768]{1,0:T(8,128)} %get-tuple-element.109, bf16[1024,768]{1,0:T(8,128)(2,1)S(1)} %collective-permute-done.17, bf16[384,768]{1,0:T(8,128)(2,1)} %collective-permute-done.18, bf16[640,768]{1,0:T(8,128)(2,1)S(1)} %collective-permute-done.15), kind=kLoop, calls=%fused_computation.1 | loop fusion | flops 5505024 | bytes 9437184 | tf_op jit(solution)/shard_map/broadcast_in_dim | solution.py:1160
  (163 shorter events, 58.8 us)
Async XLA Ops:
  7.2 137.0 %all-gather.2.cloned.1.call-start = ((), (), s32[]{:S(2)}) async-start(), calls=%async_computation.4 | async-start | bytes 10948608 | tf_op jit(solution)/shard_map/all_gather | solution.py:1005
  10.5 1.4 collective-permute-start.1
  12.6 11.3 %collective-permute-start.2 = (bf16[2,32,1152]{2,1,0:T(8,128)(2,1)S(1)}, bf16[2,32,1152]{2,1,0:T(8,128)(2,1)S(1)}, u32[]{:S(2)}, u32[]{:S(2)}) collective-permute-start(bf16[2,32,1152]{2,1,0:T(8,128)(2,1)S(1)} %pad_maximum_fusion.10), channel_id=1, source_target_pairs={{0,8},{1,9},{2,10},{3,11},{4,12},{5,13},{6,14},{7,15},{8,0},{9,1},... | collective-permute-start | bytes 442376 | tf_op jit(solution)/shard_map/ppermute | solution.py:32
  16.6 36.3 %collective-permute-start.4 = (bf16[1024,768]{1,0:T(8,128)(2,1)S(1)}, bf16[1024,768]{1,0:T(8,128)(2,1)}, u32[]{:S(2)}, u32[]{:S(2)}) collective-permute-start(bf16[1024,768]{1,0:T(8,128)(2,1)S(1)} %bitcast.125), channel_id=1, source_target_pairs={{0,1},{1,0},{2,3},{3,2},{4,5},{5,4},{6,7},{7,6},{8,9},{9,8},{10,11... | collective-permute-start | bytes 4718600 | tf_op jit(solution)/shard_map/ppermute | solution.py:32
  24.0 8.6 %collective-permute-start.3 = (bf16[2,2,32,1152]{3,2,0,1:T(8,128)(2,1)S(1)}, bf16[2,2,32,1152]{3,2,0,1:T(8,128)(2,1)S(1)}, u32[]{:S(2)}, u32[]{:S(2)}) collective-permute-start(bf16[2,2,32,1152]{3,2,0,1:T(8,128)(2,1)S(1)} %pad_maximum_fusion.9), channel_id=1, source_target_pairs={{0,4},{1,5},{2,6},{3,7},{4,0},{5,1},{6,2},{7,3},{8,12},{9,13},{10,... | collective-permute-start | bytes 884744 | tf_op jit(solution)/shard_map/ppermute | solution.py:32
  52.9 235.1 %reduce-scatter.4.cloned.1.call-start = ((), (), s32[]{:S(2)}) async-start(), calls=%async_computation.5 | async-start | bytes 6635520 | tf_op jit(solution)/shard_map/reduce_scatter | solution.py:1047
  53.0 8.1 %collective-permute-start.6 = (bf16[2,2,32,1152]{3,2,0,1:T(8,128)(2,1)S(1)}, bf16[2,2,32,1152]{3,2,0,1:T(8,128)(2,1)}, u32[]{:S(2)}, u32[]{:S(2)}) collective-permute-start(bf16[2,2,32,1152]{3,2,0,1:T(8,128)(2,1)S(1)} %get-tuple-element.152), channel_id=1, source_target_pairs={{0,2},{1,3},{2,0},{3,1},{4,6},{5,7},{6,4},{7,5},{8,10},{9,11},{10,... | collective-permute-start | bytes 884744 | tf_op jit(solution)/shard_map/ppermute | solution.py:32
  54.6 7.7 %collective-permute-start.8 = (bf16[2,2,32,1152]{3,2,0,1:T(8,128)(2,1)S(1)}, bf16[2,2,32,1152]{3,2,0,1:T(8,128)(2,1)}, u32[]{:S(2)}, u32[]{:S(2)}) collective-permute-start(bf16[2,2,32,1152]{3,2,0,1:T(8,128)(2,1)S(1)} %get-tuple-element.151), channel_id=1, source_target_pairs={{0,1},{1,0},{2,3},{3,2},{4,5},{5,4},{6,7},{7,6},{8,9},{9,8},{10,11... | collective-permute-start | bytes 884744 | tf_op jit(solution)/shard_map/ppermute | solution.py:32
  64.4 14.2 %collective-permute-start.7 = (bf16[2,2,2,32,1152]{4,3,0,1,2:T(8,128)(2,1)}, bf16[2,2,2,32,1152]{4,3,0,1,2:T(8,128)(2,1)S(1)}, u32[]{:S(2)}, u32[]{:S(2)}) collective-permute-start(bf16[2,2,2,32,1152]{4,3,0,1,2:T(8,128)(2,1)} %pad_maximum_fusion.6), channel_id=1, source_target_pairs={{0,1},{1,0},{2,3},{3,2},{4,5},{5,4},{6,7},{7,6},{8,9},{9,8},{10,11... | collective-permute-start | bytes 1769480 | tf_op jit(solution)/shard_map/ppermute | solution.py:32
  66.8 13.1 %collective-permute-start.9 = (bf16[2,2,2,32,1152]{4,3,0,1,2:T(8,128)(2,1)}, bf16[2,2,2,32,1152]{4,3,0,1,2:T(8,128)(2,1)}, u32[]{:S(2)}, u32[]{:S(2)}) collective-permute-start(bf16[2,2,2,32,1152]{4,3,0,1,2:T(8,128)(2,1)} %pad_maximum_fusion.7), channel_id=1, source_target_pairs={{0,2},{1,3},{2,0},{3,1},{4,6},{5,7},{6,4},{7,5},{8,10},{9,11},{10,... | collective-permute-start | bytes 1769480 | tf_op jit(solution)/shard_map/ppermute | solution.py:32
  67.3 18.5 %collective-permute-start = (bf16[1024,768]{1,0:T(8,128)(2,1)S(1)}, bf16[1024,768]{1,0:T(8,128)(2,1)}, u32[]{:S(2)}, u32[]{:S(2)}) collective-permute-start(bf16[1024,768]{1,0:T(8,128)(2,1)S(1)} %bitcast.126), channel_id=1, source_target_pairs={{0,16},{16,0},{1,17},{17,1},{2,18},{18,2},{3,19},{19,3},{4,20},{20... | collective-permute-start | bytes 4718600 | tf_op jit(solution)/shard_map/ppermute | solution.py:32
  67.3 18.5 %collective-permute-start.5 = (bf16[1024,768]{1,0:T(8,128)(2,1)}, bf16[1024,768]{1,0:T(8,128)(2,1)}, u32[]{:S(2)}, u32[]{:S(2)}) collective-permute-start(bf16[1024,768]{1,0:T(8,128)(2,1)} %collective-permute-done.4.x2), channel_id=1, source_target_pairs={{0,16},{16,0},{1,17},{17,1},{2,18},{18,2},{3,19},{19,3},{4,20},{20... | collective-permute-start | bytes 4718600 | tf_op jit(solution)/shard_map/ppermute | solution.py:32
  142.0 2.3 collective-permute-start.10
  205.0 10.2 %collective-permute-start.12 = (bf16[4,4,9,24,768]{4,3,2,1,0:T(8,128)(2,1)}, bf16[4,4,9,24,768]{4,3,2,1,0:T(8,128)(2,1)S(1)}, u32[]{:S(2)}, u32[]{:S(2)}) collective-permute-start(bf16[4,4,9,24,768]{4,3,2,1,0:T(8,128)(2,1)} %get-tuple-element.86), channel_id=1, source_target_pairs={{0,16},{16,0},{1,17},{17,1},{2,18},{18,2},{3,19},{19,3},{4,20},{20... | collective-permute-start | bytes 15925256 | tf_op jit(solution)/shard_map/ppermute | solution.py:32
  205.2 6.9 %collective-permute-start.11 = (bf16[1024,384]{1,0:T(8,128)(2,1)S(1)}, bf16[1024,384]{1,0:T(8,128)(2,1)S(1)}, u32[]{:S(2)}, u32[]{:S(2)}) collective-permute-start(bf16[1024,384]{1,0:T(8,128)(2,1)S(1)} %copy-done.15), channel_id=1, source_target_pairs={{0,16},{16,0},{1,17},{17,1},{2,18},{18,2},{3,19},{19,3},{4,20},{20... | collective-permute-start | bytes 2359304 | tf_op jit(solution)/shard_map/ppermute | solution.py:32
  221.3 100.1 %reduce-scatter.6.cloned.1.call-start = ((), (), s32[]{:S(2)}) async-start(), calls=%async_computation.6 | async-start | bytes 1474560 | tf_op jit(solution)/shard_map/reduce_scatter | solution.py:1047
  283.7 2.2 collective-permute-start.13
  288.1 78.1 %reduce-scatter.8.cloned.1.call-start = ((), (), s32[]{:S(2)}) async-start(), calls=%async_computation.7 | async-start | bytes 2027520 | tf_op jit(solution)/shard_map/reduce_scatter | solution.py:1052
  321.3 3.6 collective-permute-start.14
  326.3 24.1 %collective-permute-start.15 = (bf16[640,768]{1,0:T(8,128)(2,1)S(1)}, bf16[640,768]{1,0:T(8,128)(2,1)S(1)}, u32[]{:S(2)}, u32[]{:S(2)}) collective-permute-start(bf16[640,768]{1,0:T(8,128)(2,1)S(1)} %add_convert_fusion.1), channel_id=1, source_target_pairs={{0,1},{1,0},{2,3},{3,2},{4,5},{5,4},{6,7},{7,6},{8,9},{9,8},{10,11... | collective-permute-start | bytes 2949128 | tf_op jit(solution)/shard_map/ppermute | solution.py:32
  334.7 1.9 collective-permute-start.16
  352.5 23.4 %all-to-all-start = ((bf16[16,32,768]{2,1,0:T(8,128)(2,1)}), bf16[16,32,768]{2,1,0:T(8,128)(2,1)S(1)}, u32[]{:S(2)}, u32[]{:S(2)}) async-start(bf16[16,32,768]{2,1,0:T(8,128)(2,1)} %bitcast.59), calls=%async_computation.3 | async-start | bytes 1572864 | tf_op jit(solution)/shard_map/all_to_all | solution.py:1088
  366.2 18.9 %collective-permute-start.17 = (bf16[1024,768]{1,0:T(8,128)(2,1)}, bf16[1024,768]{1,0:T(8,128)(2,1)S(1)}, u32[]{:S(2)}, u32[]{:S(2)}) collective-permute-start(bf16[1024,768]{1,0:T(8,128)(2,1)} %get-tuple-element.113), channel_id=1, source_target_pairs={{0,16},{16,0},{1,17},{17,1},{2,18},{18,2},{3,19},{19,3},{4,20},{20... | collective-permute-start | bytes 4718600 | tf_op jit(solution)/shard_map/ppermute | solution.py:32
  366.2 18.9 %collective-permute-start.18 = (bf16[384,768]{1,0:T(8,128)(2,1)}, bf16[384,768]{1,0:T(8,128)(2,1)}, u32[]{:S(2)}, u32[]{:S(2)}) collective-permute-start(bf16[384,768]{1,0:T(8,128)(2,1)} %add_convert_fusion.2), channel_id=1, source_target_pairs={{0,1},{1,0},{2,3},{3,2},{4,5},{5,4},{6,7},{7,6},{8,9},{9,8},{10,11... | collective-permute-start | bytes 1769480 | tf_op jit(solution)/shard_map/ppermute | solution.py:32
  (17 other events, 197.5 us)
Sparse Core Ops, SparseCore 0:
  53.0 87.7 all-gather.1
  221.5 60.7 reduce-scatter.3
  288.2 26.4 reduce-scatter.5
  323.9 34.1 reduce-scatter.7

commit v4 on v3

--- a/solution.py
+++ b/solution.py
@@ -83,7 +83,7 @@
 
 
 def attend_kernel(
-    sc, q_ref, ka_ref, kb_ref, va_ref, vb_ref, o_ref, lse_ref, keys, values, key_norm, *, heads, step
+    sc, q_ref, ka_ref, kb_ref, va_ref, vb_ref, own_ref, sib_ref, lse_ref, keys, values, key_norm, *, heads, step
 ):
     pair = pl.program_id(0)
     count = keys.shape[1]
@@ -121,9 +121,17 @@
 
     def finish(outs, peaks):
         totals = [jnp.broadcast_to(o[HD : HD + 1, :], (HD, rows)) for o in outs]
-        o_ref[...] = (
-            jnp.concatenate([o[:HD, :] / t for o, t in zip(outs, totals)], axis=0).T.astype(BF16)
-        )
+        out = jnp.concatenate([o[:HD, :] / t for o, t in zip(outs, totals)], axis=0).T.astype(BF16)
+        mine = pl.program_id(1) < pl.num_programs(1) // 2
+
+        @pl.when(mine)
+        def _():
+            own_ref[...] = out
+
+        @pl.when(jnp.logical_not(mine))
+        def _():
+            sib_ref[...] = out
+
         lse = jnp.concatenate([jnp.log(totals[1]), jnp.log(totals[0])], axis=0).T
         if peaks is not None:
             lse = lse + jnp.where(own0, peaks[1], peaks[0])
@@ -162,9 +170,14 @@
     return [key_value(0, 1), key_value(1, 1), key_value(0, 2), key_value(1, 2)]
 
 
+def halves_specs(rows, blocks, skip=0):
+    first = pl.BlockSpec((rows, LANES), lambda p, i, sc: (jnp.minimum(i, blocks // 2 - 1), p + skip))
+    return [first, pl.BlockSpec((rows, LANES), lambda p, i, sc: (jnp.maximum(i - blocks // 2, 0), p + skip))]
+
+
 def attend(sc, qkv, width):
     count = qkv.shape[1]
-    rows = min(1024, count)
+    rows = min(1024, count // 2)
     row_spec = pl.BlockSpec((rows, LANES), lambda p, i, sc: (i, p))
     q_spec = pl.BlockSpec((1, rows, LANES), lambda p, i, sc: (0, i, p))
     heads = width // HD
@@ -174,7 +187,7 @@
             num_scalar_prefetch=1,
             grid=(width // LANES, count // rows),
             in_specs=[q_spec] + pair_specs(count, width),
-            out_specs=[row_spec, row_spec],
+            out_specs=halves_specs(rows, count // rows) + [row_spec],
             scratch_shapes=[
                 pltpu.VMEM((2, count, LANES), BF16),
                 pltpu.VMEM((2, HD + 16, count), BF16),
@@ -182,7 +195,8 @@
             ],
         ),
         out_shape=[
-            jax.ShapeDtypeStruct((count, width), BF16),
+            jax.ShapeDtypeStruct((count // 2, width), BF16),
+            jax.ShapeDtypeStruct((count // 2, width), BF16),
             jax.ShapeDtypeStruct((count, width), F32),
         ],
         compiler_params=pltpu.CompilerParams(vmem_limit_bytes=VMEM_BYTES),
@@ -200,17 +214,26 @@
     kb_ref,
     va_ref,
     vb_ref,
-    o_ref,
+    o_own,
+    o_sib,
+    do_own,
+    do_sib,
     lse_ref,
-    do_ref,
+    x0,
+    x1,
+    x2,
+    x3,
     dq_ref,
     dkv_ref,
     sum_ref,
+    keep_ref,
+    send_ref,
     keys,
     keys_t,
     values,
     dk_sum,
     dv_sum,
+    dq_all,
     *,
     heads,
     step,
@@ -240,7 +263,9 @@
         dv_sum[...] = jnp.zeros_like(dv_sum)
 
     q = q_ref[0]
-    do = do_ref[...]
+    mine = block < pl.num_programs(1) // 2
+    do = jnp.where(mine, do_own[...], do_sib[...])
+    out = jnp.where(mine, o_own[...], o_sib[...])
     own0, sub = first_head(rows)
     qf = q.astype(F32) * scale
     first, second, third = three_parts(lse_ref[...])
@@ -248,7 +273,7 @@
         sub == 0, first, jnp.where(sub == 1, second, jnp.where(sub == 2, third, jnp.where(sub == 3, 1.0, 0.0)))
     )
     dof = do.astype(F32)
-    product = dof * o_ref[...].astype(F32)
+    product = dof * out.astype(F32)
     inner_a = jnp.sum(jnp.where(own0, product, 0.0), axis=1, keepdims=True)
     inner_b = jnp.sum(jnp.where(own0, 0.0, product), axis=1, keepdims=True)
     first, second, third = three_parts(jnp.where(own0, -inner_b, -inner_a))
@@ -273,6 +298,12 @@
         grads.append(dq)
     dq = (jnp.concatenate(grads, axis=0) * scale).astype(BF16)
     dq_ref[...] = dq
+    for i in range(count // rows):
+
+        @pl.when(block == i)
+        def _():
+            dq_all[:, i * rows : (i + 1) * rows] = dq
+
     for c in range(0, rows, LANES):
         sum_ref[...] += dq[:, c : c + LANES].astype(F32)
 
@@ -288,10 +319,37 @@
                 dkv_ref[half, 0, own_rows, :] = jnp.where(here, dk, 0.0).astype(BF16)
                 dkv_ref[half, 1, own_rows, :] = jnp.where(here, dv, 0.0).astype(BF16)
 
-
-def attend_back(sc, qkv, context, lse, grad_context, width, skip, pairs):
+        local = x0.shape[0]
+        near = jnp.concatenate([dq_all[...], dkv_ref[0, 0], dkv_ref[0, 1]], axis=0)
+        far = jnp.concatenate([dkv_ref[1, 0], dkv_ref[1, 1]], axis=0)
+        near = dot(near[:, :local], x0[...]) + dot(near[:, local:], x1[...])
+        far = dot(far[:, :local], x2[...]) + dot(far[:, local:], x3[...])
+        grad = jnp.concatenate([near[:LANES], near[LANES:] + far], axis=0).T.astype(BF16)
+        inner, outer, unit, _ = keep_ref.shape
+        half_rows = grad.shape[0] // 2
+        for c in (0, 1):
+            part = grad[c * half_rows : (c + 1) * half_rows].reshape(outer, inner, unit, 3 * LANES)
+            core = sc[heads + 3]
+
+            @pl.when(core == c)
+            def _():
+                for o in range(outer):
+                    keep_ref[:, o] = part[o]
+
+            @pl.when(core != c)
+            def _():
+                for o in range(outer):
+                    send_ref[:, o] = part[o]
+
+
+def attend_back(sc, qkv, contexts, lse, grads, pieces, width, skip, pairs, inner, outer):
+    model = pieces[0].shape[1]
+    unit = model // (2 * inner * outer)
+    piece = pl.BlockSpec(pieces[0].shape, lambda p, i, sc: (0, 0), pipeline_mode=pl.Buffered(1))
+    grad_spec = pl.BlockSpec((inner, outer, unit, 3 * LANES), lambda p, i, sc: (0, 0, 0, p))
+    grad_shape = jax.ShapeDtypeStruct((inner, outer, unit, 3 * pairs * LANES), BF16)
     count = qkv.shape[1]
-    rows = min(1024, count)
+    rows = min(1024, count // 2)
     row_spec = pl.BlockSpec((rows, LANES), lambda p, i, sc: (i, p + skip))
     q_spec = pl.BlockSpec((1, rows, LANES), lambda p, i, sc: (0, i, p + skip))
     dq_spec = pl.BlockSpec((LANES, rows), lambda p, i, sc: (p, i))
@@ -302,27 +360,38 @@
         grid_spec=pltpu.PrefetchScalarGridSpec(
             num_scalar_prefetch=1,
             grid=(pairs, count // rows),
-            in_specs=[q_spec] + pair_specs(count, width, skip) + [row_spec, row_spec, row_spec],
-            out_specs=[dq_spec, dkv_spec, pl.BlockSpec((LANES, LANES), lambda p, i, sc: (p, 0))],
+            in_specs=[q_spec] + pair_specs(count, width, skip) + halves_specs(rows, count // rows, skip) * 2
+            + [row_spec]
+            + [piece] * 4,
+            out_specs=[
+                dq_spec,
+                dkv_spec,
+                pl.BlockSpec((LANES, LANES), lambda p, i, sc: (p, 0)),
+                grad_spec,
+                grad_spec,
+            ],
             scratch_shapes=[
                 pltpu.VMEM((2, count, LANES), BF16),
                 pltpu.VMEM((2, HD, count), BF16),
                 pltpu.VMEM((2, count, LANES), BF16),
                 pltpu.VMEM((LANES, count), F32),
                 pltpu.VMEM((LANES, count), F32),
+                pltpu.VMEM((LANES, count), BF16),
             ],
         ),
         out_shape=[
             jax.ShapeDtypeStruct((pairs * LANES, count), BF16),
             jax.ShapeDtypeStruct((2, 2, pairs * LANES, count), BF16),
             jax.ShapeDtypeStruct((pairs * LANES, LANES), F32),
+            grad_shape,
+            grad_shape,
         ],
         compiler_params=pltpu.CompilerParams(vmem_limit_bytes=VMEM_BYTES),
         cost_estimate=pl.CostEstimate(
             flops=10 * 4 * count * count * pairs * LANES, bytes_accessed=2 * 12 * count * pairs * LANES, transcendentals=0
         ),
         name="attend_back",
-    )(sc, qkv, qkv, qkv, qkv, qkv, context, lse, grad_context)
+    )(sc, qkv, qkv, qkv, qkv, qkv, *contexts, *grads, lse, *pieces)
 
 
 def mean_of(value):
@@ -517,118 +586,112 @@
     )(core, x, own, other, cot, *([weights] * (3 + parts)), vec)
 
 
-def weight_grads_kernel(
-    core, act, gb, low, gh, own, other, attn, keep_ref, send_ref, stage_a, stage_b, sems, *, parts
-):
-    step = pl.program_id(0)
-    inner, outer, _, unit, width = keep_ref.shape
-    last = 2 * parts
-
-    def tn(a, b):
-        return lax.dot_general(a, b, (((0,), (0,)), ((), ())), preferred_element_type=F32).astype(BF16)
-
-    def copies(t):
-        slot = t % 2
-        runs = 2 * outer // parts if t < parts else 2 * outer
-        found = []
-        for r in range(runs):
-            g = t * runs + r if t < parts else r
-            take = slice(r * inner, (r + 1) * inner)
-            at = (slice(None), g % outer, slice(0, parts) if t < parts else t)
-            source = (stage_a if t < parts else stage_b).at[slot, take]
-            found.append(
-                (g // outer,)
-                + tuple(
-                    functools.partial(pltpu.make_async_copy, source, ref.at[at], sems.at[slot])
-                    for ref in (keep_ref, send_ref)
-                )
-            )
-        return found
-
-    def finish(t):
-        for _, keep, _ in copies(t):
-            keep().wait()
-
-    for t in range(2, last + 1):
-
-        @pl.when(step == t)
-        def _():
-            finish(t - 2)
-
-    slot = lax.rem(step, 2)
-
-    @pl.when(step < parts)
+def dot_tn(a, b):
+    return lax.dot_general(a, b, (((0,), (0,)), ((), ())), preferred_element_type=F32)
+
+
+def back_grads_kernel(core, act, gb, *refs):
+    *came, out_ref = refs
+    inner, span, parts, unit, width = out_ref.shape
+    got = dot_tn(act[...], gb[...]).reshape(span, inner, parts, unit, width)
+    for o in range(span):
+        mine = got[o]
+        for ref in came:
+            mine = mine + ref[:, o].astype(F32)
+        out_ref[:, o] = mine.astype(BF16)
+
+
+def in_grads_kernel(core, low, gh, context, attn, *refs, parts):
+    *came, out_ref = refs
+    came = came[:1]
+    inner, outer, _, unit, width = out_ref.shape
+
+    def put(value):
+        value = value.reshape(outer, inner, unit, width)
+        for o in range(outer):
+            mine = value[o]
+            for ref in came:
+                mine = mine + ref[:, o, 0].astype(F32)
+            out_ref[:, o, 0] = mine.astype(BF16)
+
+    @pl.when(pl.program_id(0) < parts)
     def _():
-        stage_a[slot] = tn(act[...], gb[...]).reshape(stage_a.shape[1:])
-
-    @pl.when(jnp.logical_and(step >= parts, step < last))
+        put(dot_tn(low[...], gh[...]))
+
+    @pl.when(pl.program_id(0) == parts)
     def _():
-        stage_b[slot] = tn(low[...], gh[...]).reshape(stage_b.shape[1:])
-
-    @pl.when(step == last)
-    def _():
-        half = stage_b.shape[1] // 2
-        stage_b[slot, :half] = tn(own[...], attn[...]).reshape((half,) + stage_b.shape[2:])
-        stage_b[slot, half:] = tn(other[...], attn[...]).reshape((half,) + stage_b.shape[2:])
-
-    for t in range(last + 1):
-
-        @pl.when(step == t)
-        def _():
-            for c, keep, send in copies(t):
-                if t == last:
-                    (keep if c == 0 else send)().start()
-                    continue
-
-                @pl.when(core[0] == c)
-                def _():
-                    keep().start()
-
-                @pl.when(core[0] != c)
-                def _():
-                    send().start()
-
-    @pl.when(step == last)
-    def _():
-        finish(last - 1)
-        finish(last)
+        put(dot_tn(context[...], attn[...]))
 
 
 def weight_grads(core, act, gb, low, gh, own, other, attn, inner, outer):
     count, width = low.shape
     parts = act.shape[1] // width
     unit = width // (2 * inner * outer)
+    tiles = parts // 2
+    span = outer // tiles
     once = pl.Buffered(1)
-    whole = lambda a: pl.BlockSpec(a.shape, lambda t, core: (0, 0), pipeline_mode=once)
-    shape = jax.ShapeDtypeStruct((inner, outer, 2 * parts + 1, unit, width), BF16)
-    return pl.pallas_call(
-        functools.partial(weight_grads_kernel, parts=parts),
-        grid_spec=pltpu.PrefetchScalarGridSpec(
-            num_scalar_prefetch=1,
-            grid=(2 * parts + 1,),
-            in_specs=[
+    whole = pl.BlockSpec((count, width), lambda t, core: (0, 0), pipeline_mode=once)
+    anywhere = pl.BlockSpec(memory_space=pl.ANY)
+
+    def call(kernel, tiles, in_specs, out_spec, slots, args, came, aliases, flops):
+        return pl.pallas_call(
+            kernel,
+            grid_spec=pltpu.PrefetchScalarGridSpec(
+                num_scalar_prefetch=1, grid=(tiles,), in_specs=in_specs, out_specs=out_spec
+            ),
+            out_shape=jax.ShapeDtypeStruct((inner, outer, slots, unit, width), BF16),
+            input_output_aliases=aliases,
+            compiler_params=pltpu.CompilerParams(vmem_limit_bytes=VMEM_BYTES),
+            cost_estimate=pl.CostEstimate(flops=flops, bytes_accessed=3 * flops // width, transcendentals=0),
+            name="weight_grads",
+        )(core, *args, *came)
+
+    def back(pick, slots, came):
+        spec = pl.BlockSpec((inner, span, parts, unit, width), lambda t, core: (0, t, 0, 0, 0))
+        tile = pl.BlockSpec((count, width), lambda t, core: (0, tiles * pick(core[0]) + t))
+        return call(
+            back_grads_kernel,
+            tiles,
+            [tile, whole] + [spec] * len(came),
+            spec,
+            slots,
+            (act, gb),
+            came,
+            {},
+            count * width * width * parts,
+        )
+
+    def into(pick, context, skip, came, base):
+        spec = lambda skip: pl.BlockSpec((inner, outer, 1, unit, width), lambda t, core: (0, 0, t + skip, 0, 0))
+        half = context.shape[1]
+        return call(
+            functools.partial(in_grads_kernel, parts=parts),
+            parts + 1,
+            [
+                pl.BlockSpec((count, half), lambda t, core: (0, pick(core[0])), pipeline_mode=once),
                 pl.BlockSpec((count, width), lambda t, core: (0, jnp.minimum(t, parts - 1))),
-                whole(gb),
-                whole(low),
-                pl.BlockSpec((count, width), lambda t, core: (0, jnp.clip(t - parts, 0, parts - 1))),
-                whole(own),
-                whole(other),
-                whole(attn),
-            ],
-            out_specs=[pl.BlockSpec(memory_space=pl.ANY)] * 2,
-            scratch_shapes=[
-                pltpu.VMEM((2, 2 * inner * outer // parts, parts, unit, width), BF16),
-                pltpu.VMEM((2, 2 * inner * outer, unit, width), BF16),
-                pltpu.SemaphoreType.DMA((2,)),
-            ],
-        ),
-        out_shape=[shape, shape],
-        compiler_params=pltpu.CompilerParams(vmem_limit_bytes=VMEM_BYTES),
-        cost_estimate=pl.CostEstimate(
-            flops=2 * count * width * width * (2 * parts + 1), bytes_accessed=2 * width * (2 * parts + 4) * (count + width), transcendentals=0
-        ),
-        name="weight_grads",
-    )(core, act, gb, low, gh, own, other, attn)
+                pl.BlockSpec((count, half), lambda t, core: (0, 0), pipeline_mode=once),
+                whole,
+            ]
+            + [spec(0)] * len(came)
+            + [anywhere] * len(base),
+            spec(skip),
+            skip + parts + 1,
+            (low, gh, context, attn),
+            came + base,
+            {6: 0} if base else {},
+            count * width * width * (parts + 1),
+        )
+
+    mine, theirs = (lambda c: c), (lambda c: 1 - c)
+    sent = back(theirs, parts, ())
+    sent, low, act = lax.optimization_barrier((sent, low, act))
+    back_came = swap(sent, "head", 1)
+    in_sent = into(theirs, other, 0, (), ())
+    back_came, in_sent, act = lax.optimization_barrier((back_came, in_sent, act))
+    in_came = swap(in_sent, "head", 1)
+    kept = back(mine, 2 * parts + 1, (back_came,))
+    return into(mine, own, parts, (in_came,), (kept,))
 
 
 def project_kernel(x0, x1, x2, x3, first, second, bias, out_ref, weight_ref, *, group):
@@ -768,81 +831,6 @@
     )(*dq, *dkv, weight, resid)
 
 
-def qkv_grads_kernel(core, dq, dkv, x0, x1, x2, x3, *refs):
-    *small, keep_ref, send_ref = refs
-    step = pl.program_id(0)
-    inner, outer = keep_ref.shape[:2]
-    unit = x0.shape[1] // (2 * inner * outer)
-    local = x0.shape[0]
-
-    def put(value):
-        value = value.T.astype(BF16)
-        half = value.shape[0] // 2
-        for h in (0, 1):
-            part = value[h * half : (h + 1) * half].reshape(outer, inner, unit, -1)
-
-            @pl.when(core[0] == h)
-            def _():
-                for o in range(outer):
-                    keep_ref[:, o, :unit, :] = part[o]
-
-            @pl.when(core[0] != h)
-            def _():
-                for o in range(outer):
-                    send_ref[:, o, :unit, :] = part[o]
-
-    @pl.when(step == 0)
-    def _():
-        put(dot(dq[:, :local], x0[...]) + dot(dq[:, local:], x1[...]))
-
-    @pl.when(step > 0)
-    def _():
-        near, far = dkv[0, 0], dkv[1, 0]
-        put(
-            dot(near[:, :local], x0[...])
-            + dot(near[:, local:], x1[...])
-            + dot(far[:, :local], x2[...])
-            + dot(far[:, local:], x3[...])
-        )
-
-    for extra in small:
-        keep_ref[:, :, unit:, :] = extra[0]
-        send_ref[:, :, unit:, :] = extra[1]
-
-
-def qkv_grads(core, dq, dkv, pieces, inner, outer, *small):
-    count, width = pieces[0].shape
-    group, full = dq.shape
-    extra = sum(part.shape[3] for part in small)
-    unit = width // (2 * inner * outer)
-    once = pl.Buffered(1)
-    whole = pl.BlockSpec((count, width), lambda t, core: (0, 0), pipeline_mode=once)
-    out_spec = pl.BlockSpec((inner, outer, unit + extra, group), lambda t, core: (0, 0, 0, t))
-    return pl.pallas_call(
-        qkv_grads_kernel,
-        grid_spec=pltpu.PrefetchScalarGridSpec(
-            num_scalar_prefetch=1,
-            grid=(3,),
-            in_specs=[
-                pl.BlockSpec((group, full), lambda t, core: (0, 0), pipeline_mode=once),
-                pl.BlockSpec((2, 1, group, full), lambda t, core: (0, jnp.maximum(t - 1, 0), 0, 0)),
-                whole,
-                whole,
-                whole,
-                whole,
-                *[pl.BlockSpec((2, inner, outer, extra, group), lambda t, core: (0, 0, 0, 0, t)) for _ in small],
-            ],
-            out_specs=[out_spec, out_spec],
-        ),
-        out_shape=[jax.ShapeDtypeStruct((inner, outer, unit + extra, 3 * group), BF16)] * 2,
-        compiler_params=pltpu.CompilerParams(vmem_limit_bytes=VMEM_BYTES),
-        cost_estimate=pl.CostEstimate(
-            flops=10 * full * width * group, bytes_accessed=8 * full * width + 20 * full * group, transcendentals=0
-        ),
-        name="qkv_grads",
-    )(core, dq, dkv, *pieces, *small)
-
-
 def unpack_kernel(core, chip, moved, back_ref, in_ref, out_ref, qkv_ref, vec_ref, *, rows, parts):
     width = chip.shape[1]
     at = lambda slot, count=1: chip[slot * rows : (slot + count) * rows, :].astype(F32)
@@ -855,15 +843,18 @@
     half = total.shape[1] // 2
     firsts = at(2 * parts + 1), at(2 * parts + 2)
     seconds = total[:rows, :half], total[:rows, half:]
-    wide, narrow = width // 3, half // 3
+    block = half // 3
     for h in (0, 1):
         own = core[0] == h
         first = jnp.where(own, *firsts)
         second = jnp.where(own, *seconds)
+        early = width // half
         for t in range(3):
-            start = (2 * t + h) * (wide + narrow)
-            qkv_ref[:, start : start + wide] = first[:, t * wide : (t + 1) * wide]
-            qkv_ref[:, start + wide : start + wide + narrow] = second[:, t * narrow : (t + 1) * narrow]
+            for p in range(early + 1):
+                start = ((2 * t + h) * (early + 1) + p) * block
+                source, at_pair = (first, p) if p < early else (second, 0)
+                lane = (3 * at_pair + t) * block
+                qkv_ref[:, start : start + block] = source[:, lane : lane + block]
 
 
 def unpack(core, chip, moved, rows, parts):
@@ -893,7 +884,8 @@
 
 
 GATE = 4
-SHARES = (20,)
+SHARES = (21,)
+ORDER = 0
 
 
 def unpacked(blocks, parts):
@@ -912,10 +904,6 @@
     return jnp.concatenate(
         [a.reshape(devices, -1, width) for a in (back, into, out)], axis=1
     )
-
-
-def dot_tn(a, b):
-    return lax.dot_general(a, b, (((0,), (0,)), ((), ())), preferred_element_type=F32)
 
 
 def per_device(
@@ -1028,16 +1016,16 @@
     bounds = [jnp.clip(length - h * half, 0, half) for h in (own_half, 1 - own_half)]
     sc = jnp.concatenate([flags, jnp.stack(bounds + [jnp.int32(local), core])]).astype(jnp.int32)
 
-    context, lse = attend(sc, qkv, group)
-    other = swap(context[local:], "head", 1)
+    context_own, context_sib, lse = attend(sc, qkv, group)
+    other = swap(context_sib, "head", 1)
     at_core = core.reshape(1).astype(jnp.int32)
     out, grad_resid1, gc_own, gc_other, low, act, gh, gb, attn, sums = middle(
-        at_core, x, context[:local], other, cotangent[0], gathered, vec
-    )
-    grad_context = jnp.concatenate([gc_own, swap(gc_other, "head", 1)], axis=0)
-
-    keep, send = weight_grads(at_core, act, gb, low, gh, context[:local], other, attn, inner, outer)
-    chip = (keep.astype(F32) + swap(send, "head", 1).astype(F32)).astype(BF16)
+        at_core, x, context_own, other, cotangent[0], gathered, vec
+    )
+    grad_context = (gc_own, swap(gc_other, "head", 1))
+    contexts = (context_own, context_sib)
+
+    chip = weight_grads(at_core, act, gb, low, gh, context_own, other, attn, inner, outer)
     grad_context, chip = lax.optimization_barrier((grad_context, chip))
     near_groups = [[o * inner + i for i in range(inner)] for o in range(outer)]
     far_groups = [[o * inner + i for o in range(outer)] for i in range(inner)]
@@ -1067,18 +1055,13 @@
     early_small = jnp.concatenate([by_rows, sums[0].reshape(cores, blocks, parts * rows)], axis=2)
     early_small, grad_context = lax.optimization_barrier((early_small, grad_context))
 
-    def part_rows(dq, dkv, *small_rows):
-        columns = 3 * dq.shape[0]
-        keep, send = qkv_grads(at_core, dq, dkv, pieces, inner, outer, *(small_rows if direct else ()))
+    def part_rows(keep, send, *small_rows):
         if not direct:
-            keep, send = (
-                jnp.concatenate(
-                    [a.transpose(1, 0, 2, 3).reshape(blocks, rows, columns)]
-                    + [b[i].transpose(1, 0, 2, 3).reshape(blocks, -1, columns) for b in small_rows],
-                    axis=1,
-                )
-                for i, a in enumerate((keep, send))
-            )
+            keep, send = (a.transpose(1, 0, 2, 3).reshape(blocks, rows, -1) for a in (keep, send))
+        for extra in small_rows:
+            if not direct:
+                extra = extra.transpose(0, 2, 1, 3, 4).reshape(2, blocks, 8, -1)
+            keep, send = (jnp.concatenate([a, b], axis=-2) for a, b in zip((keep, send), extra))
         return keep, swap(send, "head", 1)
 
     def finish_part(keep, came):
@@ -1092,16 +1075,18 @@
 
     pairs = group // LANES
     first_pairs = pairs - pairs // 3
-    dq_a, dkv_a, sum_a = attend_back(sc, qkv, context, lse, grad_context, group, 0, first_pairs)
-    keep_a, came_a = part_rows(dq_a, dkv_a)
+    dq_a, dkv_a, sum_a, *grad_a = attend_back(
+        sc, qkv, contexts, lse, grad_context, pieces, group, 0, first_pairs, inner, outer
+    )
+    keep_a, came_a = part_rows(*grad_a)
     if direct:
         part_a = jnp.concatenate([keep_a, came_a], axis=2)
         grad_context, part_a, chip = lax.optimization_barrier((grad_context, part_a, chip))
         chip = over_column(jnp.concatenate([chip, over_plane(part_a)], axis=1))
     else:
         total_a = total_of(finish_part(keep_a, came_a))
-    dq_b, dkv_b, sum_b = attend_back(
-        sc, qkv, context, lse, grad_context, group, first_pairs, pairs - first_pairs
+    dq_b, dkv_b, sum_b, *grad_b = attend_back(
+        sc, qkv, contexts, lse, grad_context, pieces, group, first_pairs, pairs - first_pairs, inner, outer
     )
 
     q_sums = jnp.sum(jnp.concatenate([sum_a, sum_b], axis=0), axis=1)
@@ -1116,6 +1101,7 @@
     small_rows = small_rows.reshape(2, blocks // inner, inner, 8, room).transpose(0, 2, 1, 3, 4)
 
     dkv = (dkv_a, dkv_b)
+    keep_b, came_b = part_rows(*grad_b, small_rows)
     keep_far, send_far = far_rows(dkv, weight)
     far_sib = swap(send_far, "head", 1)
     cuts = [0, *(local * share // 32 for share in SHARES), local]
@@ -1123,13 +1109,12 @@
         (keep_far[lo:hi].astype(F32) + far_sib[lo:hi].astype(F32)).astype(BF16)
         for lo, hi in zip(cuts, cuts[1:])
     ]
-    far_sums, dq_b = lax.optimization_barrier((far_sums, dq_b))
+    far_sums, dq_a, dq_b = lax.optimization_barrier((far_sums, dq_a, dq_b))
     far_in = [swap(part, "blk", 1) for part in far_sums]
-    keep_b, came_b = part_rows(dq_b, dkv_b, small_rows)
-    far_in[0], came_b = lax.optimization_barrier((far_in[0], came_b))
+    keep_near, send_near = near_rows((dq_a, dq_b), dkv, weight, grad_resid1)
+    if ORDER == 0:
+        far_in[0], came_b, send_near = lax.optimization_barrier((far_in[0], came_b, send_near))
     moved_b = finish_part(keep_b, came_b)
-    came_b, dq_a = lax.optimization_barrier((came_b, dq_a))
-    keep_near, send_near = near_rows((dq_a, dq_b), dkv, weight, grad_resid1)
     chip, send_near = lax.optimization_barrier((chip, send_near))
     near_sib = swap(send_near, "head", 1)
     grad_tokens = keep_near + near_sib.astype(F32) + jnp.concatenate(far_in, axis=0).astype(F32)
@@ -1146,8 +1131,8 @@
         sum_wout = chip[2 * parts * rows : (2 * parts + 1) * rows].astype(F32)
 
         def columns_of(total):
-            own_w, other_w = (total[:rows, s].reshape(rows, 3, -1) for s in (0, 1))
-            return place(own_w, other_w, core == 1, 2)
+            parts_of = lambda a: a.reshape(rows, -1, 3, LANES).transpose(0, 2, 1, 3).reshape(rows, 3, -1)
+            return place(*(parts_of(total[:rows, s]) for s in (0, 1)), core == 1, 2)
 
         sum_wqkv = jnp.concatenate([columns_of(total_a), columns_of(total_b)], axis=3).reshape(rows, 3 * width)
         vectors = jnp.sum(total_b[rows : rows + 2], axis=(0, 1))

time: 403 us -> 395 us (0.980)
  other arithmetic: 28.4 us -> 16.3 us
  Pallas kernels: 225 us -> 231 us
    ppermute x19 -> x20, waiting for transfers between devices: 81.3 us -> 69.9 us  [swap(): return lax.ppermute(value, axis, pairs)]
    pallas_call x2, Pallas kernels: 74.7 us -> 85.7 us  [attend_back(): pl.pallas_call(functools.partial(attend_back_kernel, heads=heads, step=mi...]
    all_to_all x1, waiting for transfers between devices: 7.88 us -> 16.4 us  [finish_part(): return lax.all_to_all(both_cores, 'blk', 0, 0, tiled=True)]
    pallas_call x3 -> x4, Pallas kernels: 37 us -> 29.3 us  [call(): pl.pallas_call(kernel, grid_spec=pltpu.PrefetchScalarGridSpec(num_scalar_...]
    convert_element_type x1 -> x0, other arithmetic: 6.13 us -> none  [per_device(): chip = (keep.astype(F32) + swap(send, 'head', 1).astype(F32)).astype(BF16)]
    ppermute x19 -> x20, starting transfers between devices: 15.4 us -> 16.3 us  [swap(): return lax.ppermute(value, axis, pairs)]
  transfers between devices with their start and end apart: 24 -> 25, of which waited for: 17 -> 15; matrix products, arithmetic and copies ran while one was open for 7% -> 5% of each run, Pallas kernels for 42% -> 48%
where the time goes in v4:
time: 395 us; the launch traced here: 389 us
  Pallas kernels  231 us (58%)
  waiting for transfers between devices  88.6 us (22%)
  starting transfers between devices  20 us (5%)
  local copies, waits for them, and re-layouts  17.2 us (4%)
  other arithmetic  16.3 us (4%)
  between operations  16.1 us (4%)
    pallas_call x2, Pallas kernels, attend_back(): pl.pallas_call(functools.partial(attend_back_kernel, heads=heads, step=mi...  85.7 us
    ppermute x20, waiting for transfers between devices, swap(): return lax.ppermute(value, axis, pairs)  69.9 us
    pallas_call x1, Pallas kernels, attend(): pl.pallas_call(functools.partial(attend_kernel, heads=heads, step=min(512...  41.7 us
    pallas_call x1, Pallas kernels, middle(): pl.pallas_call(functools.partial(middle_kernel, width=width, ff=ff), grid...  40.1 us
    pallas_call x4, Pallas kernels, call(): pl.pallas_call(kernel, grid_spec=pltpu.PrefetchScalarGridSpec(num_scalar_...  29.3 us
    all_to_all x1, waiting for transfers between devices, finish_part(): return lax.all_to_all(both_cores, 'blk', 0, 0, tiled=True)  16.4 us
    ppermute x20, starting transfers between devices, swap(): return lax.ppermute(value, axis, pairs)  16.3 us
    pallas_call x1, Pallas kernels, project(): pl.pallas_call(functools.partial(project_kernel, group=wide // 3), grid=(...  14.4 us
  transfers between devices with their start and end apart: 25, of which 15 were waited for; matrix products, arithmetic and copies ran while one was open for 5% of the time, Pallas kernels for 48%

profile of v4, /device:TPU:0, one launch (start us, length us, event | category | flops | bytes accessed | tf_op | source)
XLA Modules:
  0.0 389.0 jit_solution(17155084141379790512)
XLA Ops:
  12.6 4.0 %collective-permute-start.2 = (bf16[2,32,1152]{2,1,0:T(8,128)(2,1)S(1)}, bf16[2,32,1152]{2,1,0:T(8,128)(2,1)S(1)}, u32[]{:S(2)}, u32[]{:S(2)}) collective-permute-start(bf16[2,32,1152]{2,1,0:T(8,128)(2,1)S(1)} %pad_maximum_fusion.10), channel_id=1, source_target_pairs={{0,8},{1,9},{2,10},{3,11},{4,12},{5,13},{6,14},{7,15},{8,0},{9,1},... | collective-permute-start | bytes 442376 | tf_op jit(solution)/shard_map/ppermute | solution.py:32
  18.1 5.8 %collective-permute-done.2 = bf16[2,32,1152]{2,1,0:T(8,128)(2,1)S(1)} collective-permute-done((bf16[2,32,1152]{2,1,0:T(8,128)(2,1)S(1)}, bf16[2,32,1152]{2,1,0:T(8,128)(2,1)S(1)}, u32[]{:S(2)}, u32[]{:S(2)}) %collective-permute-start.2) | collective-permute-done | bytes 147488 | tf_op jit(solution)/shard_map/ppermute | solution.py:32
  25.6 7.0 %collective-permute-done.3 = bf16[2,2,32,1152]{3,2,0,1:T(8,128)(2,1)S(1)} collective-permute-done((bf16[2,2,32,1152]{3,2,0,1:T(8,128)(2,1)S(1)}, bf16[2,2,32,1152]{3,2,0,1:T(8,128)(2,1)S(1)}, u32[]{:S(2)}, u32[]{:S(2)}) %collective-permute-start.3) | collective-permute-done | bytes 294944 | tf_op jit(solution)/shard_map/ppermute | solution.py:32
  32.7 20.3 %collective-permute-done.4.x2 = bf16[1024,768]{1,0:T(8,128)(2,1)} collective-permute-done((bf16[1024,768]{1,0:T(8,128)(2,1)}, bf16[1024,768]{1,0:T(8,128)(2,1)}, u32[]{:S(2)}, u32[]{:S(2)}) %collective-permute-start.4) | collective-permute-done | bytes 1572896 | tf_op jit(solution)/shard_map/ppermute | solution.py:32
  56.3 4.9 %collective-permute-done.6 = bf16[2,2,32,1152]{3,2,0,1:T(8,128)(2,1)S(1)} collective-permute-done((bf16[2,2,32,1152]{3,2,0,1:T(8,128)(2,1)S(1)}, bf16[2,2,32,1152]{3,2,0,1:T(8,128)(2,1)S(1)}, u32[]{:S(2)}, u32[]{:S(2)}) %collective-permute-start.6) | collective-permute-done | bytes 294944 | tf_op jit(solution)/shard_map/ppermute | solution.py:32
  68.0 10.1 %collective-permute-done.7 = bf16[2,2,2,32,1152]{4,3,0,1,2:T(8,128)(2,1)S(1)} collective-permute-done((bf16[2,2,2,32,1152]{4,3,0,1,2:T(8,128)(2,1)S(1)}, bf16[2,2,2,32,1152]{4,3,0,1,2:T(8,128)(2,1)S(1)}, u32[]{:S(2)}, u32[]{:S(2)}) %collective-permute-start.7) | collective-permute-done | bytes 589856 | tf_op jit(solution)/shard_map/ppermute | solution.py:32
  82.6 14.4 %project.1 = (bf16[2,2048,1152]{2,1,0:T(8,128)(2,1)}, bf16[768,1152]{1,0:T(8,128)(2,1)}) custom-call(bf16[1024,768]{1,0:T(8,128)(2,1)} %bitcast.1.x0.x_ref, bf16[1024,768]{1,0:T(8,128)(2,1)} %collective-permute-done.x1, bf16[1024,768]{1,0:T(8,128)(2,1)} %collective-permute-done.4.x2, bf16[1024,768]{1,0:T(8,128)(2,1)} %collective-permute-done.5.x3, ...), custom_call_target="tpu_custom_call" | custom-call | flops 7247757312 | bytes 15728640 | tf_op jit(solution)/shard_map/project/pallas_call | solution.py:725
  97.0 41.7 %attend.1 = (bf16[1024,384]{1,0:T(8,128)(2,1)}, bf16[1024,384]{1,0:T(8,128)(2,1)}, f32[2048,384]{1,0:T(8,128)}) custom-call(s32[10]{0:T(128)} %concatenate.60.sc, bf16[2,2048,1152]{2,1,0:T(8,128)(2,1)} %get-tuple-element.81.q_ref.ka_ref.kb_ref.va_ref.vb_ref, bf16[2,2048,1152]{2,1,0:T(8,128)(2,1)} %get-tuple-element.81.q_ref.ka_ref.kb_ref.va_ref.vb_ref, ...), custom_call_target="tpu_custom_call" | custom-call | flops 25769803776 | bytes 9437184 | tf_op jit(solution)/shard_map/attend/pallas_call | solution.py:184
  139.5 2.5 collective-permute-done.10.other_ref.context
  142.9 40.1 %middle.1 = (bf16[1024,768]{1,0:T(8,128)(2,1)}, f32[1024,768]{1,0:T(8,128)}, bf16[1024,384]{1,0:T(8,128)(2,1)}, bf16[1024,384]{1,0:T(8,128)(2,1)}, bf16[1024,768...) custom-call(s32[1]{0:T(128)} %bitcast.core, ...), custom_call_target="tpu_custom_call" | custom-call | flops 21743271936 | bytes 44040192 | tf_op jit(solution)/shard_map/middle/pallas_call | solution.py:533
  183.0 5.8 %weight_grads.4 = bf16[4,4,4,24,768]{4,3,2,1,0:T(8,128)(2,1)} custom-call(s32[1]{0:T(128)} %bitcast.core, bf16[1024,3072]{1,0:T(8,128)(2,1)} %get-tuple-element.98.act, bf16[1024,768]{1,0:T(8,128)(2,1)} %get-tuple-element.90.gb), custom_call_target="tpu_custom_call" | custom-call | flops 2415919104 | bytes 9437184 | tf_op jit(solution)/shard_map/weight_grads/pallas_call | solution.py:637
  189.2 8.3 %weight_grads.5 = bf16[4,4,5,24,768]{4,3,2,1,0:T(8,128)(2,1)} custom-call(s32[1]{0:T(128)} %bitcast.core, bf16[1024,768]{1,0:T(8,128)(2,1)} %get-tuple-element.92.low, bf16[1024,3072]{1,0:T(8,128)(2,1)} %get-tuple-element.93.gh, bf16[1024,384]{1,0:T(8,128)(2,1)} %copy-done.9, bf16[1024,768]{1,0:T(8,128)(2,1)} %get-tuple-element.94.attn), custom_call_target="tpu_custom_call" | custom-call | flops 3019898880 | bytes 11796480 | tf_op jit(solution)/shard_map/weight_grads/pallas_call | solution.py:637
  198.9 6.2 %weight_grads.6.refs_1_ = bf16[4,4,9,24,768]{4,3,2,1,0:T(8,128)(2,1)} custom-call(s32[1]{0:T(128)} %bitcast.core, bf16[1024,3072]{1,0:T(8,128)(2,1)} %get-tuple-element.98.act, bf16[1024,768]{1,0:T(8,128)(2,1)} %get-tuple-element.90.gb, bf16[4,4,4,24,768]{4,3,2,1,0:T(8,128)(2,1)} %copy-done.4), custom_call_target="tpu_custom_call" | custom-call | flops 2415919104 | bytes 9437184 | tf_op jit(solution)/shard_map/weight_grads/pallas_call | solution.py:637
  206.7 9.0 %weight_grads.7 = bf16[4,4,9,24,768]{4,3,2,1,0:T(8,128)(2,1)} custom-call(s32[1]{0:T(128)} %bitcast.core, bf16[1024,768]{1,0:T(8,128)(2,1)} %get-tuple-element.92.low, bf16[1024,3072]{1,0:T(8,128)(2,1)} %get-tuple-element.93.gh, bf16[1024,384]{1,0:T(8,128)(2,1)} %get-tuple-element.82.own_ref.context.o_own, ...), custom_call_target="tpu_custom_call", output_to_operand_aliasing={{}: (6, {})} | custom-call | flops 3019898880 | bytes 11796480 | tf_op jit(solution)/shard_map/weight_grads/pallas_call | solution.py:637
  220.3 55.0 %attend_back.2 = (bf16[256,2048]{1,0:T(8,128)(2,1)}, bf16[2,2,256,2048]{3,2,1,0:T(8,128)(2,1)}, f32[256,128]{1,0:T(8,128)}, bf16[4,4,24,768]{3,2,1,0:T(8,128)(2,1)}, bf16[4,4,24,768]{3,2,1,0:T(8,128)(2,1)}) custom-call(s32[10]{0:T(128)} %concatenate.60.sc, bf16[2,2048,1152]{2,1,0:T(8,128)(2,1)} %get-tuple-element.81.q_ref.ka_ref.kb_ref.va_ref.vb_ref, ...), custom_call_target="tpu_custom_call" | custom-call | flops 42949672960 | bytes 12582912 | tf_op jit(solution)/shard_map/attend_back/pallas_call | solution.py:358
  277.6 2.2 pad_maximum_fusion.3
  279.9 30.7 %attend_back.3 = (bf16[128,2048]{1,0:T(8,128)(2,1)}, bf16[2,2,128,2048]{3,2,1,0:T(8,128)(2,1)}, f32[128,128]{1,0:T(8,128)}, bf16[4,4,24,384]{3,2,1,0:T(8,128)(2,1)}, bf16[4,4,24,384]{3,2,1,0:T(8,128)(2,1)}) custom-call(s32[10]{0:T(128)} %concatenate.60.sc, bf16[2,2048,1152]{2,1,0:T(8,128)(2,1)} %get-tuple-element.81.q_ref.ka_ref.kb_ref.va_ref.vb_ref, ...), custom_call_target="tpu_custom_call" | custom-call | flops 21474836480 | bytes 6291456 | tf_op jit(solution)/shard_map/attend_back/pallas_call | solution.py:358
  310.6 7.4 %far_rows.1 = (bf16[1024,768]{1,0:T(8,128)(2,1)}, bf16[1024,768]{1,0:T(8,128)(2,1)}) custom-call(bf16[2,2,256,2048]{3,2,1,0:T(8,128)(2,1)} %get-tuple-element.105.refs_0_.refs_2_, bf16[2,2,128,2048]{3,2,1,0:T(8,128)(2,1)} %get-tuple-element.111.refs_1_.refs_3_, bf16[768,1152]{1,0:T(8,128)(2,1)} %get-tuple-element.112.refs_2_.refs_4_), custom_call_target="tpu_custom_call" | custom-call | flops 2415919104 | bytes 12582912 | tf_op jit(solution)/shard_map/far_rows/pallas_call | solution.py:771
  318.2 2.3 pad_maximum_fusion
  324.5 10.0 %near_rows.1 = (f32[1024,768]{1,0:T(8,128)}, bf16[1024,768]{1,0:T(8,128)(2,1)}) custom-call(bf16[256,2048]{1,0:T(8,128)(2,1)} %get-tuple-element.117.refs_0_, bf16[128,2048]{1,0:T(8,128)(2,1)} %get-tuple-element.118.refs_1_, bf16[2,2,256,2048]{3,2,1,0:T(8,128)(2,1)} %get-tuple-element.105.refs_0_.refs_2_, ...), custom_call_target="tpu_custom_call" | custom-call | flops 3623878656 | bytes 18874368 | tf_op jit(solution)/shard_map/near_rows/pallas_call | solution.py:809
  334.5 13.7 %collective-permute-done.16 = bf16[672,768]{1,0:T(8,128)(2,1)S(1)} collective-permute-done((bf16[672,768]{1,0:T(8,128)(2,1)S(1)}, bf16[672,768]{1,0:T(8,128)(2,1)S(1)}, u32[]{:S(2)}, u32[]{:S(2)}) %collective-permute-start.16) | collective-permute-done | bytes 1032224 | tf_op jit(solution)/shard_map/ppermute | solution.py:32
  349.3 3.6 all-to-all-start
  356.3 16.4 %all-to-all-done.moved = bf16[16,32,768]{2,1,0:T(8,128)(2,1)S(1)} async-done(((bf16[16,32,768]{2,1,0:T(8,128)(2,1)}), bf16[16,32,768]{2,1,0:T(8,128)(2,1)S(1)}, u32[]{:S(2)}, u32[]{:S(2)}) %all-to-all-start) | async-done | bytes 786464 | tf_op jit(solution)/shard_map/all_to_all | solution.py:1071
  377.8 4.2 %add_bitcast_fusion = f32[1,1024,768]{2,1,0:T(8,128)} fusion(f32[1024,768]{1,0:T(8,128)} %get-tuple-element.120, bf16[1024,768]{1,0:T(8,128)(2,1)S(1)} %collective-permute-done.18, bf16[352,768]{1,0:T(8,128)(2,1)} %collective-permute-done.19, bf16[672,768]{1,0:T(8,128)(2,1)S(1)} %collective-permute-done.16), kind=kLoop, calls=%fused_computation | loop fusion | flops 5505024 | bytes 9437184 | tf_op jit(solution)/shard_map/broadcast_in_dim | solution.py:1145
  (169 shorter events, 47.1 us)
Async XLA Ops:
  7.2 135.0 %all-gather.2.cloned.1.call-start = ((), (), s32[]{:S(2)}) async-start(), calls=%async_computation.4 | async-start | bytes 10948608 | tf_op jit(solution)/shard_map/all_gather | solution.py:993
  12.6 11.3 %collective-permute-start.2 = (bf16[2,32,1152]{2,1,0:T(8,128)(2,1)S(1)}, bf16[2,32,1152]{2,1,0:T(8,128)(2,1)S(1)}, u32[]{:S(2)}, u32[]{:S(2)}) collective-permute-start(bf16[2,32,1152]{2,1,0:T(8,128)(2,1)S(1)} %pad_maximum_fusion.10), channel_id=1, source_target_pairs={{0,8},{1,9},{2,10},{3,11},{4,12},{5,13},{6,14},{7,15},{8,0},{9,1},... | collective-permute-start | bytes 442376 | tf_op jit(solution)/shard_map/ppermute | solution.py:32
  16.6 36.5 %collective-permute-start.4 = (bf16[1024,768]{1,0:T(8,128)(2,1)}, bf16[1024,768]{1,0:T(8,128)(2,1)}, u32[]{:S(2)}, u32[]{:S(2)}) collective-permute-start(bf16[1024,768]{1,0:T(8,128)(2,1)} %bitcast.1.x0.x_ref), channel_id=1, source_target_pairs={{0,1},{1,0},{2,3},{3,2},{4,5},{5,4},{6,7},{7,6},{8,9},{9,8},{10,11... | collective-permute-start | bytes 4718600 | tf_op jit(solution)/shard_map/ppermute | solution.py:32
  24.0 8.6 %collective-permute-start.3 = (bf16[2,2,32,1152]{3,2,0,1:T(8,128)(2,1)S(1)}, bf16[2,2,32,1152]{3,2,0,1:T(8,128)(2,1)S(1)}, u32[]{:S(2)}, u32[]{:S(2)}) collective-permute-start(bf16[2,2,32,1152]{3,2,0,1:T(8,128)(2,1)S(1)} %pad_maximum_fusion.9), channel_id=1, source_target_pairs={{0,4},{1,5},{2,6},{3,7},{4,0},{5,1},{6,2},{7,3},{8,12},{9,13},{10,... | collective-permute-start | bytes 884744 | tf_op jit(solution)/shard_map/ppermute | solution.py:32
  53.1 226.7 %reduce-scatter.4.cloned.1.call-start = ((), (), s32[]{:S(2)}) async-start(), calls=%async_computation.5 | async-start | bytes 6635520 | tf_op jit(solution)/shard_map/reduce_scatter | solution.py:1035
  53.2 8.0 %collective-permute-start.6 = (bf16[2,2,32,1152]{3,2,0,1:T(8,128)(2,1)S(1)}, bf16[2,2,32,1152]{3,2,0,1:T(8,128)(2,1)S(1)}, u32[]{:S(2)}, u32[]{:S(2)}) collective-permute-start(bf16[2,2,32,1152]{3,2,0,1:T(8,128)(2,1)S(1)} %get-tuple-element.168), channel_id=1, source_target_pairs={{0,2},{1,3},{2,0},{3,1},{4,6},{5,7},{6,4},{7,5},{8,10},{9,11},{10,... | collective-permute-start | bytes 884744 | tf_op jit(solution)/shard_map/ppermute | solution.py:32
  54.8 7.6 %collective-permute-start.8 = (bf16[2,2,32,1152]{3,2,0,1:T(8,128)(2,1)S(1)}, bf16[2,2,32,1152]{3,2,0,1:T(8,128)(2,1)S(1)}, u32[]{:S(2)}, u32[]{:S(2)}) collective-permute-start(bf16[2,2,32,1152]{3,2,0,1:T(8,128)(2,1)S(1)} %get-tuple-element.167), channel_id=1, source_target_pairs={{0,1},{1,0},{2,3},{3,2},{4,5},{5,4},{6,7},{7,6},{8,9},{9,8},{10,11... | collective-permute-start | bytes 884744 | tf_op jit(solution)/shard_map/ppermute | solution.py:32
  62.6 15.5 %collective-permute-start.7 = (bf16[2,2,2,32,1152]{4,3,0,1,2:T(8,128)(2,1)S(1)}, bf16[2,2,2,32,1152]{4,3,0,1,2:T(8,128)(2,1)S(1)}, u32[]{:S(2)}, u32[]{:S(2)}) collective-permute-start(bf16[2,2,2,32,1152]{4,3,0,1,2:T(8,128)(2,1)S(1)} %pad_maximum_fusion.5), channel_id=1, source_target_pairs={{0,1},{1,0},{2,3},{3,2},{4,5},{5,4},{6,7},{7,6},{8,9},{9,8},{10,11... | collective-permute-start | bytes 1769480 | tf_op jit(solution)/shard_map/ppermute | solution.py:32
  64.2 14.6 %collective-permute-start.9 = (bf16[2,2,2,32,1152]{4,3,0,1,2:T(8,128)(2,1)S(1)}, bf16[2,2,2,32,1152]{4,3,0,1,2:T(8,128)(2,1)S(1)}, u32[]{:S(2)}, u32[]{:S(2)}) collective-permute-start(bf16[2,2,2,32,1152]{4,3,0,1,2:T(8,128)(2,1)S(1)} %pad_maximum_fusion.6), channel_id=1, source_target_pairs={{0,2},{1,3},{2,0},{3,1},{4,6},{5,7},{6,4},{7,5},{8,10},{9,11},{10,... | collective-permute-start | bytes 1769480 | tf_op jit(solution)/shard_map/ppermute | solution.py:32
  64.8 17.7 %collective-permute-start = (bf16[1024,768]{1,0:T(8,128)(2,1)}, bf16[1024,768]{1,0:T(8,128)(2,1)}, u32[]{:S(2)}, u32[]{:S(2)}) collective-permute-start(bf16[1024,768]{1,0:T(8,128)(2,1)} %bitcast.1.x0.x_ref), channel_id=1, source_target_pairs={{0,16},{16,0},{1,17},{17,1},{2,18},{18,2},{3,19},{19,3},{4,20},{20... | collective-permute-start | bytes 4718600 | tf_op jit(solution)/shard_map/ppermute | solution.py:32
  64.8 17.7 %collective-permute-start.5 = (bf16[1024,768]{1,0:T(8,128)(2,1)}, bf16[1024,768]{1,0:T(8,128)(2,1)}, u32[]{:S(2)}, u32[]{:S(2)}) collective-permute-start(bf16[1024,768]{1,0:T(8,128)(2,1)} %collective-permute-done.4.x2), channel_id=1, source_target_pairs={{0,16},{16,0},{1,17},{17,1},{2,18},{18,2},{3,19},{19,3},{4,20},{20... | collective-permute-start | bytes 4718600 | tf_op jit(solution)/shard_map/ppermute | solution.py:32
  138.7 3.2 collective-permute-start.10
  188.8 8.7 %collective-permute-start.12 = (bf16[4,4,4,24,768]{4,3,2,1,0:T(8,128)(2,1)}, bf16[4,4,4,24,768]{4,3,2,1,0:T(8,128)(2,1)S(1)}, u32[]{:S(2)}, u32[]{:S(2)}) collective-permute-start(bf16[4,4,4,24,768]{4,3,2,1,0:T(8,128)(2,1)} %weight_grads.4), channel_id=1, source_target_pairs={{0,16},{16,0},{1,17},{17,1},{2,18},{18,2},{3,19},{19,3},{4,20},{20... | collective-permute-start | bytes 7077896 | tf_op jit(solution)/shard_map/ppermute | solution.py:32
  197.5 7.6 %collective-permute-start.13 = (bf16[4,4,5,24,768]{4,3,2,1,0:T(8,128)(2,1)}, bf16[4,4,5,24,768]{4,3,2,1,0:T(8,128)(2,1)S(1)}, u32[]{:S(2)}, u32[]{:S(2)}) collective-permute-start(bf16[4,4,5,24,768]{4,3,2,1,0:T(8,128)(2,1)} %weight_grads.5), channel_id=1, source_target_pairs={{0,16},{16,0},{1,17},{17,1},{2,18},{18,2},{3,19},{19,3},{4,20},{20... | collective-permute-start | bytes 8847368 | tf_op jit(solution)/shard_map/ppermute | solution.py:32
  197.7 18.0 %collective-permute-start.11 = (bf16[1024,384]{1,0:T(8,128)(2,1)}, bf16[1024,384]{1,0:T(8,128)(2,1)S(1)}, u32[]{:S(2)}, u32[]{:S(2)}) collective-permute-start(bf16[1024,384]{1,0:T(8,128)(2,1)} %get-tuple-element.88), channel_id=1, source_target_pairs={{0,16},{16,0},{1,17},{17,1},{2,18},{18,2},{3,19},{19,3},{4,20},{20... | collective-permute-start | bytes 2359304 | tf_op jit(solution)/shard_map/ppermute | solution.py:32
  216.6 101.5 %reduce-scatter.6.cloned.1.call-start = ((), (), s32[]{:S(2)}) async-start(), calls=%async_computation.6 | async-start | bytes 1474560 | tf_op jit(solution)/shard_map/reduce_scatter | solution.py:1035
  275.3 2.3 collective-permute-start.14
  279.8 75.0 %reduce-scatter.8.cloned.1.call-start = ((), (), s32[]{:S(2)}) async-start(), calls=%async_computation.7 | async-start | bytes 2027520 | tf_op jit(solution)/shard_map/reduce_scatter | solution.py:1040
  318.0 3.6 collective-permute-start.15
  323.1 25.1 %collective-permute-start.16 = (bf16[672,768]{1,0:T(8,128)(2,1)S(1)}, bf16[672,768]{1,0:T(8,128)(2,1)S(1)}, u32[]{:S(2)}, u32[]{:S(2)}) collective-permute-start(bf16[672,768]{1,0:T(8,128)(2,1)S(1)} %add_convert_fusion), channel_id=1, source_target_pairs={{0,1},{1,0},{2,3},{3,2},{4,5},{5,4},{6,7},{7,6},{8,9},{9,8},{10,11... | collective-permute-start | bytes 3096584 | tf_op jit(solution)/shard_map/ppermute | solution.py:32
  324.1 10.4 %collective-permute-start.17 = (bf16[4,4,32,384]{3,2,1,0:T(8,128)(2,1)S(1)}, bf16[4,4,32,384]{3,2,1,0:T(8,128)(2,1)S(1)}, u32[]{:S(2)}, u32[]{:S(2)}) collective-permute-start(bf16[4,4,32,384]{3,2,1,0:T(8,128)(2,1)S(1)} %pad_maximum_fusion.7), channel_id=1, source_target_pairs={{0,16},{16,0},{1,17},{17,1},{2,18},{18,2},{3,19},{19,3},{4,20},{20... | collective-permute-start | bytes 1179656 | tf_op jit(solution)/shard_map/ppermute | solution.py:32
  349.3 23.4 %all-to-all-start = ((bf16[16,32,768]{2,1,0:T(8,128)(2,1)}), bf16[16,32,768]{2,1,0:T(8,128)(2,1)S(1)}, u32[]{:S(2)}, u32[]{:S(2)}) async-start(bf16[16,32,768]{2,1,0:T(8,128)(2,1)} %bitcast.61), calls=%async_computation.3 | async-start | bytes 1572864 | tf_op jit(solution)/shard_map/all_to_all | solution.py:1071
  354.8 23.0 %collective-permute-start.18 = (bf16[1024,768]{1,0:T(8,128)(2,1)}, bf16[1024,768]{1,0:T(8,128)(2,1)S(1)}, u32[]{:S(2)}, u32[]{:S(2)}) collective-permute-start(bf16[1024,768]{1,0:T(8,128)(2,1)} %get-tuple-element.130), channel_id=1, source_target_pairs={{0,16},{16,0},{1,17},{17,1},{2,18},{18,2},{3,19},{19,3},{4,20},{20... | collective-permute-start | bytes 4718600 | tf_op jit(solution)/shard_map/ppermute | solution.py:32
  354.8 23.0 %collective-permute-start.19 = (bf16[352,768]{1,0:T(8,128)(2,1)}, bf16[352,768]{1,0:T(8,128)(2,1)}, u32[]{:S(2)}, u32[]{:S(2)}) collective-permute-start(bf16[352,768]{1,0:T(8,128)(2,1)} %add_convert_fusion.1), channel_id=1, source_target_pairs={{0,1},{1,0},{2,3},{3,2},{4,5},{5,4},{6,7},{7,6},{8,9},{9,8},{10,11... | collective-permute-start | bytes 1622024 | tf_op jit(solution)/shard_map/ppermute | solution.py:32
  (20 other events, 168.5 us)
Sparse Core Ops, SparseCore 0:
  53.2 89.0 all-gather.1
  215.9 59.3 reduce-scatter.3
  280.0 26.7 reduce-scatter.5
  320.6 34.1 reduce-scatter.7

commit v5 on v4

--- a/solution.py
+++ b/solution.py
@@ -45,8 +45,7 @@
     for bit in bits[:-2]:
         held = place(held, swap(held, "blk", bit), (index & bit) != 0, depth)
         depth += 1
-    if GATE >= 4:
-        held, also = lax.optimization_barrier((held, also))
+    held, also = lax.optimization_barrier((held, also))
     first, second = held[0], held[1]
     depth -= 1
     high, low = bits[-2], bits[-1]
@@ -121,7 +120,7 @@
 
     def finish(outs, peaks):
         totals = [jnp.broadcast_to(o[HD : HD + 1, :], (HD, rows)) for o in outs]
-        out = jnp.concatenate([o[:HD, :] / t for o, t in zip(outs, totals)], axis=0).T.astype(BF16)
+        out = jnp.concatenate([o[:HD, :] / t for o, t in zip(outs, totals)], axis=0).astype(BF16).T
         mine = pl.program_id(1) < pl.num_programs(1) // 2
 
         @pl.when(mine)
@@ -132,10 +131,11 @@
         def _():
             sib_ref[...] = out
 
-        lse = jnp.concatenate([jnp.log(totals[1]), jnp.log(totals[0])], axis=0).T
-        if peaks is not None:
-            lse = lse + jnp.where(own0, peaks[1], peaks[0])
-        lse_ref[...] = lse
+        for h in (0, 1):
+            lse = jnp.log(outs[h][HD : HD + 1, :])
+            if peaks is not None:
+                lse = lse + jnp.broadcast_to(peaks[h], (rows, LANES)).T[:1, :]
+            lse_ref[h : h + 1, :] = lse
 
     @pl.when(small)
     def _():
@@ -178,7 +178,6 @@
 def attend(sc, qkv, width):
     count = qkv.shape[1]
     rows = min(1024, count // 2)
-    row_spec = pl.BlockSpec((rows, LANES), lambda p, i, sc: (i, p))
     q_spec = pl.BlockSpec((1, rows, LANES), lambda p, i, sc: (0, i, p))
     heads = width // HD
     return pl.pallas_call(
@@ -187,7 +186,7 @@
             num_scalar_prefetch=1,
             grid=(width // LANES, count // rows),
             in_specs=[q_spec] + pair_specs(count, width),
-            out_specs=halves_specs(rows, count // rows) + [row_spec],
+            out_specs=halves_specs(rows, count // rows) + [pl.BlockSpec((8, rows), lambda p, i, sc: (p, i))],
             scratch_shapes=[
                 pltpu.VMEM((2, count, LANES), BF16),
                 pltpu.VMEM((2, HD + 16, count), BF16),
@@ -197,7 +196,7 @@
         out_shape=[
             jax.ShapeDtypeStruct((count // 2, width), BF16),
             jax.ShapeDtypeStruct((count // 2, width), BF16),
-            jax.ShapeDtypeStruct((count, width), F32),
+            jax.ShapeDtypeStruct((8 * width // LANES, count), F32),
         ],
         compiler_params=pltpu.CompilerParams(vmem_limit_bytes=VMEM_BYTES),
         cost_estimate=pl.CostEstimate(
@@ -234,6 +233,8 @@
     dk_sum,
     dv_sum,
     dq_all,
+    tokens,
+    sem,
     *,
     heads,
     step,
@@ -244,6 +245,18 @@
     count = keys.shape[1]
     rows = q_ref.shape[1]
     scale = HD ** (-0.5)
+
+    copies = [pltpu.make_async_copy(ref, tokens.at[i], sem.at[i]) for i, ref in enumerate((x0, x1, x2, x3))]
+
+    @pl.when(jnp.logical_and(pl.program_id(0) == 0, block == 0))
+    def _():
+        for copy in copies:
+            copy.start()
+
+    @pl.when(jnp.logical_and(pl.program_id(0) == 0, block == pl.num_programs(1) - 1))
+    def _():
+        for copy in copies:
+            copy.wait()
 
     @pl.when(block == 0)
     def _():
@@ -268,7 +281,8 @@
     out = jnp.where(mine, o_own[...], o_sib[...])
     own0, sub = first_head(rows)
     qf = q.astype(F32) * scale
-    first, second, third = three_parts(lse_ref[...])
+    lse = lse_ref[...].T
+    first, second, third = three_parts(jnp.where(own0, lse[:, 1:2], lse[:, 0:1]))
     q_extra = jnp.where(
         sub == 0, first, jnp.where(sub == 1, second, jnp.where(sub == 2, third, jnp.where(sub == 3, 1.0, 0.0)))
     )
@@ -319,11 +333,11 @@
                 dkv_ref[half, 0, own_rows, :] = jnp.where(here, dk, 0.0).astype(BF16)
                 dkv_ref[half, 1, own_rows, :] = jnp.where(here, dv, 0.0).astype(BF16)
 
-        local = x0.shape[0]
+        local = tokens.shape[1]
         near = jnp.concatenate([dq_all[...], dkv_ref[0, 0], dkv_ref[0, 1]], axis=0)
         far = jnp.concatenate([dkv_ref[1, 0], dkv_ref[1, 1]], axis=0)
-        near = dot(near[:, :local], x0[...]) + dot(near[:, local:], x1[...])
-        far = dot(far[:, :local], x2[...]) + dot(far[:, local:], x3[...])
+        near = dot(near[:, :local], tokens[0]) + dot(near[:, local:], tokens[1])
+        far = dot(far[:, :local], tokens[2]) + dot(far[:, local:], tokens[3])
         grad = jnp.concatenate([near[:LANES], near[LANES:] + far], axis=0).T.astype(BF16)
         inner, outer, unit, _ = keep_ref.shape
         half_rows = grad.shape[0] // 2
@@ -345,12 +359,12 @@
 def attend_back(sc, qkv, contexts, lse, grads, pieces, width, skip, pairs, inner, outer):
     model = pieces[0].shape[1]
     unit = model // (2 * inner * outer)
-    piece = pl.BlockSpec(pieces[0].shape, lambda p, i, sc: (0, 0), pipeline_mode=pl.Buffered(1))
+    piece = pl.BlockSpec(memory_space=pl.ANY)
     grad_spec = pl.BlockSpec((inner, outer, unit, 3 * LANES), lambda p, i, sc: (0, 0, 0, p))
     grad_shape = jax.ShapeDtypeStruct((inner, outer, unit, 3 * pairs * LANES), BF16)
     count = qkv.shape[1]
     rows = min(1024, count // 2)
-    row_spec = pl.BlockSpec((rows, LANES), lambda p, i, sc: (i, p + skip))
+    lse_spec = pl.BlockSpec((8, rows), lambda p, i, sc: (p + skip, i))
     q_spec = pl.BlockSpec((1, rows, LANES), lambda p, i, sc: (0, i, p + skip))
     dq_spec = pl.BlockSpec((LANES, rows), lambda p, i, sc: (p, i))
     dkv_spec = pl.BlockSpec((2, 2, LANES, count), lambda p, i, sc: (0, 0, p, 0))
@@ -361,7 +375,7 @@
             num_scalar_prefetch=1,
             grid=(pairs, count // rows),
             in_specs=[q_spec] + pair_specs(count, width, skip) + halves_specs(rows, count // rows, skip) * 2
-            + [row_spec]
+            + [lse_spec]
             + [piece] * 4,
             out_specs=[
                 dq_spec,
@@ -377,6 +391,8 @@
                 pltpu.VMEM((LANES, count), F32),
                 pltpu.VMEM((LANES, count), F32),
                 pltpu.VMEM((LANES, count), BF16),
+                pltpu.VMEM((4,) + pieces[0].shape, BF16),
+                pltpu.SemaphoreType.DMA((4,)),
             ],
         ),
         out_shape=[
@@ -641,7 +657,7 @@
             ),
             out_shape=jax.ShapeDtypeStruct((inner, outer, slots, unit, width), BF16),
             input_output_aliases=aliases,
-            compiler_params=pltpu.CompilerParams(vmem_limit_bytes=VMEM_BYTES),
+            compiler_params=pltpu.CompilerParams(vmem_limit_bytes=26 << 20),
             cost_estimate=pl.CostEstimate(flops=flops, bytes_accessed=3 * flops // width, transcendentals=0),
             name="weight_grads",
         )(core, *args, *came)
@@ -881,11 +897,6 @@
         out_shape=outs,
         name="unpack",
     )(core, chip, moved)
-
-
-GATE = 4
-SHARES = (21,)
-ORDER = 0
 
 
 def unpacked(blocks, parts):
@@ -984,12 +995,7 @@
     shard = jnp.concatenate(
         [w_back, w_in.reshape(rows, parts, width).transpose(1, 0, 2).reshape(parts * rows, width), w_out], axis=0
     )
-    if GATE in (1, 4):
-        shard, x_far = lax.optimization_barrier((shard, x_far))
-    elif GATE in (2, 6):
-        shard, first = lax.optimization_barrier((shard, first))
-    elif GATE == 3:
-        shard, first, x_far = lax.optimization_barrier((shard, first, x_far))
+    shard, x_far = lax.optimization_barrier((shard, x_far))
     gathered = lax.all_gather(shard, both, axis=0, tiled=True).reshape(cores * blocks, -1, width)
     direct = rows % 8 == 0 and blocks % 4 == 0 and (2 * blocks) % (4 * parts) == 0
     if direct:
@@ -1082,13 +1088,16 @@
     if direct:
         part_a = jnp.concatenate([keep_a, came_a], axis=2)
         grad_context, part_a, chip = lax.optimization_barrier((grad_context, part_a, chip))
-        chip = over_column(jnp.concatenate([chip, over_plane(part_a)], axis=1))
+        part_a = over_plane(part_a)
     else:
         total_a = total_of(finish_part(keep_a, came_a))
     dq_b, dkv_b, sum_b, *grad_b = attend_back(
         sc, qkv, contexts, lse, grad_context, pieces, group, first_pairs, pairs - first_pairs, inner, outer
     )
 
+    if direct:
+        part_a, sum_b = lax.optimization_barrier((part_a, sum_b))
+        chip = over_column(jnp.concatenate([chip, part_a], axis=1))
     q_sums = jnp.sum(jnp.concatenate([sum_a, sum_b], axis=0), axis=1)
     q_sums = lax.dynamic_update_slice_in_dim(jnp.zeros((width,), F32), q_sums, core * group, 0)
     grad_small = jnp.concatenate([q_sums.reshape(cores, blocks, rows), early_small], axis=2)
@@ -1104,20 +1113,14 @@
     keep_b, came_b = part_rows(*grad_b, small_rows)
     keep_far, send_far = far_rows(dkv, weight)
     far_sib = swap(send_far, "head", 1)
-    cuts = [0, *(local * share // 32 for share in SHARES), local]
-    far_sums = [
-        (keep_far[lo:hi].astype(F32) + far_sib[lo:hi].astype(F32)).astype(BF16)
-        for lo, hi in zip(cuts, cuts[1:])
-    ]
-    far_sums, dq_a, dq_b = lax.optimization_barrier((far_sums, dq_a, dq_b))
-    far_in = [swap(part, "blk", 1) for part in far_sums]
+    far_sum = (keep_far.astype(F32) + far_sib.astype(F32)).astype(BF16)
+    moved_b = finish_part(keep_b, came_b)
+    far_sum, dq_a, dq_b = lax.optimization_barrier((far_sum, dq_a, dq_b))
+    far_in = swap(far_sum, "blk", 1)
     keep_near, send_near = near_rows((dq_a, dq_b), dkv, weight, grad_resid1)
-    if ORDER == 0:
-        far_in[0], came_b, send_near = lax.optimization_barrier((far_in[0], came_b, send_near))
-    moved_b = finish_part(keep_b, came_b)
     chip, send_near = lax.optimization_barrier((chip, send_near))
     near_sib = swap(send_near, "head", 1)
-    grad_tokens = keep_near + near_sib.astype(F32) + jnp.concatenate(far_in, axis=0).astype(F32)
+    grad_tokens = keep_near + near_sib.astype(F32) + far_in.astype(F32)
 
     if direct:
         sum_wback, sum_win, sum_wout, sum_wqkv, vectors = unpack(at_core, chip, moved_b, rows, parts)

time: 395 us -> 386 us (0.977)
  Pallas kernels: 231 us -> 215 us
    all_to_all x1, waiting for transfers between devices: 16.4 us -> 1.11 us  [finish_part(): return lax.all_to_all(both_cores, 'blk', 0, 0, tiled=True)]
    reduce_scatter x1, waiting for transfers between devices: 1.92 us -> 15.8 us  [over_column(): lax.psum_scatter(flat, 'blk', scatter_dimension=0, axis_index_groups=far_...]
    pallas_call x4, Pallas kernels: 29.3 us -> 16.9 us  [call(): pl.pallas_call(kernel, grid_spec=pltpu.PrefetchScalarGridSpec(num_scalar_...]
    unnamed x40 -> x60, local copies, waits for them, and re-layouts: 6.05 us -> 9.37 us
    ppermute x20 -> x19, waiting for transfers between devices: 69.9 us -> 68.3 us  [swap(): return lax.ppermute(value, axis, pairs)]
    ppermute x20 -> x19, starting transfers between devices: 16.3 us -> 16.3 us  [swap(): return lax.ppermute(value, axis, pairs)]
  transfers between devices with their start and end apart: 25 -> 24, of which waited for: 15 -> 16; matrix products, arithmetic and copies ran while one was open for 5% -> 5% of each run, Pallas kernels for 48% -> 45%
where the time goes in v5:
time: 386 us; the launch traced here: 379 us
  Pallas kernels  215 us (56%)
  waiting for transfers between devices  87.6 us (23%)
  starting transfers between devices  21.2 us (5%)
  local copies, waits for them, and re-layouts  20.4 us (5%)
  other arithmetic  18.3 us (5%)
  between operations  16.2 us (4%)
    pallas_call x2, Pallas kernels, attend_back(): pl.pallas_call(functools.partial(attend_back_kernel, heads=heads, step=mi...  85.4 us
    ppermute x19, waiting for transfers between devices, swap(): return lax.ppermute(value, axis, pairs)  68.3 us
    pallas_call x1, Pallas kernels, middle(): pl.pallas_call(functools.partial(middle_kernel, width=width, ff=ff), grid...  40.1 us
    pallas_call x1, Pallas kernels, attend(): pl.pallas_call(functools.partial(attend_kernel, heads=heads, step=min(512...  39.2 us
    pallas_call x4, Pallas kernels, call(): pl.pallas_call(kernel, grid_spec=pltpu.PrefetchScalarGridSpec(num_scalar_...  16.9 us
    ppermute x19, starting transfers between devices, swap(): return lax.ppermute(value, axis, pairs)  16.3 us
    reduce_scatter x1, waiting for transfers between devices, over_column(): lax.psum_scatter(flat, 'blk', scatter_dimension=0, axis_index_groups=far_...  15.8 us
    pallas_call x1, Pallas kernels, project(): pl.pallas_call(functools.partial(project_kernel, group=wide // 3), grid=(...  14.4 us
  transfers between devices with their start and end apart: 24, of which 16 were waited for; matrix products, arithmetic and copies ran while one was open for 5% of the time, Pallas kernels for 45%

profile of v5, /device:TPU:0, one launch (start us, length us, event | category | flops | bytes accessed | tf_op | source)
XLA Modules:
  0.0 379.1 jit_solution(4695970595553805845)
XLA Ops:
  12.6 4.0 %collective-permute-start.2 = (bf16[2,32,1152]{2,1,0:T(8,128)(2,1)S(1)}, bf16[2,32,1152]{2,1,0:T(8,128)(2,1)S(1)}, u32[]{:S(2)}, u32[]{:S(2)}) collective-permute-start(bf16[2,32,1152]{2,1,0:T(8,128)(2,1)S(1)} %pad_maximum_fusion.10), channel_id=1, source_target_pairs={{0,8},{1,9},{2,10},{3,11},{4,12},{5,13},{6,14},{7,15},{8,0},{9,1},... | collective-permute-start | bytes 442376 | tf_op jit(solution)/shard_map/ppermute | solution.py:32
  18.1 5.8 %collective-permute-done.2 = bf16[2,32,1152]{2,1,0:T(8,128)(2,1)S(1)} collective-permute-done((bf16[2,32,1152]{2,1,0:T(8,128)(2,1)S(1)}, bf16[2,32,1152]{2,1,0:T(8,128)(2,1)S(1)}, u32[]{:S(2)}, u32[]{:S(2)}) %collective-permute-start.2) | collective-permute-done | bytes 147488 | tf_op jit(solution)/shard_map/ppermute | solution.py:32
  25.6 7.0 %collective-permute-done.3 = bf16[2,2,32,1152]{3,2,0,1:T(8,128)(2,1)S(1)} collective-permute-done((bf16[2,2,32,1152]{3,2,0,1:T(8,128)(2,1)S(1)}, bf16[2,2,32,1152]{3,2,0,1:T(8,128)(2,1)S(1)}, u32[]{:S(2)}, u32[]{:S(2)}) %collective-permute-start.3) | collective-permute-done | bytes 294944 | tf_op jit(solution)/shard_map/ppermute | solution.py:32
  32.7 20.3 %collective-permute-done.4.x2 = bf16[1024,768]{1,0:T(8,128)(2,1)} collective-permute-done((bf16[1024,768]{1,0:T(8,128)(2,1)}, bf16[1024,768]{1,0:T(8,128)(2,1)}, u32[]{:S(2)}, u32[]{:S(2)}) %collective-permute-start.4) | collective-permute-done | bytes 1572896 | tf_op jit(solution)/shard_map/ppermute | solution.py:32
  56.3 4.9 %collective-permute-done.6 = bf16[2,2,32,1152]{3,2,0,1:T(8,128)(2,1)S(1)} collective-permute-done((bf16[2,2,32,1152]{3,2,0,1:T(8,128)(2,1)S(1)}, bf16[2,2,32,1152]{3,2,0,1:T(8,128)(2,1)S(1)}, u32[]{:S(2)}, u32[]{:S(2)}) %collective-permute-start.6) | collective-permute-done | bytes 294944 | tf_op jit(solution)/shard_map/ppermute | solution.py:32
  68.0 10.1 %collective-permute-done.7 = bf16[2,2,2,32,1152]{4,3,0,1,2:T(8,128)(2,1)S(1)} collective-permute-done((bf16[2,2,2,32,1152]{4,3,0,1,2:T(8,128)(2,1)S(1)}, bf16[2,2,2,32,1152]{4,3,0,1,2:T(8,128)(2,1)S(1)}, u32[]{:S(2)}, u32[]{:S(2)}) %collective-permute-start.7) | collective-permute-done | bytes 589856 | tf_op jit(solution)/shard_map/ppermute | solution.py:32
  82.6 14.4 %project.1 = (bf16[2,2048,1152]{2,1,0:T(8,128)(2,1)}, bf16[768,1152]{1,0:T(8,128)(2,1)}) custom-call(bf16[1024,768]{1,0:T(8,128)(2,1)} %bitcast.1.x0.x_ref, bf16[1024,768]{1,0:T(8,128)(2,1)} %collective-permute-done.x1, bf16[1024,768]{1,0:T(8,128)(2,1)} %collective-permute-done.4.x2, bf16[1024,768]{1,0:T(8,128)(2,1)} %collective-permute-done.5.x3, ...), custom_call_target="tpu_custom_call" | custom-call | flops 7247757312 | bytes 15728640 | tf_op jit(solution)/shard_map/project/pallas_call | solution.py:741
  97.0 39.2 %attend.1 = (bf16[1024,384]{1,0:T(8,128)(2,1)}, bf16[1024,384]{1,0:T(8,128)(2,1)}, f32[24,2048]{1,0:T(8,128)}) custom-call(s32[10]{0:T(128)} %concatenate.57.sc, bf16[2,2048,1152]{2,1,0:T(8,128)(2,1)} %get-tuple-element.79.q_ref.ka_ref.kb_ref.va_ref.vb_ref, bf16[2,2048,1152]{2,1,0:T(8,128)(2,1)} %get-tuple-element.79.q_ref.ka_ref.kb_ref.va_ref.vb_ref, ...), custom_call_target="tpu_custom_call" | custom-call | flops 25769803776 | bytes 9437184 | tf_op jit(solution)/shard_map/attend/pallas_call | solution.py:183
  141.6 40.1 %middle.1 = (bf16[1024,768]{1,0:T(8,128)(2,1)}, f32[1024,768]{1,0:T(8,128)}, bf16[1024,384]{1,0:T(8,128)(2,1)}, bf16[1024,384]{1,0:T(8,128)(2,1)}, bf16[1024,768...) custom-call(s32[1]{0:T(128)} %bitcast.core, ...), custom_call_target="tpu_custom_call" | custom-call | flops 21743271936 | bytes 44040192 | tf_op jit(solution)/shard_map/middle/pallas_call | solution.py:549
  181.7 2.8 copy-done.3
  185.9 3.3 weight_grads.4
  189.8 5.0 %weight_grads.5 = bf16[4,4,5,24,768]{4,3,2,1,0:T(8,128)(2,1)S(1)} custom-call(s32[1]{0:T(128)} %bitcast.core, bf16[1024,768]{1,0:T(8,128)(2,1)S(1)} %copy-done.5, bf16[1024,3072]{1,0:T(8,128)(2,1)S(1)} %copy-done.4, bf16[1024,384]{1,0:T(8,128)(2,1)S(1)} %copy-done.11, bf16[1024,768]{1,0:T(8,128)(2,1)S(1)} %copy-done.6), custom_call_target="tpu_custom_call" | custom-call | flops 3019898880 | bytes 11796480 | tf_op jit(solution)/shard_map/weight_grads/pallas_call | solution.py:653
  195.4 3.5 weight_grads.6.refs_1_
  200.2 5.2 %weight_grads.7 = bf16[4,4,9,24,768]{4,3,2,1,0:T(8,128)(2,1)S(1)} custom-call(s32[1]{0:T(128)} %bitcast.core, bf16[1024,768]{1,0:T(8,128)(2,1)S(1)} %copy-done.5, bf16[1024,3072]{1,0:T(8,128)(2,1)S(1)} %copy-done.4, bf16[1024,384]{1,0:T(8,128)(2,1)S(1)} %copy-done.9, bf16[1024,768]{1,0:T(8,128)(2,1)S(1)} %copy-done.6, ...), custom_call_target="tpu_custom_call", output_to_operand_aliasing={{}: (6, {})} | custom-call | flops 3019898880 | bytes 11796480 | tf_op jit(solution)/shard_map/weight_grads/pallas_call | solution.py:653
  212.3 55.5 %attend_back.2 = (bf16[256,2048]{1,0:T(8,128)(2,1)}, bf16[2,2,256,2048]{3,2,1,0:T(8,128)(2,1)}, f32[256,128]{1,0:T(8,128)}, bf16[4,4,24,768]{3,2,1,0:T(8,128)(2,1)}, bf16[4,4,24,768]{3,2,1,0:T(8,128)(2,1)}) custom-call(s32[10]{0:T(128)} %concatenate.57.sc, bf16[2,2048,1152]{2,1,0:T(8,128)(2,1)} %get-tuple-element.79.q_ref.ka_ref.kb_ref.va_ref.vb_ref, ...), custom_call_target="tpu_custom_call" | custom-call | flops 42949672960 | bytes 12582912 | tf_op jit(solution)/shard_map/attend_back/pallas_call | solution.py:372
  272.4 29.9 %attend_back.3 = (bf16[128,2048]{1,0:T(8,128)(2,1)}, bf16[2,2,128,2048]{3,2,1,0:T(8,128)(2,1)}, f32[128,128]{1,0:T(8,128)}, bf16[4,4,24,384]{3,2,1,0:T(8,128)(2,1)}, bf16[4,4,24,384]{3,2,1,0:T(8,128)(2,1)}) custom-call(s32[10]{0:T(128)} %concatenate.57.sc, bf16[2,2048,1152]{2,1,0:T(8,128)(2,1)} %get-tuple-element.79.q_ref.ka_ref.kb_ref.va_ref.vb_ref, ...), custom_call_target="tpu_custom_call" | custom-call | flops 21474836480 | bytes 6291456 | tf_op jit(solution)/shard_map/attend_back/pallas_call | solution.py:372
  304.6 7.3 %far_rows.1 = (bf16[1024,768]{1,0:T(8,128)(2,1)}, bf16[1024,768]{1,0:T(8,128)(2,1)}) custom-call(bf16[2,2,256,2048]{3,2,1,0:T(8,128)(2,1)} %get-tuple-element.103.refs_0_.refs_2_, bf16[2,2,128,2048]{3,2,1,0:T(8,128)(2,1)} %get-tuple-element.109.refs_1_.refs_3_, bf16[768,1152]{1,0:T(8,128)(2,1)} %get-tuple-element.110.refs_2_.refs_4_), custom_call_target="tpu_custom_call" | custom-call | flops 2415919104 | bytes 12582912 | tf_op jit(solution)/shard_map/far_rows/pallas_call | solution.py:787
  313.5 2.5 collective-permute-done.18
  317.0 4.7 %all-to-all-start = ((bf16[16,32,768]{2,1,0:T(8,128)(2,1)}), bf16[16,32,768]{2,1,0:T(8,128)(2,1)S(1)}, u32[]{:S(2)}, u32[]{:S(2)}) async-start(bf16[16,32,768]{2,1,0:T(8,128)(2,1)} %bitcast.61), calls=%async_computation.3 | async-start | bytes 1572864 | tf_op jit(solution)/shard_map/all_to_all | solution.py:1077
  321.8 3.0 add_convert_fusion
  326.7 9.9 %near_rows.1 = (f32[1024,768]{1,0:T(8,128)}, bf16[1024,768]{1,0:T(8,128)(2,1)}) custom-call(bf16[256,2048]{1,0:T(8,128)(2,1)} %get-tuple-element.115.refs_0_, bf16[128,2048]{1,0:T(8,128)(2,1)} %get-tuple-element.116.refs_1_, bf16[2,2,256,2048]{3,2,1,0:T(8,128)(2,1)} %get-tuple-element.103.refs_0_.refs_2_, ...), custom_call_target="tpu_custom_call" | custom-call | flops 3623878656 | bytes 18874368 | tf_op jit(solution)/shard_map/near_rows/pallas_call | solution.py:825
  336.6 15.8 %reduce-scatter.8.cloned.1.call-done.chip = bf16[264,768]{1,0:T(8,128)(2,1)} async-done(((bf16[1056,768]{1,0:T(8,128)(2,1)}), bf16[264,768]{1,0:T(8,128)(2,1)}) %reduce-scatter.8.cloned.1.call-update) | async-done | bytes 405520 | tf_op jit(solution)/shard_map/reduce_scatter | solution.py:1046
  358.6 9.0 %collective-permute-done.17 = bf16[1024,768]{1,0:T(8,128)(2,1)S(1)} collective-permute-done((bf16[1024,768]{1,0:T(8,128)(2,1)}, bf16[1024,768]{1,0:T(8,128)(2,1)S(1)}, u32[]{:S(2)}, u32[]{:S(2)}) %collective-permute-start.17) | collective-permute-done | bytes 1572896 | tf_op jit(solution)/shard_map/ppermute | solution.py:32
  367.6 4.5 %add_bitcast_fusion = f32[1,1024,768]{2,1,0:T(8,128)} fusion(bf16[1024,768]{1,0:T(8,128)(2,1)S(1)} %collective-permute-done.17, f32[1024,768]{1,0:T(8,128)} %get-tuple-element.118, bf16[1024,768]{1,0:T(8,128)(2,1)} %collective-permute-done.16), kind=kLoop, calls=%fused_computation | loop fusion | flops 3145728 | bytes 9437184 | tf_op jit(solution)/shard_map/broadcast_in_dim | solution.py:1148
  (187 shorter events, 55.3 us)
Async XLA Ops:
  7.2 134.4 %all-gather.2.cloned.1.call-start = ((), (), s32[]{:S(2)}) async-start(), calls=%async_computation.4 | async-start | bytes 10948608 | tf_op jit(solution)/shard_map/all_gather | solution.py:999
  10.5 1.4 collective-permute-start.1
  12.6 11.3 %collective-permute-start.2 = (bf16[2,32,1152]{2,1,0:T(8,128)(2,1)S(1)}, bf16[2,32,1152]{2,1,0:T(8,128)(2,1)S(1)}, u32[]{:S(2)}, u32[]{:S(2)}) collective-permute-start(bf16[2,32,1152]{2,1,0:T(8,128)(2,1)S(1)} %pad_maximum_fusion.10), channel_id=1, source_target_pairs={{0,8},{1,9},{2,10},{3,11},{4,12},{5,13},{6,14},{7,15},{8,0},{9,1},... | collective-permute-start | bytes 442376 | tf_op jit(solution)/shard_map/ppermute | solution.py:32
  16.6 36.5 %collective-permute-start.4 = (bf16[1024,768]{1,0:T(8,128)(2,1)}, bf16[1024,768]{1,0:T(8,128)(2,1)}, u32[]{:S(2)}, u32[]{:S(2)}) collective-permute-start(bf16[1024,768]{1,0:T(8,128)(2,1)} %bitcast.1.x0.x_ref), channel_id=1, source_target_pairs={{0,1},{1,0},{2,3},{3,2},{4,5},{5,4},{6,7},{7,6},{8,9},{9,8},{10,11... | collective-permute-start | bytes 4718600 | tf_op jit(solution)/shard_map/ppermute | solution.py:32
  24.0 8.6 %collective-permute-start.3 = (bf16[2,2,32,1152]{3,2,0,1:T(8,128)(2,1)S(1)}, bf16[2,2,32,1152]{3,2,0,1:T(8,128)(2,1)S(1)}, u32[]{:S(2)}, u32[]{:S(2)}) collective-permute-start(bf16[2,2,32,1152]{3,2,0,1:T(8,128)(2,1)S(1)} %pad_maximum_fusion.9), channel_id=1, source_target_pairs={{0,4},{1,5},{2,6},{3,7},{4,0},{5,1},{6,2},{7,3},{8,12},{9,13},{10,... | collective-permute-start | bytes 884744 | tf_op jit(solution)/shard_map/ppermute | solution.py:32
  53.1 219.2 %reduce-scatter.4.cloned.1.call-start = ((), (), s32[]{:S(2)}) async-start(), calls=%async_computation.5 | async-start | bytes 6635520 | tf_op jit(solution)/shard_map/reduce_scatter | solution.py:1041
  53.2 8.0 %collective-permute-start.6 = (bf16[2,2,32,1152]{3,2,0,1:T(8,128)(2,1)S(1)}, bf16[2,2,32,1152]{3,2,0,1:T(8,128)(2,1)S(1)}, u32[]{:S(2)}, u32[]{:S(2)}) collective-permute-start(bf16[2,2,32,1152]{3,2,0,1:T(8,128)(2,1)S(1)} %get-tuple-element.164), channel_id=1, source_target_pairs={{0,2},{1,3},{2,0},{3,1},{4,6},{5,7},{6,4},{7,5},{8,10},{9,11},{10,... | collective-permute-start | bytes 884744 | tf_op jit(solution)/shard_map/ppermute | solution.py:32
  54.8 7.6 %collective-permute-start.8 = (bf16[2,2,32,1152]{3,2,0,1:T(8,128)(2,1)S(1)}, bf16[2,2,32,1152]{3,2,0,1:T(8,128)(2,1)S(1)}, u32[]{:S(2)}, u32[]{:S(2)}) collective-permute-start(bf16[2,2,32,1152]{3,2,0,1:T(8,128)(2,1)S(1)} %get-tuple-element.163), channel_id=1, source_target_pairs={{0,1},{1,0},{2,3},{3,2},{4,5},{5,4},{6,7},{7,6},{8,9},{9,8},{10,11... | collective-permute-start | bytes 884744 | tf_op jit(solution)/shard_map/ppermute | solution.py:32
  62.6 15.5 %collective-permute-start.7 = (bf16[2,2,2,32,1152]{4,3,0,1,2:T(8,128)(2,1)S(1)}, bf16[2,2,2,32,1152]{4,3,0,1,2:T(8,128)(2,1)S(1)}, u32[]{:S(2)}, u32[]{:S(2)}) collective-permute-start(bf16[2,2,2,32,1152]{4,3,0,1,2:T(8,128)(2,1)S(1)} %pad_maximum_fusion.5), channel_id=1, source_target_pairs={{0,1},{1,0},{2,3},{3,2},{4,5},{5,4},{6,7},{7,6},{8,9},{9,8},{10,11... | collective-permute-start | bytes 1769480 | tf_op jit(solution)/shard_map/ppermute | solution.py:32
  64.2 14.6 %collective-permute-start.9 = (bf16[2,2,2,32,1152]{4,3,0,1,2:T(8,128)(2,1)S(1)}, bf16[2,2,2,32,1152]{4,3,0,1,2:T(8,128)(2,1)S(1)}, u32[]{:S(2)}, u32[]{:S(2)}) collective-permute-start(bf16[2,2,2,32,1152]{4,3,0,1,2:T(8,128)(2,1)S(1)} %pad_maximum_fusion.6), channel_id=1, source_target_pairs={{0,2},{1,3},{2,0},{3,1},{4,6},{5,7},{6,4},{7,5},{8,10},{9,11},{10,... | collective-permute-start | bytes 1769480 | tf_op jit(solution)/shard_map/ppermute | solution.py:32
  64.8 17.7 %collective-permute-start = (bf16[1024,768]{1,0:T(8,128)(2,1)}, bf16[1024,768]{1,0:T(8,128)(2,1)}, u32[]{:S(2)}, u32[]{:S(2)}) collective-permute-start(bf16[1024,768]{1,0:T(8,128)(2,1)} %bitcast.1.x0.x_ref), channel_id=1, source_target_pairs={{0,16},{16,0},{1,17},{17,1},{2,18},{18,2},{3,19},{19,3},{4,20},{20... | collective-permute-start | bytes 4718600 | tf_op jit(solution)/shard_map/ppermute | solution.py:32
  64.8 17.7 %collective-permute-start.5 = (bf16[1024,768]{1,0:T(8,128)(2,1)}, bf16[1024,768]{1,0:T(8,128)(2,1)}, u32[]{:S(2)}, u32[]{:S(2)}) collective-permute-start(bf16[1024,768]{1,0:T(8,128)(2,1)} %collective-permute-done.4.x2), channel_id=1, source_target_pairs={{0,16},{16,0},{1,17},{17,1},{2,18},{18,2},{3,19},{19,3},{4,20},{20... | collective-permute-start | bytes 4718600 | tf_op jit(solution)/shard_map/ppermute | solution.py:32
  136.1 3.1 collective-permute-start.10
  189.2 5.6 %collective-permute-start.12 = (bf16[4,4,4,24,768]{4,3,2,1,0:T(8,128)(2,1)S(1)}, bf16[4,4,4,24,768]{4,3,2,1,0:T(8,128)(2,1)S(1)}, u32[]{:S(2)}, u32[]{:S(2)}) collective-permute-start(bf16[4,4,4,24,768]{4,3,2,1,0:T(8,128)(2,1)S(1)} %weight_grads.4), channel_id=1, source_target_pairs={{0,16},{16,0},{1,17},{17,1},{2,18},{18,2},{3,19},{19,3},{4,20},{20... | collective-permute-start | bytes 7077896 | tf_op jit(solution)/shard_map/ppermute | solution.py:32
  194.8 5.4 %collective-permute-start.13 = (bf16[4,4,5,24,768]{4,3,2,1,0:T(8,128)(2,1)S(1)}, bf16[4,4,5,24,768]{4,3,2,1,0:T(8,128)(2,1)S(1)}, u32[]{:S(2)}, u32[]{:S(2)}) collective-permute-start(bf16[4,4,5,24,768]{4,3,2,1,0:T(8,128)(2,1)S(1)} %weight_grads.5), channel_id=1, source_target_pairs={{0,16},{16,0},{1,17},{17,1},{2,18},{18,2},{3,19},{19,3},{4,20},{20... | collective-permute-start | bytes 8847368 | tf_op jit(solution)/shard_map/ppermute | solution.py:32
  195.1 12.7 %collective-permute-start.11 = (bf16[1024,384]{1,0:T(8,128)(2,1)S(1)}, bf16[1024,384]{1,0:T(8,128)(2,1)S(1)}, u32[]{:S(2)}, u32[]{:S(2)}) collective-permute-start(bf16[1024,384]{1,0:T(8,128)(2,1)S(1)} %copy-done.25), channel_id=1, source_target_pairs={{0,16},{16,0},{1,17},{17,1},{2,18},{18,2},{3,19},{19,3},{4,20},{20... | collective-permute-start | bytes 2359304 | tf_op jit(solution)/shard_map/ppermute | solution.py:32
  208.7 93.6 %reduce-scatter.6.cloned.1.call-start = ((), (), s32[]{:S(2)}) async-start(), calls=%async_computation.6 | async-start | bytes 1474560 | tf_op jit(solution)/shard_map/reduce_scatter | solution.py:1041
  267.8 2.3 collective-permute-start.14
  272.3 80.0 %reduce-scatter.8.cloned.1.call-start = ((), (), s32[]{:S(2)}) async-start(), calls=%async_computation.7 | async-start | bytes 2027520 | tf_op jit(solution)/shard_map/reduce_scatter | solution.py:1046
  311.9 9.9 %collective-permute-start.15 = (bf16[1024,768]{1,0:T(8,128)(2,1)}, bf16[1024,768]{1,0:T(8,128)(2,1)}, u32[]{:S(2)}, u32[]{:S(2)}) collective-permute-start(bf16[1024,768]{1,0:T(8,128)(2,1)} %get-tuple-element.112), channel_id=1, source_target_pairs={{0,16},{16,0},{1,17},{17,1},{2,18},{18,2},{3,19},{19,3},{4,20},{20... | collective-permute-start | bytes 4718600 | tf_op jit(solution)/shard_map/ppermute | solution.py:32
  313.2 2.7 collective-permute-start.18
  317.0 36.5 %all-to-all-start = ((bf16[16,32,768]{2,1,0:T(8,128)(2,1)}), bf16[16,32,768]{2,1,0:T(8,128)(2,1)S(1)}, u32[]{:S(2)}, u32[]{:S(2)}) async-start(bf16[16,32,768]{2,1,0:T(8,128)(2,1)} %bitcast.61), calls=%async_computation.3 | async-start | bytes 1572864 | tf_op jit(solution)/shard_map/all_to_all | solution.py:1077
  324.8 42.8 %collective-permute-start.17 = (bf16[1024,768]{1,0:T(8,128)(2,1)}, bf16[1024,768]{1,0:T(8,128)(2,1)S(1)}, u32[]{:S(2)}, u32[]{:S(2)}) collective-permute-start(bf16[1024,768]{1,0:T(8,128)(2,1)} %add_convert_fusion), channel_id=1, source_target_pairs={{0,1},{1,0},{2,3},{3,2},{4,5},{5,4},{6,7},{7,6},{8,9},{9,8},{10,11... | collective-permute-start | bytes 4718600 | tf_op jit(solution)/shard_map/ppermute | solution.py:32
  352.4 15.2 %collective-permute-start.16 = (bf16[1024,768]{1,0:T(8,128)(2,1)}, bf16[1024,768]{1,0:T(8,128)(2,1)}, u32[]{:S(2)}, u32[]{:S(2)}) collective-permute-start(bf16[1024,768]{1,0:T(8,128)(2,1)} %get-tuple-element.124), channel_id=1, source_target_pairs={{0,16},{16,0},{1,17},{17,1},{2,18},{18,2},{3,19},{19,3},{4,20},{20... | collective-permute-start | bytes 4718600 | tf_op jit(solution)/shard_map/ppermute | solution.py:32
  (29 other events, 232.8 us)
Sparse Core Ops, SparseCore 0:
  53.2 88.3 all-gather.1
  208.0 60.5 reduce-scatter.3
  272.4 27.6 reduce-scatter.5
  304.7 47.6 reduce-scatter.7
